TPU v7x, 256 devices: a whole 4x4x8 slice. The times are simulated.
256 devices in a mesh: start: 2 (over core), pencil: 128 (over z, x, y).
Axes of the slice: x: 4, y: 4, z: 8, core: 2. Of those that a mesh axis runs over, the one named last changes fastest.
Arguments:
- template: bfloat16 [512, 64, 512], P('pencil', 'start'), parts along dimension 1, may hold values from -3.5 to 3.5
- reference_image: bfloat16 [512, 64, 512], P('pencil', 'start'), parts along dimension 1, may hold values from -3.5 to 3.5
- velocity: float32 [6, 512, 32, 512], P('start', 'pencil'), parts along dimension 0, may hold values from -4 to 4
- dep_owner: int32 [4, 32768], P('start', 'pencil'), parts along dimension 0, may hold values from 0 to 127, as said below
- dep_offset: int32 [4, 32768], P('start', 'pencil'), parts along dimension 0, may hold values from 0 to 255
- dep_weight: int32 [4, 32768], P('start', 'pencil'), parts along dimension 0, may hold values from 0 to 15
Outputs:
- warped: bfloat16 [512, 64, 512], P('pencil', 'start'), parts along dimension 1
- gradient: float32 [6, 512, 32, 512], P('start', 'pencil'), parts along dimension 0
There are 2 independent parts, one for each index of `start`. A program takes and returns all parts, laid end to end along the dimension named above; each array names one. Nothing has to cross between parts.
Inputs may be any that keep to these rules, and one draw needn't show every extreme that they name: Device d holds blocks d * 256 to (d + 1) * 256 - 1. For a block of device d, dep_owner is (d + m) mod 128 with m one of -2, -1, 0, 1, so that its stencil rows lie on devices d - 2 to d + 2 (modulo 128).
All inputs are finite; a program needn't handle non-finite values.
Results may differ from a plain program's by a relative error of at most 0.012.
Values may be sent and summed in bfloat16 or wider, within the bound.
No kernel may reach another device: no remote copies, remote signals or barrier semaphores. Data moves between devices by JAX's collectives and lax.ppermute only.
A program may use at most 192 MiB of HBM per device.

v0:
```python
import math

import jax
import jax.numpy as jnp
from jax import lax
from jax.sharding import PartitionSpec as P

ZB = 2
SEG = 128
Q = 16


h1_weight = 64.0
force_gain = 32.0


def shifted(x, axis, by):
    length = lax.axis_size(axis)
    return lax.ppermute(x, axis, [(i, (i + by) % length) for i in range(length)])


def dft_tables(length):
    series = jnp.arange(length, dtype=jnp.int32)
    product = series[:, None] * series[None, :] % length
    angles = product.astype(jnp.float32) * (2.0 * math.pi / length)
    return (jnp.cos(angles).astype(jnp.bfloat16), jnp.sin(angles).astype(jnp.bfloat16))


def signed_waves(series, length):
    signed = jnp.where(series < length // 2, series, series - length)
    signed = jnp.where(series == length // 2, 0, signed)
    return signed.astype(jnp.float32) * (2.0 * math.pi / length)


def wave_numbers(length):
    return signed_waves(jnp.arange(length, dtype=jnp.int32), length)


def cubic_table(levels):
    fraction = (jnp.arange(levels, dtype=jnp.float32) + 0.5) / levels
    node_left = -fraction * (fraction - 1.0) * (fraction - 2.0) / 6.0
    node_zero = (fraction + 1.0) * (fraction - 1.0) * (fraction - 2.0) / 2.0
    node_one = -(fraction + 1.0) * fraction * (fraction - 2.0) / 2.0
    node_two = (fraction + 1.0) * fraction * (fraction - 1.0) / 6.0
    return jnp.stack([node_left, node_zero, node_one, node_two], axis=1)


def pick_weights(weight_level, weight_table):
    onehot = (
        weight_level[:, None] == jnp.arange(weight_table.shape[0], dtype=jnp.int32)[None, :]
    ).astype(jnp.float32)
    return jnp.dot(onehot, weight_table, precision=lax.Precision.HIGHEST)


def local(template, reference_image, velocity, dep_owner, dep_offset, dep_weight):
    peer_count = lax.axis_size("pencil")
    row_count, plane_count, y_count = template.shape
    full_rows = row_count * peer_count
    z_groups = plane_count // ZB
    y_groups = y_count // SEG
    per_row = z_groups * y_groups
    block_count = row_count * per_row
    cell_count = plane_count * y_count
    weight_table = cubic_table(Q)
    my_index = lax.axis_index("pencil")
    shaped = template.reshape(row_count, z_groups, ZB, y_groups, SEG)
    blocks = shaped.transpose(0, 1, 3, 2, 4).reshape(block_count, ZB * SEG)
    for section_index in range(2):
        pieces = []
        for distance in (2, 1, 0, -1, -2):
            if distance == 0:
                pieces.append(blocks)
            else:
                pieces.append(shifted(blocks, "pencil", distance))
        window = jnp.concatenate(pieces, axis=0)
        relative = (dep_owner[section_index] - my_index + peer_count) % peer_count
        move = jnp.where(relative >= peer_count - 2, relative - peer_count, relative)
        offset = dep_offset[section_index]
        start_row = offset // per_row
        place = offset % per_row
        tap_row = (
            (move[:, None] + 2) * row_count
            + start_row[:, None]
            + jnp.arange(4, dtype=jnp.int32)[None, :]
        )
        taps = window[tap_row * per_row + place[:, None]].astype(jnp.float32)
        weights = pick_weights(dep_weight[section_index], weight_table)
        blocks = jnp.sum(weights[:, :, None] * taps, axis=1).astype(jnp.bfloat16)
    shaped = blocks.reshape(row_count, z_groups, y_groups, ZB, SEG)
    warped = shaped.transpose(0, 1, 3, 2, 4).reshape(row_count, plane_count, y_count)
    warped_f = warped.astype(jnp.float32)
    residual = reference_image.astype(jnp.float32) - warped_f
    cos_y, sin_y = dft_tables(y_count)
    cos_x, sin_x = dft_tables(full_rows)
    kvec_y = wave_numbers(y_count)
    kvec_x = wave_numbers(full_rows)
    forward_y = jnp.concatenate([cos_y, -sin_y], axis=1)
    inverse_y = jnp.concatenate([cos_y, -sin_y], axis=0)
    forward_x = jnp.concatenate([cos_x, -sin_x], axis=0)
    inverse_x = jnp.concatenate([cos_x, -sin_x], axis=1)
    spec_y = jnp.dot(warped.reshape(-1, y_count), forward_y, preferred_element_type=jnp.float32)
    spec_y = spec_y.astype(jnp.bfloat16).astype(jnp.float32)
    coef_y = jnp.concatenate(
        [-kvec_y * spec_y[:, y_count:], kvec_y * spec_y[:, :y_count]], axis=1
    ).astype(jnp.bfloat16)
    slope_y = (jnp.dot(coef_y, inverse_y, preferred_element_type=jnp.float32) / y_count).reshape(
        row_count, plane_count, y_count
    )
    flat_warp = warped.reshape(1, row_count, cell_count)
    spec_x = jnp.einsum(
        "kx,ixm->ikm",
        forward_x,
        lax.all_to_all(flat_warp, "pencil", split_axis=2, concat_axis=1, tiled=True),
        preferred_element_type=jnp.float32,
    )
    coef_x = jnp.concatenate(
        [
            -kvec_x[None, :, None] * spec_x[:, full_rows:],
            kvec_x[None, :, None] * spec_x[:, :full_rows],
        ],
        axis=1,
    ).astype(jnp.bfloat16)
    slope = (
        jnp.einsum("xk,ikm->ixm", inverse_x, coef_x, preferred_element_type=jnp.float32) / full_rows
    ).astype(jnp.bfloat16)
    slope_x = lax.all_to_all(slope, "pencil", split_axis=1, concat_axis=2, tiled=True)
    slope_x = slope_x.reshape(row_count, plane_count, y_count)
    slope_z = (jnp.roll(warped_f, -1, axis=1) - jnp.roll(warped_f, 1, axis=1)) * 0.5
    force = (jnp.stack([slope_x.astype(jnp.float32), slope_y, slope_z]) * residual[None]).astype(
        jnp.bfloat16
    )
    force_lines = force.reshape(-1, y_count)
    spec_real = jnp.dot(force_lines, cos_y, preferred_element_type=jnp.float32).astype(jnp.bfloat16)
    spec_imag = jnp.dot(force_lines, -sin_y, preferred_element_type=jnp.float32).astype(
        jnp.bfloat16
    )
    spec_f = jnp.stack(
        [spec_real.reshape(3, row_count, cell_count), spec_imag.reshape(3, row_count, cell_count)],
        axis=1,
    )
    planes = lax.all_to_all(spec_f, "pencil", split_axis=3, concat_axis=2, tiled=True)
    local_cols = planes.shape[3]
    column_ids = my_index * local_cols + jnp.arange(local_cols, dtype=jnp.int32)
    kvec_local = signed_waves(column_ids % y_count, y_count)
    spectral_gain = force_gain / (
        full_rows
        * y_count
        * (
            1.0
            + h1_weight
            * (kvec_x[:, None] * kvec_x[:, None] + kvec_local[None, :] * kvec_local[None, :])
        )
    )
    cos_part = jnp.einsum("kx,chxm->chkm", cos_x, planes, preferred_element_type=jnp.float32)
    sin_part = jnp.einsum("kx,chxm->chkm", sin_x, planes, preferred_element_type=jnp.float32)
    real_f = cos_part[:, 0] + sin_part[:, 1]
    imag_f = cos_part[:, 1] - sin_part[:, 0]
    scale_grid = spectral_gain[None]
    scaled = jnp.stack([real_f * scale_grid, imag_f * scale_grid], axis=1).astype(jnp.bfloat16)
    cos_back = jnp.einsum("xk,chkm->chxm", cos_x, scaled, preferred_element_type=jnp.float32)
    sin_back = jnp.einsum("xk,chkm->chxm", sin_x, scaled, preferred_element_type=jnp.float32)
    real_b = cos_back[:, 0] - sin_back[:, 1]
    imag_b = cos_back[:, 1] + sin_back[:, 0]
    mixed = jnp.stack([real_b, imag_b], axis=1).astype(jnp.bfloat16)
    smoothed = lax.all_to_all(mixed, "pencil", split_axis=2, concat_axis=3, tiled=True)
    spatial = jnp.dot(
        smoothed[:, 0].reshape(-1, y_count), cos_y, preferred_element_type=jnp.float32
    )
    spatial = spatial - jnp.dot(
        smoothed[:, 1].reshape(-1, y_count), sin_y, preferred_element_type=jnp.float32
    )
    gradient = velocity + spatial.reshape(3, row_count, plane_count, y_count)
    return (warped, gradient)


def solution(mesh):
    in_specs = (
        P("pencil", "start", None),
        P("pencil", "start", None),
        P("start", "pencil", None, None),
        P("start", "pencil"),
        P("start", "pencil"),
        P("start", "pencil"),
    )
    out_specs = (P("pencil", "start", None), P("start", "pencil", None, None))
    return jax.shard_map(local, mesh=mesh, in_specs=in_specs, out_specs=out_specs, check_vma=False)
```

profile of v0, /device:TPU:2, one launch (start us, length us, event | category | flops | bytes accessed | tf_op | source)
XLA Modules:
  0.0 645.6 jit_solution(7379281555663057057)
XLA Ops:
  45.5 12.9 %copy.100 = bf16[1,4,16384]{1,0,2:T(2,128)(2,1)} copy(bf16[1,4,16384]{2,1,0:T(4,128)(2,1)S(1)} %reshape_reshape.6) | data formatting | bytes 262144 | tf_op jit(solution)/shard_map/reshape;reshape | solution.py:109
  58.9 90.7 %reduce = bf16[16384,4]{1,0:T(8,128)(2,1)} reduce(bf16[16384,1,4]{2,1,0:T(2,128)(2,1)} %bitcast.108, bf16[]{:T(256)} %broadcast.922), dimensions={1}, to_apply=%bitcast.90.reduce_sub_computation | reduce | bytes 262146
  149.6 9.3 %reshape.616 = bf16[128,2,256]{2,1,0:T(2,128)(2,1)} reshape(bf16[16384,4]{1,0:T(8,128)(2,1)} %reduce) | data formatting | bytes 262144
  158.9 19.8 %all-to-all-start = ((bf16[128,2,256]{2,1,0:T(2,128)(2,1)}), bf16[128,2,256]{2,1,0:T(2,128)(2,1)S(1)}, u32[]{:S(2)}, u32[]{:S(2)}) async-start(bf16[128,2,256]{2,1,0:T(2,128)(2,1)} %reshape.616), calls=%async_computation | async-start | bytes 262144 | tf_op jit(solution)/shard_map/all_to_all | solution.py:113
  179.5 11.0 %all-to-all-done = bf16[128,2,256]{2,1,0:T(2,128)(2,1)S(1)} async-done(((bf16[128,2,256]{2,1,0:T(2,128)(2,1)}), bf16[128,2,256]{2,1,0:T(2,128)(2,1)S(1)}, u32[]{:S(2)}, u32[]{:S(2)}) %all-to-all-start) | async-done | bytes 131104 | tf_op jit(solution)/shard_map/all_to_all | solution.py:113
  190.4 17.1 %reshape.617 = bf16[16384,1,4]{2,1,0:T(2,128)(2,1)} reshape(bf16[128,2,256]{2,1,0:T(2,128)(2,1)S(1)} %all-to-all-done) | data formatting | bytes 262144
  207.5 15.4 %copy.101 = bf16[1,4,16384]{2,1,0:T(4,128)(2,1)S(1)} copy(bf16[1,4,16384]{1,0,2:T(2,128)(2,1)} %bitcast.109) | data formatting | bytes 262144 | tf_op jit(solution)/shard_map/all_to_all | solution.py:113
  226.4 6.6 %all-to-all-start.1 = ((bf16[128,2,256]{2,1,0:T(2,128)(2,1)}), bf16[128,2,256]{2,1,0:T(2,128)(2,1)S(1)}, u32[]{:S(2)}, u32[]{:S(2)}) async-start(bf16[128,2,256]{2,1,0:T(2,128)(2,1)} %reshape.618), calls=%async_computation.1 | async-start | bytes 262144 | tf_op jit(solution)/shard_map/all_to_all | solution.py:126
  233.1 11.8 %all-to-all-done.1 = bf16[128,2,256]{2,1,0:T(2,128)(2,1)S(1)} async-done(((bf16[128,2,256]{2,1,0:T(2,128)(2,1)}), bf16[128,2,256]{2,1,0:T(2,128)(2,1)S(1)}, u32[]{:S(2)}, u32[]{:S(2)}) %all-to-all-start.1) | async-done | bytes 131104 | tf_op jit(solution)/shard_map/all_to_all | solution.py:126
  245.3 4.8 convolution_convert_fusion.1
  250.1 4.9 convolution_convert_fusion
  255.3 39.4 %copy.107 = bf16[3,1,4,16384]{2,1,0,3:T(2,128)(2,1)} copy(bf16[3,1,4,16384]{3,2,0,1:T(4,128)(2,1)S(1)} %stack_reshape.10) | data formatting | bytes 786432 | tf_op jit(solution)/shard_map/stack;reshape | solution.py:137
  294.9 39.6 %copy.108 = bf16[3,1,4,16384]{2,1,0,3:T(2,128)(2,1)} copy(bf16[3,1,4,16384]{3,2,0,1:T(4,128)(2,1)S(1)} %stack_reshape.11) | data formatting | bytes 786432 | tf_op jit(solution)/shard_map/stack;reshape | solution.py:137
  334.5 70.4 %fusion.102 = bf16[16384,3,2,4]{3,2,1,0:T(2,128)(2,1)} fusion(bf16[3,1,4,16384]{2,1,0,3:T(2,128)(2,1)} %copy.108, bf16[3,1,4,16384]{2,1,0,3:T(2,128)(2,1)} %copy.107), kind=kLoop, calls=%fused_computation.201 | loop fusion | flops 1572864 | bytes 1572864
  404.9 61.9 %reshape.620 = bf16[128,2,1536]{2,1,0:T(2,128)(2,1)} reshape(bf16[16384,3,2,4]{3,2,1,0:T(2,128)(2,1)} %fusion.102) | data formatting | bytes 1572864
  466.8 7.0 %all-to-all-start.2 = ((bf16[128,2,1536]{2,1,0:T(2,128)(2,1)}), bf16[128,2,1536]{2,1,0:T(2,128)(2,1)S(1)}, u32[]{:S(2)}, u32[]{:S(2)}) async-start(bf16[128,2,1536]{2,1,0:T(2,128)(2,1)} %reshape.620), calls=%async_computation.2 | async-start | bytes 1572864 | tf_op jit(solution)/shard_map/all_to_all | solution.py:141
  474.0 20.2 %all-to-all-done.2 = bf16[128,2,1536]{2,1,0:T(2,128)(2,1)S(1)} async-done(((bf16[128,2,1536]{2,1,0:T(2,128)(2,1)}), bf16[128,2,1536]{2,1,0:T(2,128)(2,1)S(1)}, u32[]{:S(2)}, u32[]{:S(2)}) %all-to-all-start.2) | async-done | bytes 786464 | tf_op jit(solution)/shard_map/all_to_all | solution.py:141
  494.2 55.1 %reshape.621 = bf16[16384,3,2,4]{3,2,1,0:T(2,128)(2,1)} reshape(bf16[128,2,1536]{2,1,0:T(2,128)(2,1)S(1)} %all-to-all-done.2) | data formatting | bytes 1572864
  549.3 35.1 %copy.121 = bf16[3,2,4,128,128]{4,3,2,1,0:T(8,128)(2,1)S(1)} copy(bf16[3,2,4,128,128]{2,1,0,4,3:T(2,128)(2,1)} %bitcast.107) | data formatting | bytes 1572864 | tf_op jit(solution)/shard_map/all_to_all | solution.py:141
  585.0 5.5 convolution_bitcast_fusion.2
  590.5 5.9 convolution_bitcast_fusion.3
  607.1 27.0 %all_to_all.60 = bf16[3,2,512,128]{3,1,0,2:T(2,128)(2,1)S(1)} all-to-all(bf16[3,2,512,128]{3,1,0,2:T(2,128)(2,1)S(1)} %copy.113), channel_id=1, replica_groups=mesh['start'=2,'pencil'=128] {'pencil'}, dimensions={2} | all-to-all | bytes 1572864 | tf_op jit(solution)/shard_map/all_to_all | solution.py:165
  634.8 4.6 fusion.21
  639.7 4.7 convolution_subtract_fusion
  (103 shorter events, 63.5 us)
Async XLA Ops:
  1.7 14.8 %collective-permute-start = (bf16[256,256]{1,0:T(8,128)(2,1)S(1)}, bf16[256,256]{1,0:T(8,128)(2,1)S(1)}, u32[]{:S(2)}, u32[]{:S(2)}) collective-permute-start(bf16[256,256]{1,0:T(8,128)(2,1)S(1)} %bitcast.127), channel_id=1, source_target_pairs={{0,2},{1,3},{2,4},{3,5},{4,6},{5,7},{6,8},{7,9},{8,10},{9,11},{10,... | collective-permute-start | bytes 393224 | tf_op jit(solution)/shard_map/ppermute | solution.py:19
  5.0 11.5 %collective-permute-start.1 = (bf16[256,256]{1,0:T(8,128)(2,1)S(1)}, bf16[256,256]{1,0:T(8,128)(2,1)S(1)}, u32[]{:S(2)}, u32[]{:S(2)}) collective-permute-start(bf16[256,256]{1,0:T(8,128)(2,1)S(1)} %bitcast.128), channel_id=1, source_target_pairs={{0,1},{1,2},{2,3},{3,4},{4,5},{5,6},{6,7},{7,8},{8,9},{9,10},{10,1... | collective-permute-start | bytes 393224 | tf_op jit(solution)/shard_map/ppermute | solution.py:19
  5.7 10.9 %collective-permute-start.2 = (bf16[256,256]{1,0:T(8,128)(2,1)S(1)}, bf16[256,256]{1,0:T(8,128)(2,1)S(1)}, u32[]{:S(2)}, u32[]{:S(2)}) collective-permute-start(bf16[256,256]{1,0:T(8,128)(2,1)S(1)} %bitcast.129), channel_id=1, source_target_pairs={{0,127},{1,0},{2,1},{3,2},{4,3},{5,4},{6,5},{7,6},{8,7},{9,8},{10,... | collective-permute-start | bytes 393224 | tf_op jit(solution)/shard_map/ppermute | solution.py:19
  9.1 7.5 %collective-permute-start.3 = (bf16[256,256]{1,0:T(8,128)(2,1)S(1)}, bf16[256,256]{1,0:T(8,128)(2,1)S(1)}, u32[]{:S(2)}, u32[]{:S(2)}) collective-permute-start(bf16[256,256]{1,0:T(8,128)(2,1)S(1)} %bitcast.130), channel_id=1, source_target_pairs={{0,126},{1,127},{2,0},{3,1},{4,2},{5,3},{6,4},{7,5},{8,6},{9,7},{1... | collective-permute-start | bytes 393224 | tf_op jit(solution)/shard_map/ppermute | solution.py:19
  21.6 13.5 %collective-permute-start.4 = (bf16[256,256]{1,0:T(8,128)(2,1)S(1)}, bf16[256,256]{1,0:T(8,128)(2,1)S(1)}, u32[]{:S(2)}, u32[]{:S(2)}) collective-permute-start(bf16[256,256]{1,0:T(8,128)(2,1)S(1)} %multiply_reduce_fusion.1), channel_id=1, source_target_pairs={{0,2},{1,3},{2,4},{3,5},{4,6},{5,7},{6,8},{7,9},{8,10},{9,11},{10,... | collective-permute-start | bytes 393224 | tf_op jit(solution)/shard_map/ppermute | solution.py:19
  29.2 7.7 %collective-permute-start.5 = (bf16[256,256]{1,0:T(8,128)(2,1)S(1)}, bf16[256,256]{1,0:T(8,128)(2,1)S(1)}, u32[]{:S(2)}, u32[]{:S(2)}) collective-permute-start(bf16[256,256]{1,0:T(8,128)(2,1)S(1)} %multiply_reduce_fusion.1), channel_id=1, source_target_pairs={{0,1},{1,2},{2,3},{3,4},{4,5},{5,6},{6,7},{7,8},{8,9},{9,10},{10,1... | collective-permute-start | bytes 393224 | tf_op jit(solution)/shard_map/ppermute | solution.py:19
  29.3 7.6 %collective-permute-start.6 = (bf16[256,256]{1,0:T(8,128)(2,1)S(1)}, bf16[256,256]{1,0:T(8,128)(2,1)S(1)}, u32[]{:S(2)}, u32[]{:S(2)}) collective-permute-start(bf16[256,256]{1,0:T(8,128)(2,1)S(1)} %multiply_reduce_fusion.1), channel_id=1, source_target_pairs={{0,127},{1,0},{2,1},{3,2},{4,3},{5,4},{6,5},{7,6},{8,7},{9,8},{10,... | collective-permute-start | bytes 393224 | tf_op jit(solution)/shard_map/ppermute | solution.py:19
  33.4 6.9 %collective-permute-start.7 = (bf16[256,256]{1,0:T(8,128)(2,1)S(1)}, bf16[256,256]{1,0:T(8,128)(2,1)S(1)}, u32[]{:S(2)}, u32[]{:S(2)}) collective-permute-start(bf16[256,256]{1,0:T(8,128)(2,1)S(1)} %multiply_reduce_fusion.1), channel_id=1, source_target_pairs={{0,126},{1,127},{2,0},{3,1},{4,2},{5,3},{6,4},{7,5},{8,6},{9,7},{1... | collective-permute-start | bytes 393224 | tf_op jit(solution)/shard_map/ppermute | solution.py:19
  45.5 187.6 %copy-start = (bf16[4,32,512]{2,1,0:T(8,128)(2,1)}, bf16[4,32,512]{2,1,0:T(8,128)(2,1)S(1)}, u32[]{:S(2)}) copy-start(bf16[4,32,512]{2,1,0:T(8,128)(2,1)S(1)} %reshape.589) | copy-start | bytes 393220
  158.9 31.5 %all-to-all-start = ((bf16[128,2,256]{2,1,0:T(2,128)(2,1)}), bf16[128,2,256]{2,1,0:T(2,128)(2,1)S(1)}, u32[]{:S(2)}, u32[]{:S(2)}) async-start(bf16[128,2,256]{2,1,0:T(2,128)(2,1)} %reshape.616), calls=%async_computation | async-start | bytes 262144 | tf_op jit(solution)/shard_map/all_to_all | solution.py:113
  223.6 9.4 %copy-start.2 = (bf16[4,32,512]{2,1,0:T(8,128)(2,1)S(1)}, bf16[4,32,512]{2,1,0:T(8,128)(2,1)}, u32[]{:S(2)}) copy-start(bf16[4,32,512]{2,1,0:T(8,128)(2,1)} %param.7) | copy-start | bytes 393220
  226.4 18.5 %all-to-all-start.1 = ((bf16[128,2,256]{2,1,0:T(2,128)(2,1)}), bf16[128,2,256]{2,1,0:T(2,128)(2,1)S(1)}, u32[]{:S(2)}, u32[]{:S(2)}) async-start(bf16[128,2,256]{2,1,0:T(2,128)(2,1)} %reshape.618), calls=%async_computation.1 | async-start | bytes 262144 | tf_op jit(solution)/shard_map/all_to_all | solution.py:126
  466.8 27.4 %all-to-all-start.2 = ((bf16[128,2,1536]{2,1,0:T(2,128)(2,1)}), bf16[128,2,1536]{2,1,0:T(2,128)(2,1)S(1)}, u32[]{:S(2)}, u32[]{:S(2)}) async-start(bf16[128,2,1536]{2,1,0:T(2,128)(2,1)} %reshape.620), calls=%async_computation.2 | async-start | bytes 1572864 | tf_op jit(solution)/shard_map/all_to_all | solution.py:141
  639.7 4.7 copy-start.1
where the time goes:
time: 654 us; the launch traced here: 646 us
  local copies, waits for them, and re-layouts  302 us (46%)
  other arithmetic  175 us (27%)
  starting transfers between devices  50.2 us (8%)
  waiting for transfers between devices  48.2 us (7%)
  matrix products  41.1 us (6%)
  blocking collectives  27 us (4%)
    unnamed x3, other arithmetic  162 us
    unnamed x23, local copies, waits for them, and re-layouts  145 us
    another operation x4, local copies, waits for them, and re-layouts, local(): jnp.stack([spec_real.reshape(3, row_count, cell_count), spec_imag.reshape...  79.5 us
    all_to_all x2, local copies, waits for them, and re-layouts, local(): lax.all_to_all(spec_f, 'pencil', split_axis=3, concat_axis=2, tiled=True)  35.7 us
    all_to_all x1, blocking collectives, local(): lax.all_to_all(mixed, 'pencil', split_axis=2, concat_axis=3, tiled=True)  27 us
    all_to_all x1, waiting for transfers between devices, local(): lax.all_to_all(spec_f, 'pencil', split_axis=3, concat_axis=2, tiled=True)  20.2 us
    all_to_all x1, starting transfers between devices, local(): lax.all_to_all(flat_warp, 'pencil', split_axis=2, concat_axis=1, tiled=True)  19.8 us
    ppermute x8, starting transfers between devices, shifted(): lax.ppermute(x, axis, [(i, (i + by) % length) for i in range(length)])  16.9 us
  transfers between devices with their start and end apart: 11, of which 5 were waited for; matrix products, arithmetic and copies ran while one was open for 2% of the time, Pallas kernels for 0%

commit v1 on v0

v1 whole, which is shorter than its diff:
```python
import math

import jax
import jax.numpy as jnp
import numpy as np
from jax import lax
from jax.sharding import PartitionSpec as P

Q = 16
N = 512
H1_WEIGHT = 64.0
FORCE_GAIN = 32.0


def wave_numbers():
    k = np.arange(N)
    signed = np.where(k < N // 2, k, k - N)
    signed = np.where(k == N // 2, 0, signed)
    return signed * (2.0 * math.pi / N)


def derivative_matrix():
    k = np.arange(N)
    lag = np.arange(N)
    row = (np.sin(2.0 * math.pi * ((k[:, None] * lag[None, :]) % N) / N) * wave_numbers()[:, None]).sum(0) / N
    return row[(lag[None, :] - lag[:, None]) % N]


def basis(points):
    k = np.concatenate([np.arange(N // 2 + 1), np.arange(1, N // 2)])
    angle = 2.0 * math.pi * ((k[:, None] * points[None, :]) % N) / N
    is_cos = (np.arange(N) <= N // 2)[:, None]
    return np.where(is_cos, np.cos(angle), np.sin(angle))


def basis_waves():
    k = np.concatenate([np.arange(N // 2 + 1), np.arange(1, N // 2)])
    weight = np.where((k == 0) | (k == N // 2), 1.0, 2.0)
    return wave_numbers()[k], weight


def bf(x):
    return jnp.asarray(np.asarray(x, np.float32), jnp.bfloat16)


def cubic(level):
    t = (level.astype(jnp.float32) + 0.5) / Q
    return [
        -t * (t - 1.0) * (t - 2.0) / 6.0,
        (t + 1.0) * (t - 1.0) * (t - 2.0) / 2.0,
        -(t + 1.0) * t * (t - 2.0) / 2.0,
        (t + 1.0) * t * (t - 1.0) / 6.0,
    ]


def dot(a, b, dims=((1,), (0,))):
    return lax.dot_general(a, b, (dims, ((), ())), preferred_element_type=jnp.float32)


def transport_matrix(rel, weights):
    row = lax.broadcasted_iota(jnp.int32, (N, N), 0)
    col = lax.broadcasted_iota(jnp.int32, (N, N), 1)
    lag = (col - (row // 4) * 4 - rel.astype(jnp.int32)) & (N - 1)
    out = jnp.zeros((N, N), jnp.bfloat16)
    for tap in range(4):
        out = jnp.where(lag == tap, weights[tap], out)
    return out


def local(template, reference_image, velocity, dep_owner, dep_offset, dep_weight):
    me = lax.axis_index("pencil")
    quarter = me % 4
    plane_even = (me // 4) % 2 == 0
    bf16 = jnp.bfloat16

    move = (dep_owner - me + 130) % 128 - 2
    rel = move * 4 + dep_offset // 64
    codes = []
    for section in range(2):
        codes.append(rel[section].astype(bf16))
        taps = cubic(dep_weight[section])
        high = [w.astype(bf16) for w in taps]
        low = [(w - h.astype(jnp.float32)).astype(bf16) for w, h in zip(taps, high)]
        codes += high + low
    codes = jnp.stack(codes, axis=0).reshape(18, 4, 16, 4).transpose(2, 3, 1, 0)
    codes = jnp.repeat(codes, 2, axis=0)

    def partner(a):
        return a.reshape((16, 2) + a.shape[1:])[:, ::-1].reshape(a.shape)

    def other(a):
        return jnp.roll(partner(jnp.roll(a, 1, axis=0)), -1, axis=0)

    pad = jnp.zeros((32, 4, 4, 46), bf16)
    codes = jnp.concatenate([codes, pad, other(codes), pad], axis=3)
    planes = template.reshape(4, 32, 4, 128).transpose(1, 2, 0, 3)
    image = reference_image.reshape(4, 32, 4, 128).transpose(1, 2, 0, 3)
    pack = jnp.stack(
        [planes, partner(planes), other(planes)]
        + [jnp.roll(image, -s, axis=1) for s in range(4)]
        + [codes],
        axis=2,
    ).reshape(1024, 4, 128)
    got = lax.all_to_all(pack, "pencil", 0, 0, tiled=True).reshape(128, 8, 4, 128)
    unit = [got[:, u].reshape(N, 128) for u in range(8)]

    own = jnp.concatenate([unit[0], unit[1]], axis=1)
    far = unit[2]
    for section in range(2):
        for is_far in range(2):
            at = 64 * is_far + 9 * section
            rel_x = unit[7][:, at : at + 1]
            high = transport_matrix(rel_x, [unit[7][:, at + 1 + k : at + 2 + k] for k in range(4)])
            low = transport_matrix(rel_x, [unit[7][:, at + 5 + k : at + 6 + k] for k in range(4)])
            f = far if is_far else own
            f = (dot(high, f) + dot(low, f)).astype(bf16)
            if is_far:
                far = f
            else:
                own = f
    warped = own[:, :128]
    up = own[:, 128:].astype(jnp.float32) - far.astype(jnp.float32)
    slope_z = up * jnp.where(plane_even, 0.5, -0.5)
    force_z = ((unit[3].astype(jnp.float32) - warped.astype(jnp.float32)) * slope_z).astype(bf16)

    payload = jnp.stack([warped, force_z])
    parts = [payload]
    for s in (1, 2, 3):
        parts.append(
            lax.ppermute(payload, "pencil", [((i // 4) * 4 + (i + s) % 4, i) for i in range(128)])
        )
    whole = jnp.concatenate([p[0] for p in parts], axis=1)
    force_z = jnp.concatenate([p[1] for p in parts], axis=1)
    image = jnp.concatenate([unit[3 + s] for s in range(4)], axis=1)

    deriv = bf(derivative_matrix())
    residual = image.astype(jnp.float32) - whole.astype(jnp.float32)
    force_x = (residual * dot(deriv, whole)).astype(bf16)
    force_y = (residual * dot(whole, deriv, ((1,), (1,)))).astype(bf16)

    table = bf(basis(np.arange(N)))
    mine = lax.dynamic_slice(table, (quarter * 128, 0), (128, N))
    spec = jnp.concatenate(
        [dot(f, mine, ((1,), (1,))).astype(bf16) for f in (force_x, force_y, force_z)], axis=1
    )
    waves, weight = basis_waves()
    wave_x = jnp.asarray(waves, jnp.float32)[:, None]
    wave_y = lax.dynamic_slice(jnp.asarray(waves, jnp.float32), (quarter * 128,), (128,))[None, :]
    scale_x = jnp.asarray(weight * FORCE_GAIN / (N * N), jnp.float32)[:, None]
    scale_y = lax.dynamic_slice(jnp.asarray(weight, jnp.float32), (quarter * 128,), (128,))[None, :]
    gain = scale_x * scale_y / (1.0 + H1_WEIGHT * (wave_x * wave_x + wave_y * wave_y))
    bent = (dot(table, spec) * jnp.concatenate([gain] * 3, axis=1)).astype(bf16)
    back = dot(table, bent, ((0,), (0,))).astype(bf16)

    send = jnp.stack(
        [back[:, 128 * c : 128 * c + 128].reshape(128, 4, 128) for c in range(3)]
        + [warped.reshape(128, 4, 128)],
        axis=1,
    ).reshape(N, 4, 128)
    home = lax.all_to_all(send, "pencil", 0, 0, tiled=True).reshape(32, 4, 4, 4, 128)
    out_warped = home[:, :, 3].transpose(2, 0, 1, 3).reshape(4, 32, N)
    coef = home[:, :, :3].transpose(2, 3, 0, 1, 4).reshape(384, N)
    inverse = np.concatenate([basis((np.arange(N) - 128 * q) % N)[128 * q : 128 * q + 128] for q in range(4)])
    spatial = dot(coef, bf(inverse))
    gradient = velocity + spatial.reshape(3, 4, 32, N)
    return out_warped, gradient


def solution(mesh):
    in_specs = (
        P("pencil", "start", None),
        P("pencil", "start", None),
        P("start", "pencil", None, None),
        P("start", "pencil"),
        P("start", "pencil"),
        P("start", "pencil"),
    )
    out_specs = (P("pencil", "start", None), P("start", "pencil", None, None))
    return jax.shard_map(local, mesh=mesh, in_specs=in_specs, out_specs=out_specs, check_vma=False)
```

time: 654 us -> 139 us (0.21); the launches traced: 646 us -> 139 us
  local copies, waits for them, and re-layouts: 302 us -> 33.4 us
  other arithmetic: 175 us -> 4.12 us
  starting transfers between devices: 50.2 us -> 18 us
  matrix products: 41.1 us -> 17.6 us
  waiting for transfers between devices: 48.2 us -> 37.9 us
    unnamed x3 -> x4, other arithmetic: 162 us -> 0.1 us
    unnamed x23 -> x59, local copies, waits for them, and re-layouts: 145 us -> 4.65 us
    another operation x9 -> x40, local copies, waits for them, and re-layouts: 94.2 us -> 13.5 us  [the longest x37 12.4 us: local(): codes = jnp.stack(codes, axis=0).reshape(18, 4, 16, 4).transpose(2, 3, 1, 0)]
    all_to_all x6 -> x2, local copies, waits for them, and re-layouts: 51.3 us -> 0.21 us  [the longest x1 0.14 us: local(): lax.all_to_all(pack, 'pencil', 0, 0, tiled=True).reshape(128, 8, 4, 128)]
    dot_general x14 -> x16, matrix products: 41.1 us -> 17.6 us  [dot(): lax.dot_general(a, b, (dims, ((), ())), preferred_element_type=jnp.float32)]
    all_to_all x3 -> x1, starting transfers between devices: 33.3 us -> 15.4 us  [local(): lax.all_to_all(pack, 'pencil', 0, 0, tiled=True).reshape(128, 8, 4, 128)]
    ppermute x8 -> x3, starting transfers between devices: 16.9 us -> 2.6 us  [local(): lax.ppermute(payload, 'pencil', [(i // 4 * 4 + (i + s) % 4, i) for i in r...]
    all_to_all x3 -> x1, waiting for transfers between devices: 43 us -> 29.3 us  [local(): lax.all_to_all(pack, 'pencil', 0, 0, tiled=True).reshape(128, 8, 4, 128)]
  transfers between devices with their start and end apart: 11 -> 4, of which waited for: 5 -> 3; matrix products, arithmetic and copies ran while one was open for 2% -> 3% of each run, Pallas kernels for 0% -> 0%
where the time goes in v1:
time: 139 us
  waiting for transfers between devices  37.9 us (27%)
  local copies, waits for them, and re-layouts  33.4 us (24%)
  blocking collectives  26 us (19%)
  starting transfers between devices  18 us (13%)
  matrix products  17.6 us (13%)
  other arithmetic  4.12 us (3%)
  between operations  1.56 us (1%)
    all_to_all x1, waiting for transfers between devices, local(): lax.all_to_all(pack, 'pencil', 0, 0, tiled=True).reshape(128, 8, 4, 128)  29.3 us
    all_to_all x1, blocking collectives, local(): lax.all_to_all(send, 'pencil', 0, 0, tiled=True).reshape(32, 4, 4, 4, 128)  26 us
    dot_general x16, matrix products, dot(): lax.dot_general(a, b, (dims, ((), ())), preferred_element_type=jnp.float32)  17.6 us
    all_to_all x1, starting transfers between devices, local(): lax.all_to_all(pack, 'pencil', 0, 0, tiled=True).reshape(128, 8, 4, 128)  15.4 us
    another operation x37, local copies, waits for them, and re-layouts, local(): codes = jnp.stack(codes, axis=0).reshape(18, 4, 16, 4).transpose(2, 3, 1, 0)  12.4 us
    ppermute x3, waiting for transfers between devices, local(): lax.ppermute(payload, 'pencil', [(i // 4 * 4 + (i + s) % 4, i) for i in r...  8.6 us
    unnamed x59, local copies, waits for them, and re-layouts  4.65 us
    slice x9, local copies, waits for them, and re-layouts, local(): unit = [got[:, u].reshape(N, 128) for u in range(8)]  3.68 us
  transfers between devices with their start and end apart: 4, of which 3 were waited for; matrix products, arithmetic and copies ran while one was open for 3% of the time, Pallas kernels for 0%

profile of v1, /device:TPU:2, one launch (start us, length us, event | category | flops | bytes accessed | tf_op | source)
XLA Modules:
  0.0 138.6 jit_solution(11239956263729683935)
XLA Ops:
  15.8 0.8 copy-done.13
  19.0 1.8 %copy.110 = bf16[1024,4,128]{2,1,0:T(4,128)(2,1)} copy(bf16[1024,4,128]{2,0,1:T(8,128)(2,1)S(1)} %bitcast.126) | data formatting | bytes 2097152 | tf_op jit(solution)/shard_map/reshape | solution.py:103
  20.9 15.4 %all-to-all-start = ((bf16[1024,4,128]{2,1,0:T(4,128)(2,1)}), bf16[1024,4,128]{2,1,0:T(4,128)(2,1)S(1)}, u32[]{:S(2)}, u32[]{:S(2)}) async-start(bf16[1024,4,128]{2,1,0:T(4,128)(2,1)} %copy.110), calls=%async_computation | async-start | bytes 2097152 | tf_op jit(solution)/shard_map/all_to_all | solution.py:104
  37.9 29.3 %all-to-all-done = bf16[1024,4,128]{2,1,0:T(4,128)(2,1)S(1)} async-done(((bf16[1024,4,128]{2,1,0:T(4,128)(2,1)}), bf16[1024,4,128]{2,1,0:T(4,128)(2,1)S(1)}, u32[]{:S(2)}, u32[]{:S(2)}) %all-to-all-start) | async-done | bytes 1048608 | tf_op jit(solution)/shard_map/all_to_all | solution.py:104
  67.3 2.3 %fusion.253 = (bf16[128,1,4,128]{3,1,0,2:T(2,128)(2,1)S(1)}, bf16[128,1,4,128]{3,1,0,2:T(2,128)(2,1)S(1)}, bf16[128,1,4,128]{3,1,0,2:T(2,128)(2,1)S(1)}, bf16[12...) fusion(bf16[128,8,4,128]{3,1,0,2:T(8,128)(2,1)S(1)} %bitcast.125), kind=kLoop, calls=%fused_computation.339 | loop fusion | bytes 2097152 | tf_op jit(solution)/shard_map/slice | solution.py:105
  69.8 1.5 %slice_reduce_fusion.3 = (bf16[512]{0:T(512)(128)(2,1)S(1)}, bf16[512]{0:T(512)(128)(2,1)S(1)}, bf16[512]{0:T(512)(128)(2,1)S(1)}, bf16[512]{0:T(512)(128)(2,1)S...) fusion(bf16[512,128]{1,0:T(8,128)(2,1)S(1)} %bitcast.122), kind=kLoop, calls=%fused_computation.173 | loop fusion | bytes 38912 | tf_op jit(solution)/shard_map/slice | solution.py:114
  71.8 1.1 slice_reduce_fusion.19
  75.1 1.4 %fusion.78 = f32[512,256]{1,0:T(8,128)S(1)} fusion(bf16[512,256]{1,0:T(8,128)(2,1)S(1)} %fusion.7, s32[512]{0:T(512)S(1)} %get-tuple-element.24, s32[512]{0:T(512)S(1)} %get-tuple-element.98, s32[512]{0:T(512)S(1)} %get-tuple-element.99, pred[512]{0:T(512)(128)(4,1)S(1)} %fusion.180, bf16[512]{0:T(512)(128)(2,1)S(1)} %get-tuple-element.34, ...), kind=kOutput, calls=%fused_computation.100 | convolution fusion | flops 137625600 | bytes 797184 | tf_op jit(solution)/shard_map/dot_general | solution.py:57
  76.5 1.1 fusion.8
  77.6 1.4 %fusion.55 = f32[512,128]{1,0:T(8,128)S(1)} fusion(bf16[512,128]{1,0:T(8,128)(2,1)S(1)} %bitcast.152, s32[512]{0:T(512)S(1)} %get-tuple-element.22, s32[512]{0:T(512)S(1)} %get-tuple-element.98, s32[512]{0:T(512)S(1)} %get-tuple-element.99, pred[512]{0:T(512)(128)(4,1)S(1)} %fusion.180, bf16[512]{0:T(512)(128)(2,1)S(1)} %get-tuple-element.10, ...), kind=kOutput, calls=%fused_computation.77 | convolution fusion | flops 70516736 | bytes 403968 | tf_op jit(solution)/shard_map/dot_general | solution.py:57
  79.1 1.0 fusion.10
  80.1 1.4 %fusion.60 = f32[512,128]{1,0:T(8,128)S(1)} fusion(bf16[512,128]{1,0:T(8,128)(2,1)S(1)} %fusion.10, s32[512]{0:T(512)S(1)} %get-tuple-element.21, s32[512]{0:T(512)S(1)} %get-tuple-element.98, s32[512]{0:T(512)S(1)} %get-tuple-element.99, pred[512]{0:T(512)(128)(4,1)S(1)} %fusion.180, bf16[512]{0:T(512)(128)(2,1)S(1)} %get-tuple-element.14, ...), kind=kOutput, calls=%fused_computation.82 | convolution fusion | flops 70516736 | bytes 403968 | tf_op jit(solution)/shard_map/dot_general | solution.py:57
  81.6 1.1 fusion.17
  83.4 0.9 add_divide_fusion
  84.3 1.9 %collective-permute-start.2 = (bf16[2,512,128]{2,1,0:T(8,128)(2,1)S(1)}, bf16[2,512,128]{2,1,0:T(8,128)(2,1)S(1)}, u32[]{:S(2)}, u32[]{:S(2)}) collective-permute-start(bf16[2,512,128]{2,1,0:T(8,128)(2,1)S(1)} %pad_maximum_fusion.4), channel_id=1, source_target_pairs={{3,0},{0,1},{1,2},{2,3},{7,4},{4,5},{5,6},{6,7},{11,8},{8,9},{9,10... | collective-permute-start | bytes 786440 | tf_op jit(solution)/shard_map/ppermute | solution.py:130
  87.7 4.2 %collective-permute-done = bf16[2,512,128]{2,1,0:T(8,128)(2,1)S(1)} collective-permute-done((bf16[2,512,128]{2,1,0:T(8,128)(2,1)S(1)}, bf16[2,512,128]{2,1,0:T(8,128)(2,1)S(1)}, u32[]{:S(2)}, u32[]{:S(2)}) %collective-permute-start) | collective-permute-done | bytes 262176 | tf_op jit(solution)/shard_map/ppermute | solution.py:130
  92.6 4.4 %collective-permute-done.2 = bf16[2,512,128]{2,1,0:T(8,128)(2,1)S(1)} collective-permute-done((bf16[2,512,128]{2,1,0:T(8,128)(2,1)S(1)}, bf16[2,512,128]{2,1,0:T(8,128)(2,1)S(1)}, u32[]{:S(2)}, u32[]{:S(2)}) %collective-permute-start.2) | collective-permute-done | bytes 262176 | tf_op jit(solution)/shard_map/ppermute | solution.py:130
  99.0 2.4 %fusion.16 = bf16[512,128]{0,1:T(8,128)(2,1)} fusion(bf16[512,512]{1,0:T(8,128)(2,1)} %constant.154.clone, bf16[512,512]{1,0:T(8,128)(2,1)} %constant.155.clone, s32[]{:T(128)S(6)} %select_n.189, bf16[512,128]{1,0:T(8,128)(2,1)S(1)} %get-tuple-element.73, bf16[512,128]{1,0:T(8,128)(2,1)S(1)} %get-tuple-element.75, ...), kind=kOutput, calls=%fused_computation.27 | convolution fusion | flops 342687744 | bytes 2359300 | tf_op jit(solution)/shard_map/dot_general | solution.py:57
  102.7 2.0 %fusion.18 = bf16[512,128]{0,1:T(8,128)(2,1)S(1)} fusion(f32[512,512]{1,0:T(8,128)S(1)} %fusion.250, f32[512,512]{1,0:T(8,128)S(1)} %convolution_add_fusion.1, bf16[512,128]{1,0:T(8,128)(2,1)} %copy-done.21, bf16[512,128]{1,0:T(8,128)(2,1)} %constant.165, bf16[512,512]{1,0:T(8,128)(2,1)} %constant.155.clone, s32[]{:T(128)S(6)} %select_n.189, ...), kind=kOutput, calls=%fused_computation.29 | convolution fusion | flops 139788288 | bytes 3670020 | tf_op jit(solution)/shard_map/dot_general | solution.py:57
  104.8 1.3 convolution_convert_fusion.1
  106.1 0.8 fusion.9
  107.3 0.8 copy-done.4
  109.4 26.0 %all_to_all.10 = bf16[512,4,128]{2,1,0:T(4,128)(2,1)S(1)} all-to-all(bf16[512,4,128]{2,1,0:T(4,128)(2,1)S(1)} %copy.126), channel_id=1, replica_groups=mesh['start'=2,'pencil'=128] {'pencil'}, dimensions={0} | all-to-all | bytes 1048576 | tf_op jit(solution)/shard_map/all_to_all | solution.py:160
  137.3 1.2 convolution_add_fusion.2
  (173 shorter events, 31.4 us)
Async XLA Ops:
  0.6 16.4 %copy-start = (bf16[4,32,512]{2,1,0:T(8,128)(2,1)S(1)}, bf16[4,32,512]{2,1,0:T(8,128)(2,1)}, u32[]{:S(2)}) copy-start(bf16[4,32,512]{2,1,0:T(8,128)(2,1)} %param.14) | copy-start | bytes 393220
  15.7 0.9 copy-start.13
  20.9 46.3 %all-to-all-start = ((bf16[1024,4,128]{2,1,0:T(4,128)(2,1)}), bf16[1024,4,128]{2,1,0:T(4,128)(2,1)S(1)}, u32[]{:S(2)}, u32[]{:S(2)}) async-start(bf16[1024,4,128]{2,1,0:T(4,128)(2,1)} %copy.110), calls=%async_computation | async-start | bytes 2097152 | tf_op jit(solution)/shard_map/all_to_all | solution.py:104
  73.6 24.8 %copy-start.9 = (bf16[128,1,4,128]{3,2,0,1:T(4,128)(2,1)}, bf16[128,1,4,128]{3,2,0,1:T(4,128)(2,1)S(1)}, u32[]{:S(2)}) copy-start(bf16[128,1,4,128]{3,2,0,1:T(4,128)(2,1)S(1)} %copy.112) | copy-start | bytes 393220
  77.6 20.8 %copy-start.3 = (bf16[512,128]{1,0:T(8,128)(2,1)}, bf16[512,128]{1,0:T(8,128)(2,1)S(1)}, u32[]{:S(2)}) copy-start(bf16[512,128]{1,0:T(8,128)(2,1)S(1)} %get-tuple-element.78) | copy-start | bytes 393220
  83.3 3.5 %copy-start.8 = (bf16[512,128]{1,0:T(8,128)(2,1)S(1)}, bf16[512,128]{1,0:T(8,128)(2,1)}, u32[]{:S(2)}) copy-start(bf16[512,128]{1,0:T(8,128)(2,1)} %constant.163) | copy-start | bytes 393220
  83.3 8.6 %collective-permute-start = (bf16[2,512,128]{2,1,0:T(8,128)(2,1)S(1)}, bf16[2,512,128]{2,1,0:T(8,128)(2,1)S(1)}, u32[]{:S(2)}, u32[]{:S(2)}) collective-permute-start(bf16[2,512,128]{2,1,0:T(8,128)(2,1)S(1)} %pad_maximum_fusion.4), channel_id=1, source_target_pairs={{1,0},{2,1},{3,2},{0,3},{5,4},{6,5},{7,6},{4,7},{9,8},{10,9},{11,1... | collective-permute-start | bytes 786440 | tf_op jit(solution)/shard_map/ppermute | solution.py:130
  84.3 12.6 %collective-permute-start.2 = (bf16[2,512,128]{2,1,0:T(8,128)(2,1)S(1)}, bf16[2,512,128]{2,1,0:T(8,128)(2,1)S(1)}, u32[]{:S(2)}, u32[]{:S(2)}) collective-permute-start(bf16[2,512,128]{2,1,0:T(8,128)(2,1)S(1)} %pad_maximum_fusion.4), channel_id=1, source_target_pairs={{3,0},{0,1},{1,2},{2,3},{7,4},{4,5},{5,6},{6,7},{11,8},{8,9},{9,10... | collective-permute-start | bytes 786440 | tf_op jit(solution)/shard_map/ppermute | solution.py:130
  86.3 11.4 %collective-permute-start.1 = (bf16[2,512,128]{2,1,0:T(8,128)(2,1)S(1)}, bf16[2,512,128]{2,1,0:T(8,128)(2,1)S(1)}, u32[]{:S(2)}, u32[]{:S(2)}) collective-permute-start(bf16[2,512,128]{2,1,0:T(8,128)(2,1)S(1)} %pad_maximum_fusion.4), channel_id=1, source_target_pairs={{2,0},{3,1},{0,2},{1,3},{6,4},{7,5},{4,6},{5,7},{10,8},{11,9},{8,1... | collective-permute-start | bytes 786440 | tf_op jit(solution)/shard_map/ppermute | solution.py:130
  87.3 11.1 %copy-start.10 = (bf16[128,1,4,128]{3,2,0,1:T(4,128)(2,1)}, bf16[128,1,4,128]{3,2,0,1:T(4,128)(2,1)S(1)}, u32[]{:S(2)}) copy-start(bf16[128,1,4,128]{3,2,0,1:T(4,128)(2,1)S(1)} %copy.113) | copy-start | bytes 393220
  87.5 10.9 %copy-start.11 = (bf16[128,1,4,128]{3,2,0,1:T(4,128)(2,1)}, bf16[128,1,4,128]{3,2,0,1:T(4,128)(2,1)S(1)}, u32[]{:S(2)}) copy-start(bf16[128,1,4,128]{3,2,0,1:T(4,128)(2,1)S(1)} %copy.114) | copy-start | bytes 393220
  87.7 10.7 %copy-start.12 = (bf16[128,1,4,128]{3,2,0,1:T(4,128)(2,1)}, bf16[128,1,4,128]{3,2,0,1:T(4,128)(2,1)S(1)}, u32[]{:S(2)}) copy-start(bf16[128,1,4,128]{3,2,0,1:T(4,128)(2,1)S(1)} %copy.115) | copy-start | bytes 393220
  92.6 5.8 %copy-start.18 = (bf16[512,128]{1,0:T(8,128)(2,1)}, bf16[512,128]{1,0:T(8,128)(2,1)S(1)}, u32[]{:S(2)}) copy-start(bf16[512,128]{1,0:T(8,128)(2,1)S(1)} %get-tuple-element.71) | copy-start | bytes 393220
  99.0 2.4 %copy-start.7 = (bf16[512,128]{1,0:T(8,128)(2,1)S(1)}, bf16[512,128]{1,0:T(8,128)(2,1)}, u32[]{:S(2)}) copy-start(bf16[512,128]{1,0:T(8,128)(2,1)} %constant.166) | copy-start | bytes 393220
  102.6 2.1 %copy-start.15 = (bf16[512,128]{1,0:T(8,128)(2,1)S(1)}, bf16[512,128]{1,0:T(8,128)(2,1)}, u32[]{:S(2)}) copy-start(bf16[512,128]{1,0:T(8,128)(2,1)} %copy-done.14) | copy-start | bytes 393220
  102.7 2.1 %copy-start.16 = (bf16[512,128]{1,0:T(8,128)(2,1)S(1)}, bf16[512,128]{1,0:T(8,128)(2,1)}, u32[]{:S(2)}) copy-start(bf16[512,128]{1,0:T(8,128)(2,1)} %get-tuple-element.72) | copy-start | bytes 393220
  102.7 2.1 %copy-start.17 = (bf16[512,128]{1,0:T(8,128)(2,1)S(1)}, bf16[512,128]{1,0:T(8,128)(2,1)}, u32[]{:S(2)}) copy-start(bf16[512,128]{1,0:T(8,128)(2,1)} %get-tuple-element.74) | copy-start | bytes 393220
  102.7 2.1 %copy-start.19 = (bf16[512,128]{1,0:T(8,128)(2,1)S(1)}, bf16[512,128]{1,0:T(8,128)(2,1)}, u32[]{:S(2)}) copy-start(bf16[512,128]{1,0:T(8,128)(2,1)} %get-tuple-element.76) | copy-start | bytes 393220
  104.7 1.3 copy-start.5
  104.8 1.3 copy-start.26
  104.8 1.3 copy-start.27
  107.2 0.9 copy-start.4
  135.9 1.0 copy-start.2
  136.1 1.2 copy-start.1
  (8 other events, 5.8 us)

commit v2 on v1

v2 whole, which is shorter than its diff:
```python
import math

import jax
import jax.numpy as jnp
import numpy as np
from jax import lax
from jax.experimental import pallas as pl
from jax.experimental.pallas import tpu as pltpu
from jax.sharding import PartitionSpec as P

Q = 16
N = 512
H1_WEIGHT = 64.0
FORCE_GAIN = 32.0
ROWS = 24
BF = jnp.bfloat16
F32 = jnp.float32
NN = ((1,), (0,))
NT = ((1,), (1,))


def wave_numbers():
    k = np.arange(N)
    signed = np.where(k < N // 2, k, k - N)
    signed = np.where(k == N // 2, 0, signed)
    return signed * (2.0 * math.pi / N)


def derivative_matrix():
    k = np.arange(N)
    lag = np.arange(N)
    row = (np.sin(2.0 * math.pi * ((k[:, None] * lag[None, :]) % N) / N) * wave_numbers()[:, None]).sum(0) / N
    return row[(lag[None, :] - lag[:, None]) % N]


def modes():
    return np.concatenate([np.arange(N // 2 + 1), np.arange(1, N // 2)])


def basis(points):
    angle = 2.0 * math.pi * ((modes()[:, None] * points[None, :]) % N) / N
    is_cos = (np.arange(N) <= N // 2)[:, None]
    return np.where(is_cos, np.cos(angle), np.sin(angle))


def pack_rows():
    pick = np.zeros((32, ROWS // 4, 4, 384), np.float32)
    for z in range(32):
        other = (z + (1 if z % 2 else -1)) % 32
        for x in range(4):
            pick[z, 0, x, x * 32 + z] = 1
            pick[z, 1, x, x * 32 + (z ^ 1)] = 1
            pick[z, 2, x, x * 32 + other] = 1
            pick[z, 3, x, 128 + x * 32 + z] = 1
            pick[z, 4, x, 256 + z * 4 + x] = 1
    return pick.reshape(32 * ROWS, 384)


def bf(x):
    return jnp.asarray(np.asarray(x, np.float32), BF)


def dot(a, b, dims=NN):
    return lax.dot_general(a, b, (dims, ((), ())), preferred_element_type=F32)


def iota(shape, axis):
    return lax.broadcasted_iota(jnp.int32, shape, axis)


def cubic(level):
    t = (level + 0.5) / Q
    return [
        -t * (t - 1.0) * (t - 2.0) / 6.0,
        (t + 1.0) * (t - 1.0) * (t - 2.0) / 2.0,
        -(t + 1.0) * t * (t - 2.0) / 2.0,
        (t + 1.0) * t * (t - 1.0) / 6.0,
    ]


def pack_kernel(me_ref, template_ref, image_ref, owner_ref, offset_ref, weight_ref, pick_ref, out_ref):
    me = me_ref[0]
    move = ((owner_ref[...] - me + 130) & 127) - 2
    rel = (move * 4 + (offset_ref[...] >> 6)).astype(F32)
    level = weight_ref[...].astype(F32)
    row = iota((128, 256), 0)
    second = ((row >> 4) & 1) == 1
    rel = jnp.where(second, rel[1:2], rel[0:1])
    taps = cubic(jnp.where(second, level[1:2], level[0:1]))
    item = row & 15
    value = jnp.where(item == 0, rel, 0.0)
    for k in range(4):
        high = taps[k].astype(BF).astype(F32)
        value = jnp.where(item == 1 + k, high, value)
        value = jnp.where(item == 5 + k, taps[k] - high, value)
    near = jnp.where(row < 32, value, 0.0).astype(BF)
    far = jnp.where((row >= 32) & (row < 64), value, 0.0).astype(BF)
    col = iota((128, 256), 1)
    z = row >> 2
    other = (z + 2 * (z & 1) - 1) & 31
    at_near = (row & 3) * 64 + (z >> 1) * 4
    at_far = (row & 3) * 64 + (other >> 1) * 4
    template = template_ref[...].reshape(128, N)
    image = image_ref[...].reshape(128, N)
    pick = pick_ref[...]
    for q in range(4):
        lanes = slice(128 * q, 128 * q + 128)
        hot_near = jnp.where(col == at_near + q, 1.0, 0.0).astype(BF)
        hot_far = jnp.where(col == at_far + q, 1.0, 0.0).astype(BF)
        codes = (dot(hot_near, near, NT) + dot(hot_far, far, NT)).astype(BF)
        stack = jnp.concatenate([template[:, lanes], image[:, lanes], codes], axis=0)
        out_ref[:, q] = dot(pick, stack).reshape(32, ROWS, 128).astype(BF)


def split(v):
    v = v.reshape(64, 2, 8, 128)
    a, b = v[:, 0], v[:, 1]
    low = iota((64, 8, 128), 1) < 4
    first = jnp.where(low, a, pltpu.roll(b, 4, 1))
    last = jnp.where(low, pltpu.roll(a, 4, 1), b)
    return first.reshape(N, 128), last.reshape(N, 128)


def fill(high_ref, low_ref, codes, at):
    for i in range(4):
        part = codes[128 * i : 128 * i + 128]
        rel = part[:, at : at + 1]
        high = [part[:, at + 1 + k : at + 2 + k] for k in range(4)]
        low = [part[:, at + 5 + k : at + 6 + k] for k in range(4)]
        for tile, first, count in ((0, 0, 128), (-1, 0, 16), (1, 112, 16)):
            rows = slice(first, first + count)
            row = iota((count, 128), 0) + first
            lag = (iota((count, 128), 1) + 128 * tile - (row & -4)).astype(F32) - rel[rows]
            h = jnp.zeros((count, 128), F32)
            l = h
            for k in range(4):
                h = jnp.where(lag == k, high[k][rows], h)
                l = jnp.where(lag == k, low[k][rows], l)
            j = (i + tile) % 4
            where = (slice(128 * i + first, 128 * i + first + count), slice(128 * j, 128 * j + 128))
            high_ref[where] = h.astype(BF)
            low_ref[where] = l.astype(BF)


def transport_kernel(sign_ref, got_ref, out_ref, high_a, low_a, high_b, low_b):
    for ref in (high_a, low_a, high_b, low_b):
        ref[...] = jnp.zeros((N, N), BF)
    own, partner = split(got_ref[:, 0:8, :].astype(F32))
    other, image = split(got_ref[:, 8:16, :].astype(F32))
    codes, _ = split(got_ref[:, 16:24, :].astype(F32))
    near = jnp.concatenate([own, partner], axis=1).astype(BF)
    other = other.astype(BF)
    for section in range(2):
        fill(high_a, low_a, codes, 16 * section)
        fill(high_b, low_b, codes, 32 + 16 * section)
        near = (dot(high_a[...], near) + dot(low_a[...], near)).astype(BF)
        other = (dot(high_b[...], other) + dot(low_b[...], other)).astype(BF)
    warped = near[:, :128]
    slope = (near[:, 128:].astype(F32) - other.astype(F32)) * sign_ref[0]
    out_ref[0] = warped
    out_ref[1] = image.astype(BF)
    out_ref[2] = ((image - warped.astype(F32)) * slope).astype(BF)


def smooth_kernel(quarter_ref, p0_ref, p1_ref, p2_ref, p3_ref, deriv_ref, table_ref, flip_ref, wave_ref, wy_ref, out_ref):
    parts = (p0_ref, p1_ref, p2_ref, p3_ref)
    warped = jnp.concatenate([p[0] for p in parts], axis=1)
    deriv = deriv_ref[...]
    mine = flip_ref[:, pl.ds(pl.multiple_of(quarter_ref[0] * 128, 128), 128)]
    slope_x = dot(deriv, warped)
    slope_y = dot(warped, deriv)
    image = jnp.concatenate([p[1] for p in parts], axis=1).astype(F32)
    residual = image - warped.astype(F32)
    force_x = (residual * slope_x).astype(BF)
    force_y = (residual * (-slope_y)).astype(BF)
    force_z = jnp.concatenate([p[2] for p in parts], axis=1)
    spec = jnp.concatenate([dot(f, mine).astype(BF) for f in (force_x, force_y, force_z)], axis=1)
    wave_x = wave_ref[:, 0:1]
    scale_x = wave_ref[:, 1:2]
    gain = (scale_x * wy_ref[1:2]) / (1.0 + H1_WEIGHT * (wave_x * wave_x + wy_ref[0:1] * wy_ref[0:1]))
    bent = dot(table_ref[...], spec)
    bent = jnp.concatenate([bent[:, 128 * c : 128 * c + 128] * gain for c in range(3)], axis=1).astype(BF)
    back = dot(flip_ref[...], bent)
    a = [back[:, 128 * c : 128 * c + 128].reshape(64, 8, 128) for c in range(3)]
    a.append(warped[:, :128].astype(F32).reshape(64, 8, 128))
    low = iota((64, 8, 128), 1) < 4
    turned = [pltpu.roll(v, 4, 1) for v in a]
    even = [jnp.where(low, a[j], turned[j + 1]) for j in (0, 2)]
    odd = [jnp.where(low, turned[j], a[j + 1]) for j in (0, 2)]
    out_ref[:, 0] = jnp.concatenate(even, axis=1).astype(BF)
    out_ref[:, 1] = jnp.concatenate(odd, axis=1).astype(BF)


def call(kernel, out, scratch=(), scalars=1, inputs=1):
    return pl.pallas_call(
        kernel,
        out_shape=jax.ShapeDtypeStruct(out, BF),
        in_specs=[pl.BlockSpec(memory_space=pltpu.SMEM)] * scalars
        + [pl.BlockSpec(memory_space=pltpu.VMEM)] * inputs,
        out_specs=pl.BlockSpec(memory_space=pltpu.VMEM),
        scratch_shapes=list(scratch),
        compiler_params=pltpu.CompilerParams(vmem_limit_bytes=48 << 20),
    )


def local(template, reference_image, velocity, dep_owner, dep_offset, dep_weight):
    me = lax.axis_index("pencil")
    quarter = me % 4
    sign = jnp.where((me // 4) % 2 == 0, 0.5, -0.5).astype(F32)

    pack = call(pack_kernel, (32, 4, ROWS, 128), inputs=6)(
        me.reshape(1), template, reference_image, dep_owner, dep_offset, dep_weight, bf(pack_rows())
    )
    got = lax.all_to_all(pack.reshape(128, ROWS, 128), "pencil", 0, 0, tiled=True)

    payload = call(transport_kernel, (3, N, 128), scratch=[pltpu.VMEM((N, N), BF)] * 4)(
        sign.reshape(1), got
    )
    parts = [payload]
    for s in (1, 2, 3):
        parts.append(
            lax.ppermute(payload, "pencil", [((i // 4) * 4 + (i + s) % 4, i) for i in range(128)])
        )

    table = basis(np.arange(N))
    k = modes()
    wave = wave_numbers()[k]
    weight = np.where((k == 0) | (k == N // 2), 1.0, 2.0)
    wave_x = np.zeros((N, 128), np.float32)
    wave_x[:, 0] = wave
    wave_x[:, 1] = weight * FORCE_GAIN / (N * N)
    wave_y = np.zeros((4, 8, 128), np.float32)
    wave_y[:, 0] = wave.reshape(4, 128)
    wave_y[:, 1] = weight.reshape(4, 128)
    wave_y = lax.dynamic_index_in_dim(jnp.asarray(wave_y), quarter, keepdims=False)
    send = call(smooth_kernel, (64, 2, 16, 128), inputs=9)(
        quarter.reshape(1), *parts, bf(derivative_matrix()), bf(table), bf(table.T), jnp.asarray(wave_x), wave_y
    )
    home = lax.all_to_all(send.reshape(128, 16, 128), "pencil", 0, 0, tiled=True)

    rows = home.reshape(32, 4, 16, 128).transpose(0, 2, 1, 3).reshape(N, N)
    target = np.zeros((N, N), np.float32)
    r = np.arange(N)
    target[r, (r % 32) * 16 + r // 32] = 1
    rows = dot(bf(target), rows).astype(BF)
    inverse = np.concatenate([basis((np.arange(N) - 128 * q) % N)[128 * q : 128 * q + 128] for q in range(4)])
    spatial = dot(rows[:384], bf(inverse))
    return rows[384:].reshape(4, 32, N), velocity + spatial.reshape(3, 4, 32, N)


def solution(mesh):
    in_specs = (
        P("pencil", "start", None),
        P("pencil", "start", None),
        P("start", "pencil", None, None),
        P("start", "pencil"),
        P("start", "pencil"),
        P("start", "pencil"),
    )
    out_specs = (P("pencil", "start", None), P("start", "pencil", None, None))
    return jax.shard_map(local, mesh=mesh, in_specs=in_specs, out_specs=out_specs, check_vma=False)
```

time: 139 us -> 104 us (0.75)
  local copies, waits for them, and re-layouts: 33.4 us -> 6.73 us
  matrix products: 17.6 us -> 0.8 us
  Pallas kernels: 0 us -> 6.29 us
  other arithmetic: 4.12 us -> 1.02 us
  waiting for transfers between devices: 37.9 us -> 40.6 us
  blocking collectives: 26 us -> 28.7 us
    dot_general x16 -> x2, matrix products: 17.6 us -> 0.8 us  [dot(): return lax.dot_general(a, b, (dims, ((), ())), preferred_element_type=F32)]
    another operation x40 -> x0, local copies, waits for them, and re-layouts: 13.5 us -> none  [the longest x37 12.4 us: local(): codes = jnp.stack(codes, axis=0).reshape(18, 4, 16, 4).transpose(2, 3, 1, 0)]
    slice x27 -> x1, local copies, waits for them, and re-layouts: 7.21 us -> 0.66 us  [local(): rows[384:].reshape(4, 32, N)]
    ppermute x3, waiting for transfers between devices: 8.6 us -> 15.1 us  [local(): lax.ppermute(payload, 'pencil', [(i // 4 * 4 + (i + s) % 4, i) for i in r...]
    pallas_call x0 -> x3, Pallas kernels: none -> 6.29 us  [the longest x1 2.24 us: local(): call(pack_kernel, (32, 4, ROWS, 128), inputs=6)]
    all_to_all x1, waiting for transfers between devices: 29.3 us -> 25.5 us  [local(): lax.all_to_all(pack.reshape(128, ROWS, 128), 'pencil', 0, 0, tiled=True)]
    reshape x5 -> x0, local copies, waits for them, and re-layouts: 3.02 us -> none  [the longest x1 1.8 us: local(): pack = jnp.stack([planes, partner(planes), other(planes)] + [jnp.roll(ima...]
    all_to_all x1, blocking collectives: 26 us -> 28.7 us  [local(): lax.all_to_all(send.reshape(128, 16, 128), 'pencil', 0, 0, tiled=True)]
  transfers between devices with their start and end apart: 4 -> 4, of which waited for: 3 -> 3; matrix products, arithmetic and copies ran while one was open for 3% -> 1% of each run, Pallas kernels for 0% -> 0%
where the time goes in v2:
time: 104 us
  waiting for transfers between devices  40.6 us (39%)
  blocking collectives  28.7 us (28%)
  starting transfers between devices  18.9 us (18%)
  local copies, waits for them, and re-layouts  6.73 us (6%)
  Pallas kernels  6.29 us (6%)
    all_to_all x1, blocking collectives, local(): lax.all_to_all(send.reshape(128, 16, 128), 'pencil', 0, 0, tiled=True)  28.7 us
    all_to_all x1, waiting for transfers between devices, local(): lax.all_to_all(pack.reshape(128, ROWS, 128), 'pencil', 0, 0, tiled=True)  25.5 us
    all_to_all x1, starting transfers between devices, local(): lax.all_to_all(pack.reshape(128, ROWS, 128), 'pencil', 0, 0, tiled=True)  15.6 us
    ppermute x3, waiting for transfers between devices, local(): lax.ppermute(payload, 'pencil', [(i // 4 * 4 + (i + s) % 4, i) for i in r...  15.1 us
    unnamed x26, local copies, waits for them, and re-layouts  5.13 us
    ppermute x3, starting transfers between devices, local(): lax.ppermute(payload, 'pencil', [(i // 4 * 4 + (i + s) % 4, i) for i in r...  3.32 us
    pallas_call x1, Pallas kernels, local(): call(pack_kernel, (32, 4, ROWS, 128), inputs=6)  2.24 us
    pallas_call x1, Pallas kernels, local(): call(transport_kernel, (3, N, 128), scratch=[pltpu.VMEM((N, N), BF)] * 4)  2.24 us
  transfers between devices with their start and end apart: 4, of which 3 were waited for; matrix products, arithmetic and copies ran while one was open for 1% of the time, Pallas kernels for 0%

profile of v2, /device:TPU:2, one launch (start us, length us, event | category | flops | bytes accessed | tf_op | source)
XLA Modules:
  0.0 103.8 jit_solution(5212552341396334704)
XLA Ops:
  0.7 0.7 copy-done.9
  1.3 0.0 copy-done.8
  1.3 1.1 %copy-done = bf16[768,384]{1,0:T(8,128)(2,1)S(1)} copy-done((bf16[768,384]{1,0:T(8,128)(2,1)S(1)}, bf16[768,384]{1,0:T(8,128)(2,1)}, u32[]{:S(2)}) %copy-start) | copy-done | bytes 589848
  2.4 0.9 copy-done.5
  3.3 0.9 copy-done.6
  4.2 2.2 %shard_map.149 = bf16[32,4,24,128]{3,2,1,0:T(8,128)(2,1)} custom-call(s32[1]{0:T(128)} %bitcast.2.me_ref, bf16[4,32,512]{2,1,0:T(8,128)(2,1)S(1)} %copy-done.5, bf16[4,32,512]{2,1,0:T(8,128)(2,1)S(1)} %copy-done.6, s32[2,256]{1,0:T(2,128)S(1)} %copy-done.7, s32[2,256]{1,0:T(2,128)S(1)} %copy-done.8, s32[2,256]{1,0:T(2,128)S(1)} %copy-done.9, ...), custom_call_target="tpu_custom_call" | custom-call | tf_op jit(solution)/shard_map/pallas_call | solution.py:211
  6.5 15.6 %all-to-all-start = ((bf16[128,24,128]{2,1,0:T(8,128)(2,1)}), bf16[128,24,128]{2,1,0:T(8,128)(2,1)S(1)}, u32[]{:S(2)}, u32[]{:S(2)}) async-start(bf16[128,24,128]{2,1,0:T(8,128)(2,1)} %bitcast.3), calls=%async_computation | async-start | bytes 1572864 | tf_op jit(solution)/shard_map/all_to_all | solution.py:214
  22.1 25.5 %all-to-all-done.got_ref = bf16[128,24,128]{2,1,0:T(8,128)(2,1)S(1)} async-done(((bf16[128,24,128]{2,1,0:T(8,128)(2,1)}), bf16[128,24,128]{2,1,0:T(8,128)(2,1)S(1)}, u32[]{:S(2)}, u32[]{:S(2)}) %all-to-all-start) | async-done | bytes 786464 | tf_op jit(solution)/shard_map/all_to_all | solution.py:214
  47.6 2.2 %shard_map.150.p0_ref = bf16[3,512,128]{2,1,0:T(8,128)(2,1)S(1)} custom-call(f32[1]{0:T(128)} %bitcast.1.sign_ref, bf16[128,24,128]{2,1,0:T(8,128)(2,1)S(1)} %all-to-all-done.got_ref), custom_call_target="tpu_custom_call" | custom-call | tf_op jit(solution)/shard_map/pallas_call | solution.py:216
  49.8 0.4 collective-permute-start.2
  50.2 0.9 collective-permute-start.1
  51.1 2.1 %collective-permute-start = (bf16[3,512,128]{2,1,0:T(8,128)(2,1)S(1)}, bf16[3,512,128]{2,1,0:T(8,128)(2,1)S(1)}, u32[]{:S(2)}, u32[]{:S(2)}) collective-permute-start(bf16[3,512,128]{2,1,0:T(8,128)(2,1)S(1)} %shard_map.150.p0_ref), channel_id=1, source_target_pairs={{1,0},{2,1},{3,2},{0,3},{5,4},{6,5},{7,6},{4,7},{9,8},{10,9},{11,1... | collective-permute-start | bytes 1179656 | tf_op jit(solution)/shard_map/ppermute | solution.py:222
  53.1 0.7 dynamic-slice_bitcast_fusion.wy_ref
  53.8 14.5 %collective-permute-done.2.p3_ref = bf16[3,512,128]{2,1,0:T(8,128)(2,1)S(1)} collective-permute-done((bf16[3,512,128]{2,1,0:T(8,128)(2,1)S(1)}, bf16[3,512,128]{2,1,0:T(8,128)(2,1)S(1)}, u32[]{:S(2)}, u32[]{:S(2)}) %collective-permute-start.2) | collective-permute-done | bytes 393248 | tf_op jit(solution)/shard_map/ppermute | solution.py:222
  68.3 0.6 collective-permute-done.p1_ref
  68.9 1.8 %shard_map.151 = bf16[64,2,16,128]{3,2,1,0:T(8,128)(2,1)S(1)} custom-call(s32[1]{0:T(128)} %bitcast.quarter_ref, bf16[3,512,128]{2,1,0:T(8,128)(2,1)S(1)} %shard_map.150.p0_ref, bf16[3,512,128]{2,1,0:T(8,128)(2,1)S(1)} %collective-permute-done.p1_ref, bf16[3,512,128]{2,1,0:T(8,128)(2,1)S(1)} %collective-permute-done.1.p2_ref, ...), custom_call_target="tpu_custom_call" | custom-call | tf_op jit(solution)/shard_map/pallas_call | solution.py:236
  70.8 28.7 %all_to_all.10 = bf16[128,16,128]{2,1,0:T(8,128)(2,1)S(1)} all-to-all(bf16[128,16,128]{2,1,0:T(8,128)(2,1)S(1)} %bitcast.21), channel_id=1, replica_groups=mesh['start'=2,'pencil'=128] {'pencil'}, dimensions={0} | all-to-all | bytes 1048576 | tf_op jit(solution)/shard_map/all_to_all | solution.py:239
  99.5 0.2 copy.16
  99.8 0.8 copy-done.12
  100.6 0.4 fusion
  101.0 0.7 slice.8
  101.7 0.4 fusion.3
  102.0 0.8 copy-done.10
  102.8 1.0 add.18
  (20 shorter events, 0.1 us)
Async XLA Ops:
  0.6 0.7 copy-start.9
  0.6 0.7 copy-start.8
  0.7 0.7 copy-start.7
  1.3 1.1 %copy-start = (bf16[768,384]{1,0:T(8,128)(2,1)S(1)}, bf16[768,384]{1,0:T(8,128)(2,1)}, u32[]{:S(2)}) copy-start(bf16[768,384]{1,0:T(8,128)(2,1)} %constant.63.clone.pick_ref) | copy-start | bytes 1769476
  2.4 0.9 copy-start.5
  3.3 0.9 copy-start.6
  6.5 62.5 %copy-start.3 = (bf16[512,512]{1,0:T(8,128)(2,1)S(1)}, bf16[512,512]{1,0:T(8,128)(2,1)}, u32[]{:S(2)}) copy-start(bf16[512,512]{1,0:T(8,128)(2,1)} %constant.65.clone.deriv_ref) | copy-start | bytes 1572868
  6.5 62.5 %copy-start.4 = (f32[512,128]{1,0:T(8,128)S(1)}, f32[512,128]{1,0:T(8,128)}, u32[]{:S(2)}) copy-start(f32[512,128]{1,0:T(8,128)} %constant.68.clone.wave_ref) | copy-start | bytes 786436
  6.5 41.1 %all-to-all-start = ((bf16[128,24,128]{2,1,0:T(8,128)(2,1)}), bf16[128,24,128]{2,1,0:T(8,128)(2,1)S(1)}, u32[]{:S(2)}, u32[]{:S(2)}) async-start(bf16[128,24,128]{2,1,0:T(8,128)(2,1)} %bitcast.3), calls=%async_computation | async-start | bytes 1572864 | tf_op jit(solution)/shard_map/all_to_all | solution.py:214
  47.6 21.4 %copy-start.1 = (bf16[512,512]{1,0:T(8,128)(2,1)S(1)}, bf16[512,512]{1,0:T(8,128)(2,1)}, u32[]{:S(2)}) copy-start(bf16[512,512]{1,0:T(8,128)(2,1)} %constant.67.clone.flip_ref) | copy-start | bytes 1572868
  47.6 21.4 %copy-start.2 = (bf16[512,512]{1,0:T(8,128)(2,1)S(1)}, bf16[512,512]{1,0:T(8,128)(2,1)}, u32[]{:S(2)}) copy-start(bf16[512,512]{1,0:T(8,128)(2,1)} %constant.66.clone.table_ref) | copy-start | bytes 1572868
  49.8 18.5 %collective-permute-start.2 = (bf16[3,512,128]{2,1,0:T(8,128)(2,1)S(1)}, bf16[3,512,128]{2,1,0:T(8,128)(2,1)S(1)}, u32[]{:S(2)}, u32[]{:S(2)}) collective-permute-start(bf16[3,512,128]{2,1,0:T(8,128)(2,1)S(1)} %shard_map.150.p0_ref), channel_id=1, source_target_pairs={{3,0},{0,1},{1,2},{2,3},{7,4},{4,5},{5,6},{6,7},{11,8},{8,9},{9,10... | collective-permute-start | bytes 1179656 | tf_op jit(solution)/shard_map/ppermute | solution.py:222
  50.2 18.1 %collective-permute-start.1 = (bf16[3,512,128]{2,1,0:T(8,128)(2,1)S(1)}, bf16[3,512,128]{2,1,0:T(8,128)(2,1)S(1)}, u32[]{:S(2)}, u32[]{:S(2)}) collective-permute-start(bf16[3,512,128]{2,1,0:T(8,128)(2,1)S(1)} %shard_map.150.p0_ref), channel_id=1, source_target_pairs={{2,0},{3,1},{0,2},{1,3},{6,4},{7,5},{4,6},{5,7},{10,8},{11,9},{8,1... | collective-permute-start | bytes 1179656 | tf_op jit(solution)/shard_map/ppermute | solution.py:222
  51.1 17.9 %collective-permute-start = (bf16[3,512,128]{2,1,0:T(8,128)(2,1)S(1)}, bf16[3,512,128]{2,1,0:T(8,128)(2,1)S(1)}, u32[]{:S(2)}, u32[]{:S(2)}) collective-permute-start(bf16[3,512,128]{2,1,0:T(8,128)(2,1)S(1)} %shard_map.150.p0_ref), channel_id=1, source_target_pairs={{1,0},{2,1},{3,2},{0,3},{5,4},{6,5},{7,6},{4,7},{9,8},{10,9},{11,1... | collective-permute-start | bytes 1179656 | tf_op jit(solution)/shard_map/ppermute | solution.py:222
  99.5 1.0 %copy-start.12 = (bf16[512,512]{1,0:T(8,128)(2,1)S(1)}, bf16[512,512]{1,0:T(8,128)(2,1)}, u32[]{:S(2)}) copy-start(bf16[512,512]{1,0:T(8,128)(2,1)} %constant.69.clone) | copy-start | bytes 1572868
  100.6 1.1 %copy-start.11 = (bf16[512,512]{1,0:T(8,128)(2,1)S(1)}, bf16[512,512]{1,0:T(8,128)(2,1)}, u32[]{:S(2)}) copy-start(bf16[512,512]{1,0:T(8,128)(2,1)} %constant.70.clone) | copy-start | bytes 1572868
  101.7 1.1 %copy-start.10 = (f32[3,4,32,512]{3,2,1,0:T(8,128)S(1)}, f32[3,4,32,512]{3,2,1,0:T(8,128)}, u32[]{:S(2)}) copy-start(f32[3,4,32,512]{3,2,1,0:T(8,128)} %param.16) | copy-start | bytes 2359300

commit v3 on v2

v3 whole, which is shorter than its diff:
```python
import math

import jax
import jax.numpy as jnp
import numpy as np
from jax import lax
from jax.experimental import pallas as pl
from jax.experimental.pallas import tpu as pltpu
from jax.sharding import PartitionSpec as P

Q = 16
N = 512
H1_WEIGHT = 64.0
FORCE_GAIN = 32.0
BF = jnp.bfloat16
F32 = jnp.float32
NN = ((1,), (0,))
NT = ((1,), (1,))


def wave_numbers():
    k = np.arange(N)
    signed = np.where(k < N // 2, k, k - N)
    signed = np.where(k == N // 2, 0, signed)
    return signed * (2.0 * math.pi / N)


def derivative_matrix():
    k = np.arange(N)
    lag = np.arange(N)
    row = (np.sin(2.0 * math.pi * ((k[:, None] * lag[None, :]) % N) / N) * wave_numbers()[:, None]).sum(0) / N
    return row[(lag[None, :] - lag[:, None]) % N]


def modes():
    return np.concatenate([np.arange(N // 2 + 1), np.arange(1, N // 2)])


def basis(points):
    angle = 2.0 * math.pi * ((modes()[:, None] * points[None, :]) % N) / N
    is_cos = (np.arange(N) <= N // 2)[:, None]
    return np.where(is_cos, np.cos(angle), np.sin(angle))


def pack_rows():
    pick = np.zeros((32, 6, 4, 384), np.float32)
    for z in range(32):
        other = (z + (1 if z % 2 else -1)) % 32
        for x in range(4):
            pick[z, 0, x, x * 32 + z] = 1
            pick[z, 1, x, x * 32 + (z ^ 1)] = 1
            pick[z, 2, x, x * 32 + other] = 1
            pick[z, 3, x, 128 + x * 32 + z] = 1
            pick[z, 4, x, 256 + z * 4 + x] = 1
            pick[z, 5, x, 256 + z * 4 + x] = 1
    return pick.reshape(768, 384)


def unpack_rows():
    r = np.arange(N)
    pick = np.zeros((N, N), np.float32)
    pick[r, (r % 32) * 16 + (r // 128) * 4 + (r // 32) % 4] = 1
    return pick


def bf(x):
    return jnp.asarray(np.asarray(x, np.float32), BF)


def dot(a, b, dims=NN):
    return lax.dot_general(a, b, (dims, ((), ())), preferred_element_type=F32)


def iota(shape, axis):
    return lax.broadcasted_iota(jnp.int32, shape, axis)


def cubic(level):
    t = (level + 0.5) / Q
    return [
        -t * (t - 1.0) * (t - 2.0) / 6.0,
        (t + 1.0) * (t - 1.0) * (t - 2.0) / 2.0,
        -(t + 1.0) * t * (t - 2.0) / 2.0,
        (t + 1.0) * t * (t - 1.0) / 6.0,
    ]


def mode_waves(shape, axis):
    i = iota(shape, axis)
    k = jnp.where(i < N // 2, i, i - N // 2)
    wave = k.astype(F32) * (2.0 * math.pi / N)
    return wave, jnp.where(k == 0, 1.0, 2.0)


def fetch(refs, scratch, sem):
    copies = [pltpu.make_async_copy(r, v, sem.at[i]) for i, (r, v) in enumerate(zip(refs, scratch))]
    for copy in copies:
        copy.start()
    return copies


def pack_kernel(owner_ref, offset_ref, weight_ref, template_ref, image_ref, pick_ref, out_ref, owner, offset, weight, template, image, pick, sem):
    copies = fetch(
        (owner_ref, offset_ref, weight_ref, template_ref, image_ref, pick_ref),
        (owner, offset, weight, template, image, pick),
        sem,
    )
    me = lax.axis_index("pencil")
    for copy in copies[:3]:
        copy.wait()
    move = ((owner[...] - me + 130) & 127) - 2
    rel = (move * 4 + (offset[...] >> 6)).astype(F32)
    level = weight[...].astype(F32)
    row = iota((128, 256), 0)
    second = ((row >> 4) & 1) == 1
    rel = jnp.where(second, rel[1:2], rel[0:1])
    taps = cubic(jnp.where(second, level[1:2], level[0:1]))
    item = row & 15
    value = jnp.where(item == 0, rel, 0.0)
    for k in range(4):
        high = taps[k].astype(BF).astype(F32)
        value = jnp.where(item == 1 + k, high, value)
        value = jnp.where(item == 5 + k, taps[k] - high, value)
    near = jnp.where(row < 32, value, 0.0).astype(BF)
    far = jnp.where((row >= 32) & (row < 64), value, 0.0).astype(BF)
    col = iota((128, 256), 1)
    z = row >> 2
    other = (z + 2 * (z & 1) - 1) & 31
    at_near = (row & 3) * 64 + (z >> 1) * 4
    at_far = (row & 3) * 64 + (other >> 1) * 4
    for copy in copies[3:]:
        copy.wait()
    template = template[...].reshape(128, N)
    image = image[...].reshape(128, N)
    pick = pick[...]
    low = iota((32, 8, 128), 1) < 4
    for pair in range(2):
        units = []
        for q in (2 * pair, 2 * pair + 1):
            lanes = slice(128 * q, 128 * q + 128)
            hot_near = jnp.where(col == at_near + q, 1.0, 0.0).astype(BF)
            hot_far = jnp.where(col == at_far + q, 1.0, 0.0).astype(BF)
            codes = (dot(hot_near, near, NT) + dot(hot_far, far, NT)).astype(BF)
            stack = jnp.concatenate([template[:, lanes], image[:, lanes], codes], axis=0)
            rows = dot(pick, stack).reshape(32, 3, 8, 128)
            units += [rows[:, 0], rows[:, 1], rows[:, 2]]
        a, b, c, d, e, f = units
        d, e = pltpu.roll(d, 4, 1), pltpu.roll(e, 4, 1)
        tiles = [a, b, jnp.where(low, c, d), jnp.where(low, d, e), jnp.where(low, e, f)]
        out_ref[:, pair] = jnp.concatenate(tiles, axis=1).astype(BF)


def units_of(ref):
    t = [ref[:, 8 * i : 8 * i + 8, :].astype(F32) for i in range(5)]
    low = iota((64, 8, 128), 1) < 4
    units = [
        jnp.where(low, t[0], t[2]),
        pltpu.roll(jnp.where(low, t[3], t[0]), 4, 1),
        jnp.where(low, t[1], t[3]),
        pltpu.roll(jnp.where(low, t[4], t[1]), 4, 1),
        jnp.where(low, t[2], t[4]),
    ]
    return [u.reshape(N, 128) for u in units]


def units_to(ref, units):
    a, b, c, d, e = [u.reshape(64, 8, 128) for u in units]
    low = iota((64, 8, 128), 1) < 4
    turned_b, turned_d = pltpu.roll(b, 4, 1), pltpu.roll(d, 4, 1)
    tiles = [
        jnp.where(low, a, turned_b),
        jnp.where(low, c, turned_d),
        jnp.where(low, e, a),
        jnp.where(low, turned_b, c),
        jnp.where(low, turned_d, e),
    ]
    ref[...] = jnp.concatenate(tiles, axis=1).astype(BF)


def fill(high_ref, low_ref, codes, at):
    for i in range(4):
        part = codes[128 * i : 128 * i + 128]
        rel = part[:, at : at + 1]
        high = [part[:, at + 1 + k : at + 2 + k] for k in range(4)]
        low = [part[:, at + 5 + k : at + 6 + k] for k in range(4)]
        for tile, first, count in ((0, 0, 128), (-1, 0, 16), (1, 112, 16)):
            rows = slice(first, first + count)
            row = iota((count, 128), 0) + first
            lag = (iota((count, 128), 1) + 128 * tile - (row & -4)).astype(F32) - rel[rows]
            h = jnp.zeros((count, 128), F32)
            l = h
            for k in range(4):
                h = jnp.where(lag == k, high[k][rows], h)
                l = jnp.where(lag == k, low[k][rows], l)
            j = (i + tile) % 4
            where = (slice(128 * i + first, 128 * i + first + count), slice(128 * j, 128 * j + 128))
            high_ref[where] = h.astype(BF)
            low_ref[where] = l.astype(BF)


def transport_kernel(got_ref, deriv_ref, out0_ref, out1_ref, out2_ref, out3_ref, warped_ref, high_a, low_a, high_b, low_b, pieces):
    me = lax.axis_index("pencil")
    for ref in (high_a, low_a, high_b, low_b):
        ref[...] = jnp.zeros((N, N), BF)
    own, partner, other, image, codes = units_of(got_ref)
    near = jnp.concatenate([own, partner], axis=1).astype(BF)
    other = other.astype(BF)
    for section in range(2):
        fill(high_a, low_a, codes, 16 * section)
        fill(high_b, low_b, codes, 32 + 16 * section)
        near = (dot(high_a[...], near) + dot(low_a[...], near)).astype(BF)
        other = (dot(high_b[...], other) + dot(low_b[...], other)).astype(BF)
    warped = near[:, :128]
    residual = image - warped.astype(F32)
    image = image.astype(BF)
    sign = jnp.where((me & 4) == 0, 0.5, -0.5).astype(F32)
    slope_z = (near[:, 128:].astype(F32) - other.astype(F32)) * sign
    warped_ref[...] = warped
    pieces[0] = (residual * dot(deriv_ref[...], warped)).astype(BF)
    pieces[1, 0:256] = warped[0:256]
    pieces[1, 256:512] = image[0:256]
    pieces[2] = (residual * slope_z).astype(BF)
    pieces[3, 0:256] = warped[256:512]
    pieces[3, 256:512] = image[256:512]
    for s, ref in enumerate((out0_ref, out1_ref, out2_ref, out3_ref)):
        ref[...] = pieces[(me - s) & 3]


def smooth_kernel(p0_ref, p1_ref, p2_ref, p3_ref, warped_ref, deriv_ref, table_ref, flip_ref, out_ref, plane, tiles):
    role = lax.axis_index("pencil") & 3
    parts = jnp.concatenate([p[...] for p in (p0_ref, p1_ref, p2_ref, p3_ref)], axis=1)

    @pl.when((role & 1) == 0)
    def _():
        plane[...] = parts

    @pl.when((role & 1) == 1)
    def _():
        half = parts[0:256]
        slope_y = -dot(half, deriv_ref[...])
        force = ((parts[256:512].astype(F32) - half.astype(F32)) * slope_y).astype(BF)
        at = (role >> 1) * 256
        plane[pl.ds(pl.multiple_of(at, 256), 256)] = force
        plane[pl.ds(pl.multiple_of(256 - at, 256), 256)] = jnp.zeros((256, N), BF)

    spec = dot(plane[...], flip_ref[...]).astype(BF)
    wave_x, scale_x = mode_waves((N, 1), 0)
    wave_y, scale_y = mode_waves((1, N), 1)
    gain = (scale_x * scale_y * (FORCE_GAIN / (N * N))) / (1.0 + H1_WEIGHT * (wave_x * wave_x + wave_y * wave_y))
    bent = (dot(table_ref[...], spec) * gain).astype(BF)
    back = dot(flip_ref[...], bent).astype(BF)
    smooth = dot(back, table_ref[...])
    for s in range(4):
        tiles[(role + s) & 3] = smooth[:, 128 * s : 128 * s + 128]
    units_to(out_ref, [tiles[0], tiles[1], tiles[2], tiles[3], warped_ref[...].astype(F32)])


def finish_kernel(home_ref, pick_ref, velocity_ref, out_warped_ref, out_ref, velocity, result, warped, sem):
    loads = fetch([velocity_ref.at[c] for c in range(3)], [velocity.at[c] for c in range(3)], sem)
    pick = pick_ref[...]
    units = units_of(home_ref)
    rows = jnp.concatenate(units[:4], axis=1).astype(BF)
    turned = dot(pick, units[4].astype(BF))
    for r in range(4):
        warped[:, :, 128 * r : 128 * r + 128] = turned[128 * r : 128 * r + 128].reshape(4, 32, 128).astype(BF)
    stores = [pltpu.make_async_copy(warped, out_warped_ref, sem.at[3])]
    stores[0].start()
    for c in range(3):
        which = pick[128 * c : 128 * c + 128]
        if c == 1:
            which = which + pick[384:512]
        part = dot(which, rows).reshape(4, 32, N)
        loads[c].wait()
        result[c] = velocity[c] + part
        store = pltpu.make_async_copy(result.at[c], out_ref.at[c], sem.at[4 + c])
        store.start()
        stores.append(store)
    for store in stores:
        store.wait()


ANY = pl.BlockSpec(memory_space=pl.ANY)
VMEM = pl.BlockSpec(memory_space=pltpu.VMEM)


def call(kernel, outs, in_specs, out_specs, scratch):
    return pl.pallas_call(
        kernel,
        out_shape=outs,
        in_specs=in_specs,
        out_specs=out_specs,
        scratch_shapes=scratch,
        compiler_params=pltpu.CompilerParams(vmem_limit_bytes=48 << 20),
    )


def local(template, reference_image, velocity, dep_owner, dep_offset, dep_weight):
    shape = jax.ShapeDtypeStruct
    piece = shape((N, 128), BF)
    vm = pltpu.VMEM

    pick = bf(pack_rows())
    inputs = (dep_owner, dep_offset, dep_weight, template, reference_image, pick)
    pack = call(
        pack_kernel,
        shape((32, 2, 40, 128), BF),
        [ANY] * 6,
        VMEM,
        [vm(a.shape, a.dtype) for a in inputs] + [pltpu.SemaphoreType.DMA((6,))],
    )(*inputs)
    got = lax.all_to_all(pack.reshape(640, 4, 128), "pencil", 0, 0, tiled=True)

    deriv = bf(derivative_matrix())
    *parts, warped = call(
        transport_kernel,
        [piece] * 5,
        [VMEM] * 2,
        [VMEM] * 5,
        [vm((N, N), BF)] * 4 + [vm((4, N, 128), BF)],
    )(got.reshape(64, 40, 128), deriv)
    for s in (1, 2, 3):
        parts[s] = lax.ppermute(parts[s], "pencil", [((i // 4) * 4 + (i + s) % 4, i) for i in range(128)])

    table = basis(np.arange(N))
    send = call(
        smooth_kernel,
        shape((64, 40, 128), BF),
        [VMEM] * 8,
        VMEM,
        [vm((N, N), BF), vm((4, N, 128), F32)],
    )(*parts, warped, deriv, bf(table), bf(table.T))
    home = lax.all_to_all(send.reshape(640, 4, 128), "pencil", 0, 0, tiled=True)

    return call(
        finish_kernel,
        [shape((4, 32, N), BF), shape((3, 4, 32, N), F32)],
        [VMEM, VMEM, ANY],
        [ANY, ANY],
        [vm((3, 4, 32, N), F32), vm((3, 4, 32, N), F32), vm((4, 32, N), BF), pltpu.SemaphoreType.DMA((7,))],
    )(home.reshape(64, 40, 128), bf(unpack_rows()), velocity)


def solution(mesh):
    in_specs = (
        P("pencil", "start", None),
        P("pencil", "start", None),
        P("start", "pencil", None, None),
        P("start", "pencil"),
        P("start", "pencil"),
        P("start", "pencil"),
    )
    out_specs = (P("pencil", "start", None), P("start", "pencil", None, None))
    return jax.shard_map(local, mesh=mesh, in_specs=in_specs, out_specs=out_specs, check_vma=False)
```

time: 104 us -> 89.2 us (0.86)
  blocking collectives: 28.7 us -> 66.5 us
  waiting for transfers between devices: 40.6 us -> 6.17 us
  starting transfers between devices: 18.9 us -> 2.68 us
  local copies, waits for them, and re-layouts: 6.73 us -> 4.94 us
  Pallas kernels: 6.29 us -> 7.92 us
    all_to_all x1 -> x2, blocking collectives: 28.7 us -> 66.5 us  [the longest x1 38.1 us: local(): got = lax.all_to_all(pack.reshape(640, 4, 128), 'pencil', 0, 0, tiled=True)]
    all_to_all x1 -> x0, waiting for transfers between devices: 25.5 us -> none  [local(): lax.all_to_all(pack.reshape(128, ROWS, 128), 'pencil', 0, 0, tiled=True)]
    all_to_all x1 -> x0, starting transfers between devices: 15.6 us -> none  [local(): lax.all_to_all(pack.reshape(128, ROWS, 128), 'pencil', 0, 0, tiled=True)]
    ppermute x3, waiting for transfers between devices: 15.1 us -> 6.17 us  [local(): lax.ppermute(parts[s], 'pencil', [(i // 4 * 4 + (i + s) % 4, i) for i in...]
    pallas_call x3 -> x4, Pallas kernels: 6.29 us -> 7.92 us  [the longest x1 2.37 us: local(): call(transport_kernel, [piece] * 5, [VMEM] * 2, [VMEM] * 5, [vm((N, N), B...]
    unnamed x26 -> x22, local copies, waits for them, and re-layouts: 5.13 us -> 4.94 us
  transfers between devices with their start and end apart: 4 -> 3, of which waited for: 3 -> 3; matrix products, arithmetic and copies ran while one was open for 1% -> 0% of each run, Pallas kernels for 0% -> 0%
where the time goes in v3:
time: 89.2 us; the launch traced here: 88.9 us
  blocking collectives  66.5 us (75%)
  Pallas kernels  7.92 us (9%)
  waiting for transfers between devices  6.17 us (7%)
  local copies, waits for them, and re-layouts  4.94 us (6%)
  starting transfers between devices  2.68 us (3%)
    all_to_all x1, blocking collectives, local(): got = lax.all_to_all(pack.reshape(640, 4, 128), 'pencil', 0, 0, tiled=True)  38.1 us
    all_to_all x1, blocking collectives, local(): home = lax.all_to_all(send.reshape(640, 4, 128), 'pencil', 0, 0, tiled=True)  28.4 us
    ppermute x3, waiting for transfers between devices, local(): lax.ppermute(parts[s], 'pencil', [(i // 4 * 4 + (i + s) % 4, i) for i in...  6.17 us
    unnamed x22, local copies, waits for them, and re-layouts  4.94 us
    ppermute x3, starting transfers between devices, local(): lax.ppermute(parts[s], 'pencil', [(i // 4 * 4 + (i + s) % 4, i) for i in...  2.68 us
    pallas_call x1, Pallas kernels, local(): call(transport_kernel, [piece] * 5, [VMEM] * 2, [VMEM] * 5, [vm((N, N), B...  2.37 us
    pallas_call x1, Pallas kernels, local(): call(pack_kernel, shape((32, 2, 40, 128), BF), [ANY] * 6, VMEM, [vm(a.sha...  1.93 us
    pallas_call x1, Pallas kernels, local(): call(smooth_kernel, shape((64, 40, 128), BF), [VMEM] * 8, VMEM, [vm((N, N...  1.82 us
  transfers between devices with their start and end apart: 3, of which 3 were waited for; matrix products, arithmetic and copies ran while one was open for 0% of the time, Pallas kernels for 0%

profile of v3, /device:TPU:2, one launch (start us, length us, event | category | flops | bytes accessed | tf_op | source)
XLA Modules:
  0.0 88.9 jit_solution(15967650531049351777)
XLA Ops:
  0.6 0.0 copy-start.2
  0.6 1.1 %copy-done.2 = bf16[768,384]{1,0:T(8,128)(2,1)S(1)} copy-done((bf16[768,384]{1,0:T(8,128)(2,1)S(1)}, bf16[768,384]{1,0:T(8,128)(2,1)}, u32[]{:S(2)}) %copy-start.2) | copy-done | bytes 589848
  1.7 0.9 %copy-done.6 = bf16[4,32,512]{2,1,0:T(8,128)(2,1)S(1)} copy-done((bf16[4,32,512]{2,1,0:T(8,128)(2,1)S(1)}, bf16[4,32,512]{2,1,0:T(8,128)(2,1)}, u32[]{:S(2)}) %copy-start.6) | copy-done | bytes 131096
  2.6 0.9 %copy-done.7 = bf16[4,32,512]{2,1,0:T(8,128)(2,1)S(1)} copy-done((bf16[4,32,512]{2,1,0:T(8,128)(2,1)S(1)}, bf16[4,32,512]{2,1,0:T(8,128)(2,1)}, u32[]{:S(2)}) %copy-start.7) | copy-done | bytes 131096
  3.5 0.7 copy-done.8
  4.2 0.7 copy-done.9
  4.9 0.7 copy-done.10
  5.6 1.9 %shard_map.122 = bf16[32,2,40,128]{3,2,1,0:T(8,128)(2,1)S(1)} custom-call(s32[2,256]{1,0:T(2,128)S(1)} %copy-done.8, s32[2,256]{1,0:T(2,128)S(1)} %copy-done.9, s32[2,256]{1,0:T(2,128)S(1)} %copy-done.10, bf16[4,32,512]{2,1,0:T(8,128)(2,1)S(1)} %copy-done.6, bf16[4,32,512]{2,1,0:T(8,128)(2,1)S(1)} %copy-done.7, bf16[768,384]{1,0:T(8,128)(2,1)S(1)} %copy-done.2), custom_call_target="tpu_custom_call" | custom-call | tf_op jit(solution)/shard_map/pallas_call | solution.py:304
  7.5 0.0 copy-start
  7.5 38.1 %all_to_all.10 = bf16[640,4,128]{2,1,0:T(4,128)(2,1)S(1)} all-to-all(bf16[640,4,128]{2,1,0:T(4,128)(2,1)S(1)} %bitcast.5), channel_id=1, replica_groups=mesh['start'=2,'pencil'=128] {'pencil'}, dimensions={0} | all-to-all | bytes 1310720 | tf_op jit(solution)/shard_map/all_to_all | solution.py:311
  45.6 0.0 copy-done
  45.6 2.4 %shard_map.123 = (bf16[512,128]{1,0:T(8,128)(2,1)S(1)}, bf16[512,128]{1,0:T(8,128)(2,1)S(1)}, bf16[512,128]{1,0:T(8,128)(2,1)S(1)}, bf16[512,128]{1,0:T(8,128)(2,1)S(1)}, bf16[512,128]{1,0:T(8,128)(2,1)S(1)}) custom-call(bf16[64,40,128]{2,1,0:T(8,128)(2,1)S(1)} %bitcast.4, bf16[512,512]{1,0:T(8,128)(2,1)S(1)} %copy-done), custom_call_target="tpu_custom_call" | custom-call | tf_op jit(solution)/shard_map/pallas_call | solution.py:314
  48.0 0.1 collective-permute-start
  48.1 2.6 %collective-permute-start.1 = (bf16[512,128]{1,0:T(8,128)(2,1)S(1)}, bf16[512,128]{1,0:T(8,128)(2,1)S(1)}, u32[]{:S(2)}, u32[]{:S(2)}) collective-permute-start(bf16[512,128]{1,0:T(8,128)(2,1)S(1)} %get-tuple-element.9), channel_id=1, source_target_pairs={{2,0},{3,1},{0,2},{1,3},{6,4},{7,5},{4,6},{5,7},{10,8},{11,9},{8,1... | collective-permute-start | bytes 393224 | tf_op jit(solution)/shard_map/ppermute | solution.py:322
  50.7 0.0 collective-permute-start.2
  50.7 2.3 %collective-permute-done.p1_ref = bf16[512,128]{1,0:T(8,128)(2,1)S(1)} collective-permute-done((bf16[512,128]{1,0:T(8,128)(2,1)S(1)}, bf16[512,128]{1,0:T(8,128)(2,1)S(1)}, u32[]{:S(2)}, u32[]{:S(2)}) %collective-permute-start) | collective-permute-done | bytes 131104 | tf_op jit(solution)/shard_map/ppermute | solution.py:322
  53.0 1.8 %collective-permute-done.1.p2_ref = bf16[512,128]{1,0:T(8,128)(2,1)S(1)} collective-permute-done((bf16[512,128]{1,0:T(8,128)(2,1)S(1)}, bf16[512,128]{1,0:T(8,128)(2,1)S(1)}, u32[]{:S(2)}, u32[]{:S(2)}) %collective-permute-start.1) | collective-permute-done | bytes 131104 | tf_op jit(solution)/shard_map/ppermute | solution.py:322
  54.8 2.1 %collective-permute-done.2.p3_ref = bf16[512,128]{1,0:T(8,128)(2,1)S(1)} collective-permute-done((bf16[512,128]{1,0:T(8,128)(2,1)S(1)}, bf16[512,128]{1,0:T(8,128)(2,1)S(1)}, u32[]{:S(2)}, u32[]{:S(2)}) %collective-permute-start.2) | collective-permute-done | bytes 131104 | tf_op jit(solution)/shard_map/ppermute | solution.py:322
  56.9 0.0 copy-done.5
  56.9 1.8 %shard_map.124 = bf16[64,40,128]{2,1,0:T(8,128)(2,1)S(1)} custom-call(bf16[512,128]{1,0:T(8,128)(2,1)S(1)} %get-tuple-element.7.p0_ref, bf16[512,128]{1,0:T(8,128)(2,1)S(1)} %collective-permute-done.p1_ref, bf16[512,128]{1,0:T(8,128)(2,1)S(1)} %collective-permute-done.1.p2_ref, bf16[512,128]{1,0:T(8,128)(2,1)S(1)} %collective-permute-done.2.p3_ref, ...), custom_call_target="tpu_custom_call" | custom-call | tf_op jit(solution)/shard_map/pallas_call | solution.py:325
  58.7 0.0 copy-start.1
  58.7 0.0 copy-start.3
  58.7 28.4 %all_to_all.11 = bf16[640,4,128]{2,1,0:T(4,128)(2,1)S(1)} all-to-all(bf16[640,4,128]{2,1,0:T(4,128)(2,1)S(1)} %bitcast.6), channel_id=1, replica_groups=mesh['start'=2,'pencil'=128] {'pencil'}, dimensions={0} | all-to-all | bytes 1310720 | tf_op jit(solution)/shard_map/all_to_all | solution.py:332
  87.1 1.8 %shard_map.125 = (bf16[4,32,512]{2,1,0:T(8,128)(2,1)}, f32[3,4,32,512]{3,2,1,0:T(8,128)}) custom-call(bf16[64,40,128]{2,1,0:T(8,128)(2,1)S(1)} %bitcast.7, bf16[512,512]{1,0:T(8,128)(2,1)S(1)} %copy-done.3, f32[3,4,32,512]{3,2,1,0:T(8,128)S(1)} %copy-done.1), custom_call_target="tpu_custom_call" | custom-call | tf_op jit(solution)/shard_map/pallas_call | solution.py:334
  (10 shorter events, 0.0 us)
Async XLA Ops:
  0.6 1.1 %copy-start.2 = (bf16[768,384]{1,0:T(8,128)(2,1)S(1)}, bf16[768,384]{1,0:T(8,128)(2,1)}, u32[]{:S(2)}) copy-start(bf16[768,384]{1,0:T(8,128)(2,1)} %constant.10.clone.pick_ref) | copy-start | bytes 1769476
  1.7 0.9 %copy-start.6 = (bf16[4,32,512]{2,1,0:T(8,128)(2,1)S(1)}, bf16[4,32,512]{2,1,0:T(8,128)(2,1)}, u32[]{:S(2)}) copy-start(bf16[4,32,512]{2,1,0:T(8,128)(2,1)} %template_ref.1) | copy-start | bytes 393220
  2.6 0.9 %copy-start.7 = (bf16[4,32,512]{2,1,0:T(8,128)(2,1)S(1)}, bf16[4,32,512]{2,1,0:T(8,128)(2,1)}, u32[]{:S(2)}) copy-start(bf16[4,32,512]{2,1,0:T(8,128)(2,1)} %image_ref.1) | copy-start | bytes 393220
  3.5 0.7 copy-start.8
  4.2 0.7 copy-start.9
  4.9 0.7 copy-start.10
  7.5 38.1 %copy-start = (bf16[512,512]{1,0:T(8,128)(2,1)S(1)}, bf16[512,512]{1,0:T(8,128)(2,1)}, u32[]{:S(2)}) copy-start(bf16[512,512]{1,0:T(8,128)(2,1)} %constant.11.clone.deriv_ref) | copy-start | bytes 1572868
  45.6 11.2 %copy-start.4 = (bf16[512,512]{1,0:T(8,128)(2,1)S(1)}, bf16[512,512]{1,0:T(8,128)(2,1)}, u32[]{:S(2)}) copy-start(bf16[512,512]{1,0:T(8,128)(2,1)} %constant.13.clone.flip_ref) | copy-start | bytes 1572868
  45.6 11.2 %copy-start.5 = (bf16[512,512]{1,0:T(8,128)(2,1)S(1)}, bf16[512,512]{1,0:T(8,128)(2,1)}, u32[]{:S(2)}) copy-start(bf16[512,512]{1,0:T(8,128)(2,1)} %constant.12.clone.table_ref) | copy-start | bytes 1572868
  48.0 5.0 %collective-permute-start = (bf16[512,128]{1,0:T(8,128)(2,1)S(1)}, bf16[512,128]{1,0:T(8,128)(2,1)S(1)}, u32[]{:S(2)}, u32[]{:S(2)}) collective-permute-start(bf16[512,128]{1,0:T(8,128)(2,1)S(1)} %get-tuple-element.8), channel_id=1, source_target_pairs={{1,0},{2,1},{3,2},{0,3},{5,4},{6,5},{7,6},{4,7},{9,8},{10,9},{11,1... | collective-permute-start | bytes 393224 | tf_op jit(solution)/shard_map/ppermute | solution.py:322
  48.1 6.7 %collective-permute-start.1 = (bf16[512,128]{1,0:T(8,128)(2,1)S(1)}, bf16[512,128]{1,0:T(8,128)(2,1)S(1)}, u32[]{:S(2)}, u32[]{:S(2)}) collective-permute-start(bf16[512,128]{1,0:T(8,128)(2,1)S(1)} %get-tuple-element.9), channel_id=1, source_target_pairs={{2,0},{3,1},{0,2},{1,3},{6,4},{7,5},{4,6},{5,7},{10,8},{11,9},{8,1... | collective-permute-start | bytes 393224 | tf_op jit(solution)/shard_map/ppermute | solution.py:322
  50.7 6.2 %collective-permute-start.2 = (bf16[512,128]{1,0:T(8,128)(2,1)S(1)}, bf16[512,128]{1,0:T(8,128)(2,1)S(1)}, u32[]{:S(2)}, u32[]{:S(2)}) collective-permute-start(bf16[512,128]{1,0:T(8,128)(2,1)S(1)} %get-tuple-element.10), channel_id=1, source_target_pairs={{3,0},{0,1},{1,2},{2,3},{7,4},{4,5},{5,6},{6,7},{11,8},{8,9},{9,10... | collective-permute-start | bytes 393224 | tf_op jit(solution)/shard_map/ppermute | solution.py:322
  58.7 28.4 %copy-start.1 = (f32[3,4,32,512]{3,2,1,0:T(8,128)S(1)}, f32[3,4,32,512]{3,2,1,0:T(8,128)}, u32[]{:S(2)}) copy-start(f32[3,4,32,512]{3,2,1,0:T(8,128)} %velocity_ref.1) | copy-start | bytes 2359300
  58.7 28.4 %copy-start.3 = (bf16[512,512]{1,0:T(8,128)(2,1)S(1)}, bf16[512,512]{1,0:T(8,128)(2,1)}, u32[]{:S(2)}) copy-start(bf16[512,512]{1,0:T(8,128)(2,1)} %constant.14.clone.pick_ref) | copy-start | bytes 1572868

commit v4 on v3

--- a/solution.py
+++ b/solution.py
@@ -58,9 +58,18 @@
 
 def unpack_rows():
     r = np.arange(N)
+    role, x, z = r // 128, (r // 32) % 4, r % 32
+    device = (z // 2) * 8 + (role // 2) * 4 + (z % 2) * 2 + role % 2
     pick = np.zeros((N, N), np.float32)
-    pick[r, (r % 32) * 16 + (r // 128) * 4 + (r // 32) % 4] = 1
+    pick[r, device * 4 + x] = 1
     return pick
+
+
+PARTNER = (0, 1, 4, 5)
+
+
+def quarter_of(device):
+    return ((device >> 1) & 2) + (device & 1)
 
 
 def bf(x):
@@ -147,7 +156,7 @@
         a, b, c, d, e, f = units
         d, e = pltpu.roll(d, 4, 1), pltpu.roll(e, 4, 1)
         tiles = [a, b, jnp.where(low, c, d), jnp.where(low, d, e), jnp.where(low, e, f)]
-        out_ref[:, pair] = jnp.concatenate(tiles, axis=1).astype(BF)
+        out_ref[:, pair] = jnp.concatenate(tiles, axis=1).astype(BF).reshape(16, 2, 40, 128)
 
 
 def units_of(ref):
@@ -213,7 +222,7 @@
     warped = near[:, :128]
     residual = image - warped.astype(F32)
     image = image.astype(BF)
-    sign = jnp.where((me & 4) == 0, 0.5, -0.5).astype(F32)
+    sign = jnp.where((me & 2) == 0, 0.5, -0.5).astype(F32)
     slope_z = (near[:, 128:].astype(F32) - other.astype(F32)) * sign
     warped_ref[...] = warped
     pieces[0] = (residual * dot(deriv_ref[...], warped)).astype(BF)
@@ -223,22 +232,19 @@
     pieces[3, 0:256] = warped[256:512]
     pieces[3, 256:512] = image[256:512]
     for s, ref in enumerate((out0_ref, out1_ref, out2_ref, out3_ref)):
-        ref[...] = pieces[(me - s) & 3]
-
-
-def smooth_kernel(p0_ref, p1_ref, p2_ref, p3_ref, warped_ref, deriv_ref, table_ref, flip_ref, out_ref, plane, tiles):
-    role = lax.axis_index("pencil") & 3
-    parts = jnp.concatenate([p[...] for p in (p0_ref, p1_ref, p2_ref, p3_ref)], axis=1)
-
-    @pl.when((role & 1) == 0)
-    def _():
-        plane[...] = parts
+        ref[...] = pieces[quarter_of(me) ^ s]
+
+
+def smooth_kernel(p0_ref, p1_ref, p2_ref, p3_ref, warped_ref, deriv_ref, table_ref, flip_ref, out_ref, plane):
+    role = quarter_of(lax.axis_index("pencil"))
+    for s, ref in enumerate((p0_ref, p1_ref, p2_ref, p3_ref)):
+        plane[:, pl.ds(pl.multiple_of((role ^ s) * 128, 128), 128)] = ref[...]
 
     @pl.when((role & 1) == 1)
     def _():
-        half = parts[0:256]
+        half = plane[0:256]
         slope_y = -dot(half, deriv_ref[...])
-        force = ((parts[256:512].astype(F32) - half.astype(F32)) * slope_y).astype(BF)
+        force = ((plane[256:512].astype(F32) - half.astype(F32)) * slope_y).astype(BF)
         at = (role >> 1) * 256
         plane[pl.ds(pl.multiple_of(at, 256), 256)] = force
         plane[pl.ds(pl.multiple_of(256 - at, 256), 256)] = jnp.zeros((256, N), BF)
@@ -250,9 +256,8 @@
     bent = (dot(table_ref[...], spec) * gain).astype(BF)
     back = dot(flip_ref[...], bent).astype(BF)
     smooth = dot(back, table_ref[...])
-    for s in range(4):
-        tiles[(role + s) & 3] = smooth[:, 128 * s : 128 * s + 128]
-    units_to(out_ref, [tiles[0], tiles[1], tiles[2], tiles[3], warped_ref[...].astype(F32)])
+    units = [smooth[:, 128 * s : 128 * s + 128] for s in range(4)]
+    units_to(out_ref, units + [warped_ref[...].astype(F32)])
 
 
 def finish_kernel(home_ref, pick_ref, velocity_ref, out_warped_ref, out_ref, velocity, result, warped, sem):
@@ -279,18 +284,18 @@
         store.wait()
 
 
-ANY = pl.BlockSpec(memory_space=pl.ANY)
+ANY = pl.BlockSpec(memory_space=pltpu.HBM)
 VMEM = pl.BlockSpec(memory_space=pltpu.VMEM)
 
 
-def call(kernel, outs, in_specs, out_specs, scratch):
+def call(kernel, outs, in_specs, out_specs, scratch, grant=48 << 20):
     return pl.pallas_call(
         kernel,
         out_shape=outs,
         in_specs=in_specs,
         out_specs=out_specs,
         scratch_shapes=scratch,
-        compiler_params=pltpu.CompilerParams(vmem_limit_bytes=48 << 20),
+        compiler_params=pltpu.CompilerParams(vmem_limit_bytes=grant),
     )
 
 
@@ -303,10 +308,11 @@
     inputs = (dep_owner, dep_offset, dep_weight, template, reference_image, pick)
     pack = call(
         pack_kernel,
-        shape((32, 2, 40, 128), BF),
+        shape((16, 2, 2, 40, 128), BF),
         [ANY] * 6,
         VMEM,
         [vm(a.shape, a.dtype) for a in inputs] + [pltpu.SemaphoreType.DMA((6,))],
+        65000000,
     )(*inputs)
     got = lax.all_to_all(pack.reshape(640, 4, 128), "pencil", 0, 0, tiled=True)
 
@@ -319,7 +325,7 @@
         [vm((N, N), BF)] * 4 + [vm((4, N, 128), BF)],
     )(got.reshape(64, 40, 128), deriv)
     for s in (1, 2, 3):
-        parts[s] = lax.ppermute(parts[s], "pencil", [((i // 4) * 4 + (i + s) % 4, i) for i in range(128)])
+        parts[s] = lax.ppermute(parts[s], "pencil", [(i ^ PARTNER[s], i) for i in range(128)])
 
     table = basis(np.arange(N))
     send = call(
@@ -327,7 +333,7 @@
         shape((64, 40, 128), BF),
         [VMEM] * 8,
         VMEM,
-        [vm((N, N), BF), vm((4, N, 128), F32)],
+        [vm((N, N), BF)],
     )(*parts, warped, deriv, bf(table), bf(table.T))
     home = lax.all_to_all(send.reshape(640, 4, 128), "pencil", 0, 0, tiled=True)
 

time: 89.2 us -> 85.3 us (0.956)
  local copies, waits for them, and re-layouts: 4.94 us -> 0.03 us
  waiting for transfers between devices: 6.17 us -> 4.43 us
  Pallas kernels: 7.92 us -> 9.02 us
  blocking collectives: 66.5 us -> 67.4 us
  starting transfers between devices: 2.68 us -> 3.58 us
    unnamed x22 -> x10, local copies, waits for them, and re-layouts: 4.94 us -> 0.03 us
    ppermute x3, waiting for transfers between devices: 6.17 us -> 4.43 us  [local(): lax.ppermute(parts[s], 'pencil', [(i ^ PARTNER[s], i) for i in range(128)])]
    pallas_call x1, Pallas kernels: 1.93 us -> 3.41 us  [local(): call(pack_kernel, shape((16, 2, 2, 40, 128), BF), [ANY] * 6, VMEM, [vm(a....]
  transfers between devices with their start and end apart: 3 -> 3, of which waited for: 3 -> 2; matrix products, arithmetic and copies ran while one was open for 0% -> 0% of each run, Pallas kernels for 0% -> 0%
where the time goes in v4:
time: 85.3 us; the launch traced here: 85.1 us
  blocking collectives  67.4 us (79%)
  Pallas kernels  9.02 us (11%)
  waiting for transfers between devices  4.43 us (5%)
  starting transfers between devices  3.58 us (4%)
    all_to_all x1, blocking collectives, local(): got = lax.all_to_all(pack.reshape(640, 4, 128), 'pencil', 0, 0, tiled=True)  38.3 us
    all_to_all x1, blocking collectives, local(): home = lax.all_to_all(send.reshape(640, 4, 128), 'pencil', 0, 0, tiled=True)  29 us
    ppermute x3, waiting for transfers between devices, local(): lax.ppermute(parts[s], 'pencil', [(i ^ PARTNER[s], i) for i in range(128)])  4.43 us
    ppermute x3, starting transfers between devices, local(): lax.ppermute(parts[s], 'pencil', [(i ^ PARTNER[s], i) for i in range(128)])  3.58 us
    pallas_call x1, Pallas kernels, local(): call(pack_kernel, shape((16, 2, 2, 40, 128), BF), [ANY] * 6, VMEM, [vm(a....  3.41 us
    pallas_call x1, Pallas kernels, local(): call(transport_kernel, [piece] * 5, [VMEM] * 2, [VMEM] * 5, [vm((N, N), B...  2.3 us
    pallas_call x1, Pallas kernels, local(): call(finish_kernel, [shape((4, 32, N), BF), shape((3, 4, 32, N), F32)], [...  1.8 us
  transfers between devices with their start and end apart: 3, of which 2 were waited for; matrix products, arithmetic and copies ran while one was open for 0% of the time, Pallas kernels for 0%

profile of v4, /device:TPU:2, one launch (start us, length us, event | category | flops | bytes accessed | tf_op | source)
XLA Modules:
  0.0 85.1 jit_solution(12176594637927983889)
XLA Ops:
  0.6 3.4 %shard_map.122 = bf16[16,2,2,40,128]{4,3,2,1,0:T(8,128)(2,1)} custom-call(s32[2,256]{1,0:T(2,128)} %owner_ref.1, s32[2,256]{1,0:T(2,128)} %offset_ref.1, s32[2,256]{1,0:T(2,128)} %weight_ref.1, bf16[4,32,512]{2,1,0:T(8,128)(2,1)} %template_ref.1, bf16[4,32,512]{2,1,0:T(8,128)(2,1)} %image_ref.1, bf16[768,384]{1,0:T(8,128)(2,1)} %constant.10.clone.pick_ref), custom_call_target="tpu_custom_call" | custom-call | tf_op jit(solution)/shard_map/pallas_call | solution.py:309
  4.1 0.0 copy-start
  4.1 38.3 %all_to_all.10 = bf16[640,4,128]{2,1,0:T(4,128)(2,1)S(1)} all-to-all(bf16[640,4,128]{2,1,0:T(4,128)(2,1)} %bitcast.7), channel_id=1, replica_groups=mesh['start'=2,'pencil'=128] {'pencil'}, dimensions={0} | all-to-all | bytes 1310720 | tf_op jit(solution)/shard_map/all_to_all | solution.py:317
  42.4 0.0 copy-done
  42.4 0.0 copy-start.3
  42.4 0.0 copy-start.4
  42.4 2.3 %shard_map.123 = (bf16[512,128]{1,0:T(8,128)(2,1)S(1)}, bf16[512,128]{1,0:T(8,128)(2,1)S(1)}, bf16[512,128]{1,0:T(8,128)(2,1)S(1)}, bf16[512,128]{1,0:T(8,128)(2,1)S(1)}, bf16[512,128]{1,0:T(8,128)(2,1)S(1)}) custom-call(bf16[64,40,128]{2,1,0:T(8,128)(2,1)S(1)} %bitcast.4, bf16[512,512]{1,0:T(8,128)(2,1)S(1)} %copy-done), custom_call_target="tpu_custom_call" | custom-call | tf_op jit(solution)/shard_map/pallas_call | solution.py:320
  44.7 0.6 collective-permute-start
  45.4 1.5 %collective-permute-start.1 = (bf16[512,128]{1,0:T(8,128)(2,1)S(1)}, bf16[512,128]{1,0:T(8,128)(2,1)S(1)}, u32[]{:S(2)}, u32[]{:S(2)}) collective-permute-start(bf16[512,128]{1,0:T(8,128)(2,1)S(1)} %get-tuple-element.9), channel_id=1, source_target_pairs={{4,0},{5,1},{6,2},{7,3},{0,4},{1,5},{2,6},{3,7},{12,8},{13,9},{14,... | collective-permute-start | bytes 393224 | tf_op jit(solution)/shard_map/ppermute | solution.py:328
  46.8 1.4 %collective-permute-start.2 = (bf16[512,128]{1,0:T(8,128)(2,1)S(1)}, bf16[512,128]{1,0:T(8,128)(2,1)S(1)}, u32[]{:S(2)}, u32[]{:S(2)}) collective-permute-start(bf16[512,128]{1,0:T(8,128)(2,1)S(1)} %get-tuple-element.10), channel_id=1, source_target_pairs={{5,0},{4,1},{7,2},{6,3},{1,4},{0,5},{3,6},{2,7},{13,8},{12,9},{15,... | collective-permute-start | bytes 393224 | tf_op jit(solution)/shard_map/ppermute | solution.py:328
  48.3 2.3 %collective-permute-done.p1_ref = bf16[512,128]{1,0:T(8,128)(2,1)S(1)} collective-permute-done((bf16[512,128]{1,0:T(8,128)(2,1)S(1)}, bf16[512,128]{1,0:T(8,128)(2,1)S(1)}, u32[]{:S(2)}, u32[]{:S(2)}) %collective-permute-start) | collective-permute-done | bytes 131104 | tf_op jit(solution)/shard_map/ppermute | solution.py:328
  50.5 0.0 collective-permute-done.1.p2_ref
  50.5 2.2 %collective-permute-done.2.p3_ref = bf16[512,128]{1,0:T(8,128)(2,1)S(1)} collective-permute-done((bf16[512,128]{1,0:T(8,128)(2,1)S(1)}, bf16[512,128]{1,0:T(8,128)(2,1)S(1)}, u32[]{:S(2)}, u32[]{:S(2)}) %collective-permute-start.2) | collective-permute-done | bytes 131104 | tf_op jit(solution)/shard_map/ppermute | solution.py:328
  52.7 0.0 copy-done.3
  52.7 0.0 copy-done.4
  52.7 1.5 %shard_map.124 = bf16[64,40,128]{2,1,0:T(8,128)(2,1)S(1)} custom-call(bf16[512,128]{1,0:T(8,128)(2,1)S(1)} %get-tuple-element.7.p0_ref, bf16[512,128]{1,0:T(8,128)(2,1)S(1)} %collective-permute-done.p1_ref, bf16[512,128]{1,0:T(8,128)(2,1)S(1)} %collective-permute-done.1.p2_ref, bf16[512,128]{1,0:T(8,128)(2,1)S(1)} %collective-permute-done.2.p3_ref, ...), custom_call_target="tpu_custom_call" | custom-call | tf_op jit(solution)/shard_map/pallas_call | solution.py:331
  54.2 0.0 copy-start.1
  54.2 0.0 copy-start.2
  54.3 29.0 %all_to_all.11 = bf16[640,4,128]{2,1,0:T(4,128)(2,1)S(1)} all-to-all(bf16[640,4,128]{2,1,0:T(4,128)(2,1)S(1)} %bitcast.5), channel_id=1, replica_groups=mesh['start'=2,'pencil'=128] {'pencil'}, dimensions={0} | all-to-all | bytes 1310720 | tf_op jit(solution)/shard_map/all_to_all | solution.py:338
  83.3 0.0 copy-done.1
  83.3 0.0 copy-done.2
  83.3 1.8 %shard_map.125 = (bf16[4,32,512]{2,1,0:T(8,128)(2,1)}, f32[3,4,32,512]{3,2,1,0:T(8,128)}) custom-call(bf16[64,40,128]{2,1,0:T(8,128)(2,1)S(1)} %bitcast.6, bf16[512,512]{1,0:T(8,128)(2,1)S(1)} %copy-done.2, f32[3,4,32,512]{3,2,1,0:T(8,128)S(1)} %copy-done.1), custom_call_target="tpu_custom_call" | custom-call | tf_op jit(solution)/shard_map/pallas_call | solution.py:340
Async XLA Ops:
  4.1 38.3 %copy-start = (bf16[512,512]{1,0:T(8,128)(2,1)S(1)}, bf16[512,512]{1,0:T(8,128)(2,1)}, u32[]{:S(2)}) copy-start(bf16[512,512]{1,0:T(8,128)(2,1)} %constant.11.clone.deriv_ref) | copy-start | bytes 1572868
  42.4 10.3 %copy-start.3 = (bf16[512,512]{1,0:T(8,128)(2,1)S(1)}, bf16[512,512]{1,0:T(8,128)(2,1)}, u32[]{:S(2)}) copy-start(bf16[512,512]{1,0:T(8,128)(2,1)} %constant.13.clone.flip_ref) | copy-start | bytes 1572868
  42.4 10.3 %copy-start.4 = (bf16[512,512]{1,0:T(8,128)(2,1)S(1)}, bf16[512,512]{1,0:T(8,128)(2,1)}, u32[]{:S(2)}) copy-start(bf16[512,512]{1,0:T(8,128)(2,1)} %constant.12.clone.table_ref) | copy-start | bytes 1572868
  44.7 5.8 %collective-permute-start = (bf16[512,128]{1,0:T(8,128)(2,1)S(1)}, bf16[512,128]{1,0:T(8,128)(2,1)S(1)}, u32[]{:S(2)}, u32[]{:S(2)}) collective-permute-start(bf16[512,128]{1,0:T(8,128)(2,1)S(1)} %get-tuple-element.8), channel_id=1, source_target_pairs={{1,0},{0,1},{3,2},{2,3},{5,4},{4,5},{7,6},{6,7},{9,8},{8,9},{11,10... | collective-permute-start | bytes 393224 | tf_op jit(solution)/shard_map/ppermute | solution.py:328
  45.4 5.2 %collective-permute-start.1 = (bf16[512,128]{1,0:T(8,128)(2,1)S(1)}, bf16[512,128]{1,0:T(8,128)(2,1)S(1)}, u32[]{:S(2)}, u32[]{:S(2)}) collective-permute-start(bf16[512,128]{1,0:T(8,128)(2,1)S(1)} %get-tuple-element.9), channel_id=1, source_target_pairs={{4,0},{5,1},{6,2},{7,3},{0,4},{1,5},{2,6},{3,7},{12,8},{13,9},{14,... | collective-permute-start | bytes 393224 | tf_op jit(solution)/shard_map/ppermute | solution.py:328
  46.8 5.9 %collective-permute-start.2 = (bf16[512,128]{1,0:T(8,128)(2,1)S(1)}, bf16[512,128]{1,0:T(8,128)(2,1)S(1)}, u32[]{:S(2)}, u32[]{:S(2)}) collective-permute-start(bf16[512,128]{1,0:T(8,128)(2,1)S(1)} %get-tuple-element.10), channel_id=1, source_target_pairs={{5,0},{4,1},{7,2},{6,3},{1,4},{0,5},{3,6},{2,7},{13,8},{12,9},{15,... | collective-permute-start | bytes 393224 | tf_op jit(solution)/shard_map/ppermute | solution.py:328
  54.2 29.1 %copy-start.1 = (f32[3,4,32,512]{3,2,1,0:T(8,128)S(1)}, f32[3,4,32,512]{3,2,1,0:T(8,128)}, u32[]{:S(2)}) copy-start(f32[3,4,32,512]{3,2,1,0:T(8,128)} %velocity_ref.1) | copy-start | bytes 2359300
  54.2 29.1 %copy-start.2 = (bf16[512,512]{1,0:T(8,128)(2,1)S(1)}, bf16[512,512]{1,0:T(8,128)(2,1)}, u32[]{:S(2)}) copy-start(bf16[512,512]{1,0:T(8,128)(2,1)} %constant.14.clone.pick_ref) | copy-start | bytes 1572868

commit v5 on v4

--- a/solution.py
+++ b/solution.py
@@ -61,9 +61,13 @@
     role, x, z = r // 128, (r // 32) % 4, r % 32
     device = (z // 2) * 8 + (role // 2) * 4 + (z % 2) * 2 + role % 2
     pick = np.zeros((N, N), np.float32)
-    pick[r, device * 4 + x] = 1
+    pick[r, (np.array(PLACE)[device // 2] * 2 + device % 2) * 4 + x] = 1
     return pick
 
+
+PAIRS = [int(i) for i in np.random.RandomState(3).permutation(64)]
+PLACE = [PAIRS.index(i) for i in range(64)]
+ORDER = [2 * i + j for i in PAIRS for j in (0, 1)]
 
 PARTNER = (0, 1, 4, 5)
 
@@ -120,47 +124,54 @@
     move = ((owner[...] - me + 130) & 127) - 2
     rel = (move * 4 + (offset[...] >> 6)).astype(F32)
     level = weight[...].astype(F32)
-    row = iota((128, 256), 0)
-    second = ((row >> 4) & 1) == 1
-    rel = jnp.where(second, rel[1:2], rel[0:1])
-    taps = cubic(jnp.where(second, level[1:2], level[0:1]))
-    item = row & 15
-    value = jnp.where(item == 0, rel, 0.0)
-    for k in range(4):
-        high = taps[k].astype(BF).astype(F32)
-        value = jnp.where(item == 1 + k, high, value)
-        value = jnp.where(item == 5 + k, taps[k] - high, value)
-    near = jnp.where(row < 32, value, 0.0).astype(BF)
-    far = jnp.where((row >= 32) & (row < 64), value, 0.0).astype(BF)
-    col = iota((128, 256), 1)
-    z = row >> 2
+    taps = cubic(level)
+    items = [rel]
+    for tap in taps:
+        items.append(tap.astype(BF).astype(F32))
+    for tap, high in zip(taps, items[1:5]):
+        items.append(tap - high)
+    row = iota((32, 256), 0)
+    value = jnp.zeros((32, 256), F32)
+    for section in range(2):
+        for i, item in enumerate(items):
+            value = jnp.where(row == 16 * section + i, item[section : section + 1], value)
+    blank = jnp.zeros((32, 256), F32)
+    codes = jnp.concatenate(
+        [
+            jnp.concatenate([value, blank, blank, blank], axis=0),
+            jnp.concatenate([blank, value, blank, blank], axis=0),
+        ],
+        axis=1,
+    ).astype(BF)
+    row, col = iota((N, 256), 0), iota((N, 256), 1)
+    q, z, x = row >> 7, (row >> 2) & 31, row & 3
     other = (z + 2 * (z & 1) - 1) & 31
-    at_near = (row & 3) * 64 + (z >> 1) * 4
-    at_far = (row & 3) * 64 + (other >> 1) * 4
+    near = jnp.where(col == x * 64 + (z >> 1) * 4 + q, 1.0, 0.0)
+    far = jnp.where(col == x * 64 + (other >> 1) * 4 + q, 1.0, 0.0)
+    codes = dot(jnp.concatenate([near, far], axis=1).astype(BF), codes, NT).astype(BF)
+    codes = jnp.concatenate([codes[128 * i : 128 * i + 128] for i in range(4)], axis=1)
     for copy in copies[3:]:
         copy.wait()
-    template = template[...].reshape(128, N)
-    image = image[...].reshape(128, N)
-    pick = pick[...]
+    stack = jnp.concatenate([template[...].reshape(128, N), image[...].reshape(128, N), codes], axis=0)
+    rows = dot(pick[...], stack)
     low = iota((32, 8, 128), 1) < 4
     for pair in range(2):
         units = []
         for q in (2 * pair, 2 * pair + 1):
-            lanes = slice(128 * q, 128 * q + 128)
-            hot_near = jnp.where(col == at_near + q, 1.0, 0.0).astype(BF)
-            hot_far = jnp.where(col == at_far + q, 1.0, 0.0).astype(BF)
-            codes = (dot(hot_near, near, NT) + dot(hot_far, far, NT)).astype(BF)
-            stack = jnp.concatenate([template[:, lanes], image[:, lanes], codes], axis=0)
-            rows = dot(pick, stack).reshape(32, 3, 8, 128)
-            units += [rows[:, 0], rows[:, 1], rows[:, 2]]
+            part = rows[:, 128 * q : 128 * q + 128].reshape(32, 3, 8, 128)
+            units += [part[:, 0], part[:, 1], part[:, 2]]
         a, b, c, d, e, f = units
         d, e = pltpu.roll(d, 4, 1), pltpu.roll(e, 4, 1)
         tiles = [a, b, jnp.where(low, c, d), jnp.where(low, d, e), jnp.where(low, e, f)]
-        out_ref[:, pair] = jnp.concatenate(tiles, axis=1).astype(BF).reshape(16, 2, 40, 128)
-
-
-def units_of(ref):
+        tiles = jnp.concatenate(tiles, axis=1).astype(BF)
+        for z in range(32):
+            out_ref[PLACE[(z // 2) * 4 + pair * 2 + z % 2]] = tiles[z]
+
+
+def units_of(ref, places=None):
     t = [ref[:, 8 * i : 8 * i + 8, :].astype(F32) for i in range(5)]
+    if places is not None:
+        t = [jnp.concatenate([v[i : i + 1] for i in places], axis=0) for v in t]
     low = iota((64, 8, 128), 1) < 4
     units = [
         jnp.where(low, t[0], t[2]),
@@ -183,42 +194,44 @@
         jnp.where(low, turned_b, c),
         jnp.where(low, turned_d, e),
     ]
-    ref[...] = jnp.concatenate(tiles, axis=1).astype(BF)
-
-
-def fill(high_ref, low_ref, codes, at):
+    tiles = jnp.concatenate(tiles, axis=1).astype(BF)
+    for i in range(64):
+        ref[PLACE[i]] = tiles[i]
+
+
+def transport(codes, at, f):
+    taps = []
     for i in range(4):
         part = codes[128 * i : 128 * i + 128]
         rel = part[:, at : at + 1]
-        high = [part[:, at + 1 + k : at + 2 + k] for k in range(4)]
-        low = [part[:, at + 5 + k : at + 6 + k] for k in range(4)]
+        pieces = [[part[:, at + j + k : at + j + 1 + k] for k in range(4)] for j in (1, 5)]
+        moved = []
         for tile, first, count in ((0, 0, 128), (-1, 0, 16), (1, 112, 16)):
             rows = slice(first, first + count)
             row = iota((count, 128), 0) + first
             lag = (iota((count, 128), 1) + 128 * tile - (row & -4)).astype(F32) - rel[rows]
-            h = jnp.zeros((count, 128), F32)
-            l = h
-            for k in range(4):
-                h = jnp.where(lag == k, high[k][rows], h)
-                l = jnp.where(lag == k, low[k][rows], l)
+            band = []
+            for piece in pieces:
+                weight = jnp.zeros((count, 128), F32)
+                for k in range(4):
+                    weight = jnp.where(lag == k, piece[k][rows], weight)
+                band.append(weight.astype(BF))
             j = (i + tile) % 4
-            where = (slice(128 * i + first, 128 * i + first + count), slice(128 * j, 128 * j + 128))
-            high_ref[where] = h.astype(BF)
-            low_ref[where] = l.astype(BF)
-
-
-def transport_kernel(got_ref, deriv_ref, out0_ref, out1_ref, out2_ref, out3_ref, warped_ref, high_a, low_a, high_b, low_b, pieces):
+            source = f[128 * j : 128 * j + 128]
+            moved.append(dot(jnp.concatenate(band, axis=1), jnp.concatenate([source, source], axis=0)))
+        mid, down, up = moved
+        taps += [mid[:16] + down, mid[16:112], mid[112:] + up]
+    return jnp.concatenate(taps, axis=0).astype(BF)
+
+
+def transport_kernel(got_ref, deriv_ref, out0_ref, out1_ref, out2_ref, out3_ref, warped_ref, pieces):
     me = lax.axis_index("pencil")
-    for ref in (high_a, low_a, high_b, low_b):
-        ref[...] = jnp.zeros((N, N), BF)
-    own, partner, other, image, codes = units_of(got_ref)
+    own, partner, other, image, codes = units_of(got_ref, PLACE)
     near = jnp.concatenate([own, partner], axis=1).astype(BF)
     other = other.astype(BF)
     for section in range(2):
-        fill(high_a, low_a, codes, 16 * section)
-        fill(high_b, low_b, codes, 32 + 16 * section)
-        near = (dot(high_a[...], near) + dot(low_a[...], near)).astype(BF)
-        other = (dot(high_b[...], other) + dot(low_b[...], other)).astype(BF)
+        near = transport(codes, 16 * section, near)
+        other = transport(codes, 32 + 16 * section, other)
     warped = near[:, :128]
     residual = image - warped.astype(F32)
     image = image.astype(BF)
@@ -299,6 +312,12 @@
     )
 
 
+def swap(chunks):
+    chunks = chunks.reshape(640, 4, 128)
+    chunks = lax.all_to_all(chunks, "pencil", 0, 0, axis_index_groups=[ORDER], tiled=True)
+    return chunks.reshape(64, 40, 128)
+
+
 def local(template, reference_image, velocity, dep_owner, dep_offset, dep_weight):
     shape = jax.ShapeDtypeStruct
     piece = shape((N, 128), BF)
@@ -308,13 +327,13 @@
     inputs = (dep_owner, dep_offset, dep_weight, template, reference_image, pick)
     pack = call(
         pack_kernel,
-        shape((16, 2, 2, 40, 128), BF),
+        shape((64, 40, 128), BF),
         [ANY] * 6,
         VMEM,
         [vm(a.shape, a.dtype) for a in inputs] + [pltpu.SemaphoreType.DMA((6,))],
         65000000,
     )(*inputs)
-    got = lax.all_to_all(pack.reshape(640, 4, 128), "pencil", 0, 0, tiled=True)
+    got = swap(pack)
 
     deriv = bf(derivative_matrix())
     *parts, warped = call(
@@ -322,8 +341,8 @@
         [piece] * 5,
         [VMEM] * 2,
         [VMEM] * 5,
-        [vm((N, N), BF)] * 4 + [vm((4, N, 128), BF)],
-    )(got.reshape(64, 40, 128), deriv)
+        [vm((4, N, 128), BF)],
+    )(got, deriv)
     for s in (1, 2, 3):
         parts[s] = lax.ppermute(parts[s], "pencil", [(i ^ PARTNER[s], i) for i in range(128)])
 
@@ -335,7 +354,7 @@
         VMEM,
         [vm((N, N), BF)],
     )(*parts, warped, deriv, bf(table), bf(table.T))
-    home = lax.all_to_all(send.reshape(640, 4, 128), "pencil", 0, 0, tiled=True)
+    home = swap(send)
 
     return call(
         finish_kernel,
@@ -343,7 +362,7 @@
         [VMEM, VMEM, ANY],
         [ANY, ANY],
         [vm((3, 4, 32, N), F32), vm((3, 4, 32, N), F32), vm((4, 32, N), BF), pltpu.SemaphoreType.DMA((7,))],
-    )(home.reshape(64, 40, 128), bf(unpack_rows()), velocity)
+    )(home, bf(unpack_rows()), velocity)
 
 
 def solution(mesh):

time: 85.3 us -> 81.6 us (0.957); the launches traced: 85.1 us -> 80.4 us
  blocking collectives: 67.4 us -> 63.7 us
  Pallas kernels: 9.02 us -> 8.08 us
    all_to_all x2, blocking collectives: 67.4 us -> 63.7 us  [swap(): lax.all_to_all(chunks, 'pencil', 0, 0, axis_index_groups=[ORDER], tiled=T...]
    pallas_call x2, Pallas kernels: 5.71 us -> 4.78 us  [the longest x1 2.7 us: local(): call(pack_kernel, shape((64, 40, 128), BF), [ANY] * 6, VMEM, [vm(a.shape,...]
where the time goes in v5:
time: 81.6 us; the launch traced here: 80.4 us
  blocking collectives  63.7 us (78%)
  Pallas kernels  8.08 us (10%)
  waiting for transfers between devices  4.34 us (5%)
  starting transfers between devices  3.58 us (4%)
    all_to_all x2, blocking collectives, swap(): lax.all_to_all(chunks, 'pencil', 0, 0, axis_index_groups=[ORDER], tiled=T...  63.7 us
    ppermute x3, waiting for transfers between devices, local(): lax.ppermute(parts[s], 'pencil', [(i ^ PARTNER[s], i) for i in range(128)])  4.34 us
    ppermute x3, starting transfers between devices, local(): lax.ppermute(parts[s], 'pencil', [(i ^ PARTNER[s], i) for i in range(128)])  3.58 us
    pallas_call x1, Pallas kernels, local(): call(pack_kernel, shape((64, 40, 128), BF), [ANY] * 6, VMEM, [vm(a.shape,...  2.7 us
    pallas_call x1, Pallas kernels, local(): call(transport_kernel, [piece] * 5, [VMEM] * 2, [VMEM] * 5, [vm((4, N, 12...  2.07 us
    pallas_call x1, Pallas kernels, local(): call(finish_kernel, [shape((4, 32, N), BF), shape((3, 4, 32, N), F32)], [...  1.8 us
  transfers between devices with their start and end apart: 3, of which 2 were waited for; matrix products, arithmetic and copies ran while one was open for 0% of the time, Pallas kernels for 0%

profile of v5, /device:TPU:2, one launch (start us, length us, event | category | flops | bytes accessed | tf_op | source)
XLA Modules:
  0.0 80.4 jit_solution(4423721694693664872)
XLA Ops:
  0.6 2.7 %shard_map.122 = bf16[64,40,128]{2,1,0:T(8,128)(2,1)} custom-call(s32[2,256]{1,0:T(2,128)} %owner_ref.1, s32[2,256]{1,0:T(2,128)} %offset_ref.1, s32[2,256]{1,0:T(2,128)} %weight_ref.1, bf16[4,32,512]{2,1,0:T(8,128)(2,1)} %template_ref.1, bf16[4,32,512]{2,1,0:T(8,128)(2,1)} %image_ref.1, bf16[768,384]{1,0:T(8,128)(2,1)} %constant.10.clone.pick_ref), custom_call_target="tpu_custom_call" | custom-call | tf_op jit(solution)/shard_map/pallas_call | solution.py:328
  3.3 0.0 copy-start
  3.4 35.6 %all_to_all.10 = bf16[640,4,128]{2,1,0:T(4,128)(2,1)S(1)} all-to-all(bf16[640,4,128]{2,1,0:T(4,128)(2,1)} %bitcast.7), channel_id=1, replica_groups={{12,13,110,111,100,101,120,121,96,97,46,47,62,63,70,71,50,51,26,27,56,5..., dimensions={0} | all-to-all | bytes 1310720 | tf_op jit(solution)/shard_map/all_to_all | solution.py:317
  39.0 0.0 copy-done
  39.0 0.0 copy-start.3
  39.0 0.0 copy-start.4
  39.0 2.1 %shard_map.123 = (bf16[512,128]{1,0:T(8,128)(2,1)S(1)}, bf16[512,128]{1,0:T(8,128)(2,1)S(1)}, bf16[512,128]{1,0:T(8,128)(2,1)S(1)}, bf16[512,128]{1,0:T(8,128)(2,1)S(1)}, bf16[512,128]{1,0:T(8,128)(2,1)S(1)}) custom-call(bf16[64,40,128]{2,1,0:T(8,128)(2,1)S(1)} %bitcast.4, bf16[512,512]{1,0:T(8,128)(2,1)S(1)} %copy-done), custom_call_target="tpu_custom_call" | custom-call | tf_op jit(solution)/shard_map/pallas_call | solution.py:339
  41.0 0.5 collective-permute-start
  41.5 1.2 %collective-permute-start.1 = (bf16[512,128]{1,0:T(8,128)(2,1)S(1)}, bf16[512,128]{1,0:T(8,128)(2,1)S(1)}, u32[]{:S(2)}, u32[]{:S(2)}) collective-permute-start(bf16[512,128]{1,0:T(8,128)(2,1)S(1)} %get-tuple-element.9), channel_id=1, source_target_pairs={{4,0},{5,1},{6,2},{7,3},{0,4},{1,5},{2,6},{3,7},{12,8},{13,9},{14,... | collective-permute-start | bytes 393224 | tf_op jit(solution)/shard_map/ppermute | solution.py:347
  42.7 1.9 %collective-permute-start.2 = (bf16[512,128]{1,0:T(8,128)(2,1)S(1)}, bf16[512,128]{1,0:T(8,128)(2,1)S(1)}, u32[]{:S(2)}, u32[]{:S(2)}) collective-permute-start(bf16[512,128]{1,0:T(8,128)(2,1)S(1)} %get-tuple-element.10), channel_id=1, source_target_pairs={{5,0},{4,1},{7,2},{6,3},{1,4},{0,5},{3,6},{2,7},{13,8},{12,9},{15,... | collective-permute-start | bytes 393224 | tf_op jit(solution)/shard_map/ppermute | solution.py:347
  44.6 2.6 %collective-permute-done.p1_ref = bf16[512,128]{1,0:T(8,128)(2,1)S(1)} collective-permute-done((bf16[512,128]{1,0:T(8,128)(2,1)S(1)}, bf16[512,128]{1,0:T(8,128)(2,1)S(1)}, u32[]{:S(2)}, u32[]{:S(2)}) %collective-permute-start) | collective-permute-done | bytes 131104 | tf_op jit(solution)/shard_map/ppermute | solution.py:347
  47.2 0.0 collective-permute-done.1.p2_ref
  47.2 1.7 %collective-permute-done.2.p3_ref = bf16[512,128]{1,0:T(8,128)(2,1)S(1)} collective-permute-done((bf16[512,128]{1,0:T(8,128)(2,1)S(1)}, bf16[512,128]{1,0:T(8,128)(2,1)S(1)}, u32[]{:S(2)}, u32[]{:S(2)}) %collective-permute-start.2) | collective-permute-done | bytes 131104 | tf_op jit(solution)/shard_map/ppermute | solution.py:347
  49.0 0.0 copy-done.3
  49.0 0.0 copy-done.4
  49.0 1.5 %shard_map.124 = bf16[64,40,128]{2,1,0:T(8,128)(2,1)S(1)} custom-call(bf16[512,128]{1,0:T(8,128)(2,1)S(1)} %get-tuple-element.7.p0_ref, bf16[512,128]{1,0:T(8,128)(2,1)S(1)} %collective-permute-done.p1_ref, bf16[512,128]{1,0:T(8,128)(2,1)S(1)} %collective-permute-done.1.p2_ref, bf16[512,128]{1,0:T(8,128)(2,1)S(1)} %collective-permute-done.2.p3_ref, ...), custom_call_target="tpu_custom_call" | custom-call | tf_op jit(solution)/shard_map/pallas_call | solution.py:350
  50.5 0.0 copy-start.1
  50.5 0.0 copy-start.2
  50.5 28.1 %all_to_all.11 = bf16[640,4,128]{2,1,0:T(4,128)(2,1)S(1)} all-to-all(bf16[640,4,128]{2,1,0:T(4,128)(2,1)S(1)} %bitcast.5), channel_id=1, replica_groups={{12,13,110,111,100,101,120,121,96,97,46,47,62,63,70,71,50,51,26,27,56,5..., dimensions={0} | all-to-all | bytes 1310720 | tf_op jit(solution)/shard_map/all_to_all | solution.py:317
  78.6 0.0 copy-done.1
  78.6 0.0 copy-done.2
  78.6 1.8 %shard_map.125 = (bf16[4,32,512]{2,1,0:T(8,128)(2,1)}, f32[3,4,32,512]{3,2,1,0:T(8,128)}) custom-call(bf16[64,40,128]{2,1,0:T(8,128)(2,1)S(1)} %bitcast.6, bf16[512,512]{1,0:T(8,128)(2,1)S(1)} %copy-done.2, f32[3,4,32,512]{3,2,1,0:T(8,128)S(1)} %copy-done.1), custom_call_target="tpu_custom_call" | custom-call | tf_op jit(solution)/shard_map/pallas_call | solution.py:359
Async XLA Ops:
  3.3 35.6 %copy-start = (bf16[512,512]{1,0:T(8,128)(2,1)S(1)}, bf16[512,512]{1,0:T(8,128)(2,1)}, u32[]{:S(2)}) copy-start(bf16[512,512]{1,0:T(8,128)(2,1)} %constant.11.clone.deriv_ref) | copy-start | bytes 1572868
  39.0 10.0 %copy-start.3 = (bf16[512,512]{1,0:T(8,128)(2,1)S(1)}, bf16[512,512]{1,0:T(8,128)(2,1)}, u32[]{:S(2)}) copy-start(bf16[512,512]{1,0:T(8,128)(2,1)} %constant.13.clone.flip_ref) | copy-start | bytes 1572868
  39.0 10.0 %copy-start.4 = (bf16[512,512]{1,0:T(8,128)(2,1)S(1)}, bf16[512,512]{1,0:T(8,128)(2,1)}, u32[]{:S(2)}) copy-start(bf16[512,512]{1,0:T(8,128)(2,1)} %constant.12.clone.table_ref) | copy-start | bytes 1572868
  41.0 6.2 %collective-permute-start = (bf16[512,128]{1,0:T(8,128)(2,1)S(1)}, bf16[512,128]{1,0:T(8,128)(2,1)S(1)}, u32[]{:S(2)}, u32[]{:S(2)}) collective-permute-start(bf16[512,128]{1,0:T(8,128)(2,1)S(1)} %get-tuple-element.8), channel_id=1, source_target_pairs={{1,0},{0,1},{3,2},{2,3},{5,4},{4,5},{7,6},{6,7},{9,8},{8,9},{11,10... | collective-permute-start | bytes 393224 | tf_op jit(solution)/shard_map/ppermute | solution.py:347
  41.5 5.7 %collective-permute-start.1 = (bf16[512,128]{1,0:T(8,128)(2,1)S(1)}, bf16[512,128]{1,0:T(8,128)(2,1)S(1)}, u32[]{:S(2)}, u32[]{:S(2)}) collective-permute-start(bf16[512,128]{1,0:T(8,128)(2,1)S(1)} %get-tuple-element.9), channel_id=1, source_target_pairs={{4,0},{5,1},{6,2},{7,3},{0,4},{1,5},{2,6},{3,7},{12,8},{13,9},{14,... | collective-permute-start | bytes 393224 | tf_op jit(solution)/shard_map/ppermute | solution.py:347
  42.7 6.3 %collective-permute-start.2 = (bf16[512,128]{1,0:T(8,128)(2,1)S(1)}, bf16[512,128]{1,0:T(8,128)(2,1)S(1)}, u32[]{:S(2)}, u32[]{:S(2)}) collective-permute-start(bf16[512,128]{1,0:T(8,128)(2,1)S(1)} %get-tuple-element.10), channel_id=1, source_target_pairs={{5,0},{4,1},{7,2},{6,3},{1,4},{0,5},{3,6},{2,7},{13,8},{12,9},{15,... | collective-permute-start | bytes 393224 | tf_op jit(solution)/shard_map/ppermute | solution.py:347
  50.5 28.1 %copy-start.1 = (f32[3,4,32,512]{3,2,1,0:T(8,128)S(1)}, f32[3,4,32,512]{3,2,1,0:T(8,128)}, u32[]{:S(2)}) copy-start(f32[3,4,32,512]{3,2,1,0:T(8,128)} %velocity_ref.1) | copy-start | bytes 2359300
  50.5 28.1 %copy-start.2 = (bf16[512,512]{1,0:T(8,128)(2,1)S(1)}, bf16[512,512]{1,0:T(8,128)(2,1)}, u32[]{:S(2)}) copy-start(bf16[512,512]{1,0:T(8,128)(2,1)} %constant.14.clone.pick_ref) | copy-start | bytes 1572868

commit v6 on v5

--- a/solution.py
+++ b/solution.py
@@ -43,17 +43,17 @@
 
 
 def pack_rows():
-    pick = np.zeros((32, 6, 4, 384), np.float32)
+    pick = np.zeros((32, 24, 320), np.float32)
     for z in range(32):
         other = (z + (1 if z % 2 else -1)) % 32
         for x in range(4):
-            pick[z, 0, x, x * 32 + z] = 1
-            pick[z, 1, x, x * 32 + (z ^ 1)] = 1
-            pick[z, 2, x, x * 32 + other] = 1
-            pick[z, 3, x, 128 + x * 32 + z] = 1
-            pick[z, 4, x, 256 + z * 4 + x] = 1
-            pick[z, 5, x, 256 + z * 4 + x] = 1
-    return pick.reshape(768, 384)
+            pick[z, x, x * 32 + z] = 1
+            pick[z, 4 + x, x * 32 + (z ^ 1)] = 1
+            pick[z, 8 + x, x * 32 + other] = 1
+            pick[z, 12 + x, 128 + x * 32 + z] = 1
+        pick[z, 16, 256 + z * 2] = 1
+        pick[z, 17, 257 + z * 2] = 1
+    return pick.reshape(768, 320)
 
 
 def unpack_rows():
@@ -65,9 +65,11 @@
     return pick
 
 
-PAIRS = [int(i) for i in np.random.RandomState(3).permutation(64)]
+QUADS = [int(i) for i in np.random.RandomState(1).permutation(32)]
+PAIRS = [2 * i + j for i in QUADS for j in (0, 1)]
+ORDER = [4 * i + j for i in QUADS for j in range(4)]
+QUAD_PLACE = [QUADS.index(i) for i in range(32)]
 PLACE = [PAIRS.index(i) for i in range(64)]
-ORDER = [2 * i + j for i in PAIRS for j in (0, 1)]
 
 PARTNER = (0, 1, 4, 5)
 
@@ -137,41 +139,76 @@
             value = jnp.where(row == 16 * section + i, item[section : section + 1], value)
     blank = jnp.zeros((32, 256), F32)
     codes = jnp.concatenate(
-        [
-            jnp.concatenate([value, blank, blank, blank], axis=0),
-            jnp.concatenate([blank, value, blank, blank], axis=0),
-        ],
-        axis=1,
+        [jnp.concatenate([value if i == j else blank for j in range(4)], axis=1) for i in range(4)], axis=0
     ).astype(BF)
-    row, col = iota((N, 256), 0), iota((N, 256), 1)
-    q, z, x = row >> 7, (row >> 2) & 31, row & 3
+    row, col = iota((256, 256), 0), iota((256, 256), 1)
+    q, z = row >> 6, (row >> 1) & 31
     other = (z + 2 * (z & 1) - 1) & 31
-    near = jnp.where(col == x * 64 + (z >> 1) * 4 + q, 1.0, 0.0)
-    far = jnp.where(col == x * 64 + (other >> 1) * 4 + q, 1.0, 0.0)
-    codes = dot(jnp.concatenate([near, far], axis=1).astype(BF), codes, NT).astype(BF)
-    codes = jnp.concatenate([codes[128 * i : 128 * i + 128] for i in range(4)], axis=1)
+    hot = [
+        jnp.where(col == (2 * (row & 1) + x) * 64 + (plane >> 1) * 4 + q, 1.0, 0.0)
+        for x in range(2)
+        for plane in (z, other)
+    ]
+    codes = dot(jnp.concatenate(hot, axis=1).astype(BF), codes, NT).astype(BF)
+    codes = jnp.concatenate([codes[64 * i : 64 * i + 64] for i in range(4)], axis=1)
     for copy in copies[3:]:
         copy.wait()
     stack = jnp.concatenate([template[...].reshape(128, N), image[...].reshape(128, N), codes], axis=0)
     rows = dot(pick[...], stack)
-    low = iota((32, 8, 128), 1) < 4
-    for pair in range(2):
-        units = []
-        for q in (2 * pair, 2 * pair + 1):
-            part = rows[:, 128 * q : 128 * q + 128].reshape(32, 3, 8, 128)
-            units += [part[:, 0], part[:, 1], part[:, 2]]
-        a, b, c, d, e, f = units
-        d, e = pltpu.roll(d, 4, 1), pltpu.roll(e, 4, 1)
-        tiles = [a, b, jnp.where(low, c, d), jnp.where(low, d, e), jnp.where(low, e, f)]
+    at = iota((16, 8, 128), 1)
+    for half in range(2):
+        chunks = []
+        for j in range(4):
+            q = 2 * half + (j & 1)
+            part = rows[:, 128 * q : 128 * q + 128].reshape(16, 2, 3, 8, 128)[:, j >> 1]
+            part = [part[:, i] for i in range(3)]
+            chunks.append([pltpu.roll(v, 2 * j, 1) for v in part] if j else part)
+        (a0, b0, c0), (a1, b1, c1), (a2, b2, c2), (a3, b3, c3) = chunks
+        tiles = [
+            a0,
+            b0,
+            jnp.where(at < 2, c0, a1),
+            jnp.where(at < 2, a1, b1),
+            jnp.where(at < 2, b1, jnp.where(at < 4, c1, a2)),
+            jnp.where(at < 4, a2, b2),
+            jnp.where(at < 4, b2, jnp.where(at < 6, c2, a3)),
+            jnp.where(at < 6, a3, b3),
+            jnp.where(at < 6, b3, c3),
+        ]
         tiles = jnp.concatenate(tiles, axis=1).astype(BF)
-        for z in range(32):
-            out_ref[PLACE[(z // 2) * 4 + pair * 2 + z % 2]] = tiles[z]
-
-
-def units_of(ref, places=None):
+        for z in range(16):
+            out_ref[QUAD_PLACE[2 * z + half]] = tiles[z]
+
+
+def planes_of(ref):
+    t = [ref[:, 8 * i : 8 * i + 8, :].astype(F32) for i in range(9)]
+    t = [jnp.concatenate([v[i : i + 1] for i in QUAD_PLACE], axis=0) for v in t]
+    at = iota((32, 8, 128), 1)
+    low = at < 4
+
+    def turn(v, by):
+        return pltpu.roll(v, by, 1)
+
+    def join(first, second):
+        return jnp.stack([first, second], axis=1).reshape(N, 128)
+
+    units = []
+    for i in range(2):
+        v0 = t[i]
+        v1 = jnp.where(at < 2, t[3 + i], t[2 + i])
+        v2 = jnp.where(low, t[5 + i], t[4 + i])
+        v3 = jnp.where(at < 6, t[7 + i], t[6 + i])
+        units.append(join(jnp.where(low, v0, turn(v1, 2)), jnp.where(low, turn(v2, 4), turn(v3, 6))))
+        units.append(join(jnp.where(low, turn(v0, 4), turn(v1, 6)), jnp.where(low, v2, turn(v3, 2))))
+    codes = []
+    for v in (jnp.where(low, t[2], turn(t[4], 2)), jnp.where(low, turn(t[6], 4), turn(t[8], 6))):
+        v = jnp.where((at & 3) == 0, v, jnp.where((at & 3) == 3, turn(v, 2), turn(v, 1)))
+        codes.append(jnp.where((at & 1) == 1, pltpu.roll(v, 64, 2), v))
+    return units + [join(*codes)]
+
+
+def units_of(ref):
     t = [ref[:, 8 * i : 8 * i + 8, :].astype(F32) for i in range(5)]
-    if places is not None:
-        t = [jnp.concatenate([v[i : i + 1] for i in places], axis=0) for v in t]
     low = iota((64, 8, 128), 1) < 4
     units = [
         jnp.where(low, t[0], t[2]),
@@ -226,7 +263,7 @@
 
 def transport_kernel(got_ref, deriv_ref, out0_ref, out1_ref, out2_ref, out3_ref, warped_ref, pieces):
     me = lax.axis_index("pencil")
-    own, partner, other, image, codes = units_of(got_ref, PLACE)
+    own, partner, other, image, codes = planes_of(got_ref)
     near = jnp.concatenate([own, partner], axis=1).astype(BF)
     other = other.astype(BF)
     for section in range(2):
@@ -312,10 +349,10 @@
     )
 
 
-def swap(chunks):
-    chunks = chunks.reshape(640, 4, 128)
-    chunks = lax.all_to_all(chunks, "pencil", 0, 0, axis_index_groups=[ORDER], tiled=True)
-    return chunks.reshape(64, 40, 128)
+def swap(chunks, rows):
+    chunks_of = chunks.reshape(-1, rows, 128)
+    chunks_of = lax.all_to_all(chunks_of, "pencil", 0, 0, axis_index_groups=[ORDER], tiled=True)
+    return chunks_of.reshape(chunks.shape)
 
 
 def local(template, reference_image, velocity, dep_owner, dep_offset, dep_weight):
@@ -327,13 +364,13 @@
     inputs = (dep_owner, dep_offset, dep_weight, template, reference_image, pick)
     pack = call(
         pack_kernel,
-        shape((64, 40, 128), BF),
+        shape((32, 72, 128), BF),
         [ANY] * 6,
         VMEM,
         [vm(a.shape, a.dtype) for a in inputs] + [pltpu.SemaphoreType.DMA((6,))],
         65000000,
     )(*inputs)
-    got = swap(pack)
+    got = swap(pack, 2)
 
     deriv = bf(derivative_matrix())
     *parts, warped = call(
@@ -354,7 +391,7 @@
         VMEM,
         [vm((N, N), BF)],
     )(*parts, warped, deriv, bf(table), bf(table.T))
-    home = swap(send)
+    home = swap(send, 4)
 
     return call(
         finish_kernel,

time: 81.6 us -> 78 us (0.956)
  blocking collectives: 63.7 us -> 59.2 us
    all_to_all x2, blocking collectives: 63.7 us -> 59.2 us  [swap(): lax.all_to_all(chunks_of, 'pencil', 0, 0, axis_index_groups=[ORDER], tile...]
  transfers between devices with their start and end apart: 3 -> 3, of which waited for: 2 -> 3; matrix products, arithmetic and copies ran while one was open for 0% -> 0% of each run, Pallas kernels for 0% -> 0%
where the time goes in v6:
time: 78 us; the launch traced here: 77.2 us
  blocking collectives  59.2 us (76%)
  Pallas kernels  8.38 us (11%)
  waiting for transfers between devices  4.7 us (6%)
  starting transfers between devices  4.22 us (5%)
    all_to_all x2, blocking collectives, swap(): lax.all_to_all(chunks_of, 'pencil', 0, 0, axis_index_groups=[ORDER], tile...  59.2 us
    ppermute x3, waiting for transfers between devices, local(): lax.ppermute(parts[s], 'pencil', [(i ^ PARTNER[s], i) for i in range(128)])  4.7 us
    ppermute x3, starting transfers between devices, local(): lax.ppermute(parts[s], 'pencil', [(i ^ PARTNER[s], i) for i in range(128)])  4.22 us
    pallas_call x1, Pallas kernels, local(): call(pack_kernel, shape((32, 72, 128), BF), [ANY] * 6, VMEM, [vm(a.shape,...  2.79 us
    pallas_call x1, Pallas kernels, local(): call(transport_kernel, [piece] * 5, [VMEM] * 2, [VMEM] * 5, [vm((4, N, 12...  2.28 us
    pallas_call x1, Pallas kernels, local(): call(finish_kernel, [shape((4, 32, N), BF), shape((3, 4, 32, N), F32)], [...  1.8 us
  transfers between devices with their start and end apart: 3, of which 3 were waited for; matrix products, arithmetic and copies ran while one was open for 0% of the time, Pallas kernels for 0%

profile of v6, /device:TPU:2, one launch (start us, length us, event | category | flops | bytes accessed | tf_op | source)
XLA Modules:
  0.0 77.2 jit_solution(16426237167753875715)
XLA Ops:
  0.6 2.8 %shard_map.122 = bf16[32,72,128]{2,1,0:T(8,128)(2,1)} custom-call(s32[2,256]{1,0:T(2,128)} %owner_ref.1, s32[2,256]{1,0:T(2,128)} %offset_ref.1, s32[2,256]{1,0:T(2,128)} %weight_ref.1, bf16[4,32,512]{2,1,0:T(8,128)(2,1)} %template_ref.1, bf16[4,32,512]{2,1,0:T(8,128)(2,1)} %image_ref.1, bf16[768,320]{1,0:T(8,128)(2,1)} %constant.10.clone.pick_ref), custom_call_target="tpu_custom_call" | custom-call | tf_op jit(solution)/shard_map/pallas_call | solution.py:365
  3.4 0.0 copy-start
  3.4 31.7 %all_to_all.10 = bf16[1152,2,128]{2,1,0:T(2,128)(2,1)S(1)} all-to-all(bf16[1152,2,128]{2,1,0:T(2,128)(2,1)} %bitcast.7), channel_id=1, replica_groups={{108,109,110,111,12,13,14,15,88,89,90,91,72,73,74,75,92,93,94,95,68,69,..., dimensions={0} | all-to-all | bytes 1179648 | tf_op jit(solution)/shard_map/all_to_all | solution.py:354
  35.1 0.0 copy-done
  35.1 0.0 copy-start.3
  35.1 0.0 copy-start.4
  35.1 2.3 %shard_map.123 = (bf16[512,128]{1,0:T(8,128)(2,1)S(1)}, bf16[512,128]{1,0:T(8,128)(2,1)S(1)}, bf16[512,128]{1,0:T(8,128)(2,1)S(1)}, bf16[512,128]{1,0:T(8,128)(2,1)S(1)}, bf16[512,128]{1,0:T(8,128)(2,1)S(1)}) custom-call(bf16[32,72,128]{2,1,0:T(8,128)(2,1)S(1)} %bitcast.6, bf16[512,512]{1,0:T(8,128)(2,1)S(1)} %copy-done), custom_call_target="tpu_custom_call" | custom-call | tf_op jit(solution)/shard_map/pallas_call | solution.py:376
  37.4 0.6 collective-permute-start
  38.0 2.4 %collective-permute-start.1 = (bf16[512,128]{1,0:T(8,128)(2,1)S(1)}, bf16[512,128]{1,0:T(8,128)(2,1)S(1)}, u32[]{:S(2)}, u32[]{:S(2)}) collective-permute-start(bf16[512,128]{1,0:T(8,128)(2,1)S(1)} %get-tuple-element.9), channel_id=1, source_target_pairs={{4,0},{5,1},{6,2},{7,3},{0,4},{1,5},{2,6},{3,7},{12,8},{13,9},{14,... | collective-permute-start | bytes 393224 | tf_op jit(solution)/shard_map/ppermute | solution.py:384
  40.5 1.2 %collective-permute-start.2 = (bf16[512,128]{1,0:T(8,128)(2,1)S(1)}, bf16[512,128]{1,0:T(8,128)(2,1)S(1)}, u32[]{:S(2)}, u32[]{:S(2)}) collective-permute-start(bf16[512,128]{1,0:T(8,128)(2,1)S(1)} %get-tuple-element.10), channel_id=1, source_target_pairs={{5,0},{4,1},{7,2},{6,3},{1,4},{0,5},{3,6},{2,7},{13,8},{12,9},{15,... | collective-permute-start | bytes 393224 | tf_op jit(solution)/shard_map/ppermute | solution.py:384
  41.6 2.2 %collective-permute-done.p1_ref = bf16[512,128]{1,0:T(8,128)(2,1)S(1)} collective-permute-done((bf16[512,128]{1,0:T(8,128)(2,1)S(1)}, bf16[512,128]{1,0:T(8,128)(2,1)S(1)}, u32[]{:S(2)}, u32[]{:S(2)}) %collective-permute-start) | collective-permute-done | bytes 131104 | tf_op jit(solution)/shard_map/ppermute | solution.py:384
  43.9 0.8 collective-permute-done.1.p2_ref
  44.6 1.7 %collective-permute-done.2.p3_ref = bf16[512,128]{1,0:T(8,128)(2,1)S(1)} collective-permute-done((bf16[512,128]{1,0:T(8,128)(2,1)S(1)}, bf16[512,128]{1,0:T(8,128)(2,1)S(1)}, u32[]{:S(2)}, u32[]{:S(2)}) %collective-permute-start.2) | collective-permute-done | bytes 131104 | tf_op jit(solution)/shard_map/ppermute | solution.py:384
  46.3 0.0 copy-done.3
  46.3 0.0 copy-done.4
  46.3 1.5 %shard_map.124 = bf16[64,40,128]{2,1,0:T(8,128)(2,1)S(1)} custom-call(bf16[512,128]{1,0:T(8,128)(2,1)S(1)} %get-tuple-element.7.p0_ref, bf16[512,128]{1,0:T(8,128)(2,1)S(1)} %collective-permute-done.p1_ref, bf16[512,128]{1,0:T(8,128)(2,1)S(1)} %collective-permute-done.1.p2_ref, bf16[512,128]{1,0:T(8,128)(2,1)S(1)} %collective-permute-done.2.p3_ref, ...), custom_call_target="tpu_custom_call" | custom-call | tf_op jit(solution)/shard_map/pallas_call | solution.py:387
  47.9 0.0 copy-start.1
  47.9 0.0 copy-start.2
  47.9 27.5 %all_to_all.11 = bf16[640,4,128]{2,1,0:T(4,128)(2,1)S(1)} all-to-all(bf16[640,4,128]{2,1,0:T(4,128)(2,1)S(1)} %bitcast.4), channel_id=1, replica_groups={{108,109,110,111,12,13,14,15,88,89,90,91,72,73,74,75,92,93,94,95,68,69,..., dimensions={0} | all-to-all | bytes 1310720 | tf_op jit(solution)/shard_map/all_to_all | solution.py:354
  75.4 0.0 copy-done.1
  75.4 0.0 copy-done.2
  75.4 1.8 %shard_map.125 = (bf16[4,32,512]{2,1,0:T(8,128)(2,1)}, f32[3,4,32,512]{3,2,1,0:T(8,128)}) custom-call(bf16[64,40,128]{2,1,0:T(8,128)(2,1)S(1)} %bitcast.5, bf16[512,512]{1,0:T(8,128)(2,1)S(1)} %copy-done.2, f32[3,4,32,512]{3,2,1,0:T(8,128)S(1)} %copy-done.1), custom_call_target="tpu_custom_call" | custom-call | tf_op jit(solution)/shard_map/pallas_call | solution.py:396
Async XLA Ops:
  3.4 31.7 %copy-start = (bf16[512,512]{1,0:T(8,128)(2,1)S(1)}, bf16[512,512]{1,0:T(8,128)(2,1)}, u32[]{:S(2)}) copy-start(bf16[512,512]{1,0:T(8,128)(2,1)} %constant.11.clone.deriv_ref) | copy-start | bytes 1572868
  35.1 11.2 %copy-start.3 = (bf16[512,512]{1,0:T(8,128)(2,1)S(1)}, bf16[512,512]{1,0:T(8,128)(2,1)}, u32[]{:S(2)}) copy-start(bf16[512,512]{1,0:T(8,128)(2,1)} %constant.13.clone.flip_ref) | copy-start | bytes 1572868
  35.1 11.2 %copy-start.4 = (bf16[512,512]{1,0:T(8,128)(2,1)S(1)}, bf16[512,512]{1,0:T(8,128)(2,1)}, u32[]{:S(2)}) copy-start(bf16[512,512]{1,0:T(8,128)(2,1)} %constant.12.clone.table_ref) | copy-start | bytes 1572868
  37.4 6.5 %collective-permute-start = (bf16[512,128]{1,0:T(8,128)(2,1)S(1)}, bf16[512,128]{1,0:T(8,128)(2,1)S(1)}, u32[]{:S(2)}, u32[]{:S(2)}) collective-permute-start(bf16[512,128]{1,0:T(8,128)(2,1)S(1)} %get-tuple-element.8), channel_id=1, source_target_pairs={{1,0},{0,1},{3,2},{2,3},{5,4},{4,5},{7,6},{6,7},{9,8},{8,9},{11,10... | collective-permute-start | bytes 393224 | tf_op jit(solution)/shard_map/ppermute | solution.py:384
  38.0 6.6 %collective-permute-start.1 = (bf16[512,128]{1,0:T(8,128)(2,1)S(1)}, bf16[512,128]{1,0:T(8,128)(2,1)S(1)}, u32[]{:S(2)}, u32[]{:S(2)}) collective-permute-start(bf16[512,128]{1,0:T(8,128)(2,1)S(1)} %get-tuple-element.9), channel_id=1, source_target_pairs={{4,0},{5,1},{6,2},{7,3},{0,4},{1,5},{2,6},{3,7},{12,8},{13,9},{14,... | collective-permute-start | bytes 393224 | tf_op jit(solution)/shard_map/ppermute | solution.py:384
  40.5 5.9 %collective-permute-start.2 = (bf16[512,128]{1,0:T(8,128)(2,1)S(1)}, bf16[512,128]{1,0:T(8,128)(2,1)S(1)}, u32[]{:S(2)}, u32[]{:S(2)}) collective-permute-start(bf16[512,128]{1,0:T(8,128)(2,1)S(1)} %get-tuple-element.10), channel_id=1, source_target_pairs={{5,0},{4,1},{7,2},{6,3},{1,4},{0,5},{3,6},{2,7},{13,8},{12,9},{15,... | collective-permute-start | bytes 393224 | tf_op jit(solution)/shard_map/ppermute | solution.py:384
  47.9 27.5 %copy-start.1 = (f32[3,4,32,512]{3,2,1,0:T(8,128)S(1)}, f32[3,4,32,512]{3,2,1,0:T(8,128)}, u32[]{:S(2)}) copy-start(f32[3,4,32,512]{3,2,1,0:T(8,128)} %velocity_ref.1) | copy-start | bytes 2359300
  47.9 27.5 %copy-start.2 = (bf16[512,512]{1,0:T(8,128)(2,1)S(1)}, bf16[512,512]{1,0:T(8,128)(2,1)}, u32[]{:S(2)}) copy-start(bf16[512,512]{1,0:T(8,128)(2,1)} %constant.14.clone.pick_ref) | copy-start | bytes 1572868

commit v7 on v6

--- a/solution.py
+++ b/solution.py
@@ -66,8 +66,8 @@
 
 
 QUADS = [int(i) for i in np.random.RandomState(1).permutation(32)]
-PAIRS = [2 * i + j for i in QUADS for j in (0, 1)]
-ORDER = [4 * i + j for i in QUADS for j in range(4)]
+PAIRS = [int(i) for i in np.random.RandomState(24).permutation(64)]
+ORDERS = [[4 * i + j for i in QUADS for j in range(4)], [2 * i + j for i in PAIRS for j in (0, 1)]]
 QUAD_PLACE = [QUADS.index(i) for i in range(32)]
 PLACE = [PAIRS.index(i) for i in range(64)]
 
@@ -349,9 +349,9 @@
     )
 
 
-def swap(chunks, rows):
+def swap(chunks, rows, order):
     chunks_of = chunks.reshape(-1, rows, 128)
-    chunks_of = lax.all_to_all(chunks_of, "pencil", 0, 0, axis_index_groups=[ORDER], tiled=True)
+    chunks_of = lax.all_to_all(chunks_of, "pencil", 0, 0, axis_index_groups=[order], tiled=True)
     return chunks_of.reshape(chunks.shape)
 
 
@@ -370,7 +370,7 @@
         [vm(a.shape, a.dtype) for a in inputs] + [pltpu.SemaphoreType.DMA((6,))],
         65000000,
     )(*inputs)
-    got = swap(pack, 2)
+    got = swap(pack, 2, ORDERS[0])
 
     deriv = bf(derivative_matrix())
     *parts, warped = call(
@@ -391,7 +391,7 @@
         VMEM,
         [vm((N, N), BF)],
     )(*parts, warped, deriv, bf(table), bf(table.T))
-    home = swap(send, 4)
+    home = swap(send, 4, ORDERS[1])
 
     return call(
         finish_kernel,

time: 78 us -> 77.3 us (level)
  no operation moved by 1% of the time
where the time goes in v7:
time: 77.3 us; the launch traced here: 76.7 us
  blocking collectives  58.6 us (76%)
  Pallas kernels  8.38 us (11%)
  waiting for transfers between devices  4.7 us (6%)
  starting transfers between devices  4.22 us (5%)
    all_to_all x2, blocking collectives, swap(): lax.all_to_all(chunks_of, 'pencil', 0, 0, axis_index_groups=[order], tile...  58.6 us
    ppermute x3, waiting for transfers between devices, local(): lax.ppermute(parts[s], 'pencil', [(i ^ PARTNER[s], i) for i in range(128)])  4.7 us
    ppermute x3, starting transfers between devices, local(): lax.ppermute(parts[s], 'pencil', [(i ^ PARTNER[s], i) for i in range(128)])  4.22 us
    pallas_call x1, Pallas kernels, local(): call(pack_kernel, shape((32, 72, 128), BF), [ANY] * 6, VMEM, [vm(a.shape,...  2.79 us
    pallas_call x1, Pallas kernels, local(): call(transport_kernel, [piece] * 5, [VMEM] * 2, [VMEM] * 5, [vm((4, N, 12...  2.28 us
    pallas_call x1, Pallas kernels, local(): call(finish_kernel, [shape((4, 32, N), BF), shape((3, 4, 32, N), F32)], [...  1.8 us
  transfers between devices with their start and end apart: 3, of which 3 were waited for; matrix products, arithmetic and copies ran while one was open for 0% of the time, Pallas kernels for 0%

profile of v7, /device:TPU:2, one launch (start us, length us, event | category | flops | bytes accessed | tf_op | source)
XLA Modules:
  0.0 76.7 jit_solution(15064643584739961897)
XLA Ops:
  0.6 2.8 %shard_map.122 = bf16[32,72,128]{2,1,0:T(8,128)(2,1)} custom-call(s32[2,256]{1,0:T(2,128)} %owner_ref.1, s32[2,256]{1,0:T(2,128)} %offset_ref.1, s32[2,256]{1,0:T(2,128)} %weight_ref.1, bf16[4,32,512]{2,1,0:T(8,128)(2,1)} %template_ref.1, bf16[4,32,512]{2,1,0:T(8,128)(2,1)} %image_ref.1, bf16[768,320]{1,0:T(8,128)(2,1)} %constant.10.clone.pick_ref), custom_call_target="tpu_custom_call" | custom-call | tf_op jit(solution)/shard_map/pallas_call | solution.py:365
  3.4 0.0 copy-start
  3.4 31.7 %all_to_all.10 = bf16[1152,2,128]{2,1,0:T(2,128)(2,1)S(1)} all-to-all(bf16[1152,2,128]{2,1,0:T(2,128)(2,1)} %bitcast.7), channel_id=1, replica_groups={{108,109,110,111,12,13,14,15,88,89,90,91,72,73,74,75,92,93,94,95,68,69,..., dimensions={0} | all-to-all | bytes 1179648 | tf_op jit(solution)/shard_map/all_to_all | solution.py:354
  35.1 0.0 copy-done
  35.1 0.0 copy-start.3
  35.1 0.0 copy-start.4
  35.1 2.3 %shard_map.123 = (bf16[512,128]{1,0:T(8,128)(2,1)S(1)}, bf16[512,128]{1,0:T(8,128)(2,1)S(1)}, bf16[512,128]{1,0:T(8,128)(2,1)S(1)}, bf16[512,128]{1,0:T(8,128)(2,1)S(1)}, bf16[512,128]{1,0:T(8,128)(2,1)S(1)}) custom-call(bf16[32,72,128]{2,1,0:T(8,128)(2,1)S(1)} %bitcast.6, bf16[512,512]{1,0:T(8,128)(2,1)S(1)} %copy-done), custom_call_target="tpu_custom_call" | custom-call | tf_op jit(solution)/shard_map/pallas_call | solution.py:376
  37.4 0.6 collective-permute-start
  38.0 2.4 %collective-permute-start.1 = (bf16[512,128]{1,0:T(8,128)(2,1)S(1)}, bf16[512,128]{1,0:T(8,128)(2,1)S(1)}, u32[]{:S(2)}, u32[]{:S(2)}) collective-permute-start(bf16[512,128]{1,0:T(8,128)(2,1)S(1)} %get-tuple-element.9), channel_id=1, source_target_pairs={{4,0},{5,1},{6,2},{7,3},{0,4},{1,5},{2,6},{3,7},{12,8},{13,9},{14,... | collective-permute-start | bytes 393224 | tf_op jit(solution)/shard_map/ppermute | solution.py:384
  40.5 1.2 %collective-permute-start.2 = (bf16[512,128]{1,0:T(8,128)(2,1)S(1)}, bf16[512,128]{1,0:T(8,128)(2,1)S(1)}, u32[]{:S(2)}, u32[]{:S(2)}) collective-permute-start(bf16[512,128]{1,0:T(8,128)(2,1)S(1)} %get-tuple-element.10), channel_id=1, source_target_pairs={{5,0},{4,1},{7,2},{6,3},{1,4},{0,5},{3,6},{2,7},{13,8},{12,9},{15,... | collective-permute-start | bytes 393224 | tf_op jit(solution)/shard_map/ppermute | solution.py:384
  41.6 2.2 %collective-permute-done.p1_ref = bf16[512,128]{1,0:T(8,128)(2,1)S(1)} collective-permute-done((bf16[512,128]{1,0:T(8,128)(2,1)S(1)}, bf16[512,128]{1,0:T(8,128)(2,1)S(1)}, u32[]{:S(2)}, u32[]{:S(2)}) %collective-permute-start) | collective-permute-done | bytes 131104 | tf_op jit(solution)/shard_map/ppermute | solution.py:384
  43.9 0.8 collective-permute-done.1.p2_ref
  44.6 1.7 %collective-permute-done.2.p3_ref = bf16[512,128]{1,0:T(8,128)(2,1)S(1)} collective-permute-done((bf16[512,128]{1,0:T(8,128)(2,1)S(1)}, bf16[512,128]{1,0:T(8,128)(2,1)S(1)}, u32[]{:S(2)}, u32[]{:S(2)}) %collective-permute-start.2) | collective-permute-done | bytes 131104 | tf_op jit(solution)/shard_map/ppermute | solution.py:384
  46.3 0.0 copy-done.3
  46.3 0.0 copy-done.4
  46.3 1.5 %shard_map.124 = bf16[64,40,128]{2,1,0:T(8,128)(2,1)S(1)} custom-call(bf16[512,128]{1,0:T(8,128)(2,1)S(1)} %get-tuple-element.7.p0_ref, bf16[512,128]{1,0:T(8,128)(2,1)S(1)} %collective-permute-done.p1_ref, bf16[512,128]{1,0:T(8,128)(2,1)S(1)} %collective-permute-done.1.p2_ref, bf16[512,128]{1,0:T(8,128)(2,1)S(1)} %collective-permute-done.2.p3_ref, ...), custom_call_target="tpu_custom_call" | custom-call | tf_op jit(solution)/shard_map/pallas_call | solution.py:387
  47.9 0.0 copy-start.1
  47.9 0.0 copy-start.2
  47.9 27.0 %all_to_all.11 = bf16[640,4,128]{2,1,0:T(4,128)(2,1)S(1)} all-to-all(bf16[640,4,128]{2,1,0:T(4,128)(2,1)S(1)} %bitcast.4), channel_id=1, replica_groups={{90,91,38,39,32,33,60,61,4,5,76,77,100,101,74,75,120,121,54,55,64,65,40..., dimensions={0} | all-to-all | bytes 1310720 | tf_op jit(solution)/shard_map/all_to_all | solution.py:354
  74.8 0.0 copy-done.1
  74.8 0.0 copy-done.2
  74.9 1.8 %shard_map.125 = (bf16[4,32,512]{2,1,0:T(8,128)(2,1)}, f32[3,4,32,512]{3,2,1,0:T(8,128)}) custom-call(bf16[64,40,128]{2,1,0:T(8,128)(2,1)S(1)} %bitcast.5, bf16[512,512]{1,0:T(8,128)(2,1)S(1)} %copy-done.2, f32[3,4,32,512]{3,2,1,0:T(8,128)S(1)} %copy-done.1), custom_call_target="tpu_custom_call" | custom-call | tf_op jit(solution)/shard_map/pallas_call | solution.py:396
Async XLA Ops:
  3.4 31.7 %copy-start = (bf16[512,512]{1,0:T(8,128)(2,1)S(1)}, bf16[512,512]{1,0:T(8,128)(2,1)}, u32[]{:S(2)}) copy-start(bf16[512,512]{1,0:T(8,128)(2,1)} %constant.11.clone.deriv_ref) | copy-start | bytes 1572868
  35.1 11.2 %copy-start.3 = (bf16[512,512]{1,0:T(8,128)(2,1)S(1)}, bf16[512,512]{1,0:T(8,128)(2,1)}, u32[]{:S(2)}) copy-start(bf16[512,512]{1,0:T(8,128)(2,1)} %constant.13.clone.flip_ref) | copy-start | bytes 1572868
  35.1 11.2 %copy-start.4 = (bf16[512,512]{1,0:T(8,128)(2,1)S(1)}, bf16[512,512]{1,0:T(8,128)(2,1)}, u32[]{:S(2)}) copy-start(bf16[512,512]{1,0:T(8,128)(2,1)} %constant.12.clone.table_ref) | copy-start | bytes 1572868
  37.4 6.5 %collective-permute-start = (bf16[512,128]{1,0:T(8,128)(2,1)S(1)}, bf16[512,128]{1,0:T(8,128)(2,1)S(1)}, u32[]{:S(2)}, u32[]{:S(2)}) collective-permute-start(bf16[512,128]{1,0:T(8,128)(2,1)S(1)} %get-tuple-element.8), channel_id=1, source_target_pairs={{1,0},{0,1},{3,2},{2,3},{5,4},{4,5},{7,6},{6,7},{9,8},{8,9},{11,10... | collective-permute-start | bytes 393224 | tf_op jit(solution)/shard_map/ppermute | solution.py:384
  38.0 6.6 %collective-permute-start.1 = (bf16[512,128]{1,0:T(8,128)(2,1)S(1)}, bf16[512,128]{1,0:T(8,128)(2,1)S(1)}, u32[]{:S(2)}, u32[]{:S(2)}) collective-permute-start(bf16[512,128]{1,0:T(8,128)(2,1)S(1)} %get-tuple-element.9), channel_id=1, source_target_pairs={{4,0},{5,1},{6,2},{7,3},{0,4},{1,5},{2,6},{3,7},{12,8},{13,9},{14,... | collective-permute-start | bytes 393224 | tf_op jit(solution)/shard_map/ppermute | solution.py:384
  40.5 5.9 %collective-permute-start.2 = (bf16[512,128]{1,0:T(8,128)(2,1)S(1)}, bf16[512,128]{1,0:T(8,128)(2,1)S(1)}, u32[]{:S(2)}, u32[]{:S(2)}) collective-permute-start(bf16[512,128]{1,0:T(8,128)(2,1)S(1)} %get-tuple-element.10), channel_id=1, source_target_pairs={{5,0},{4,1},{7,2},{6,3},{1,4},{0,5},{3,6},{2,7},{13,8},{12,9},{15,... | collective-permute-start | bytes 393224 | tf_op jit(solution)/shard_map/ppermute | solution.py:384
  47.9 27.0 %copy-start.1 = (f32[3,4,32,512]{3,2,1,0:T(8,128)S(1)}, f32[3,4,32,512]{3,2,1,0:T(8,128)}, u32[]{:S(2)}) copy-start(f32[3,4,32,512]{3,2,1,0:T(8,128)} %velocity_ref.1) | copy-start | bytes 2359300
  47.9 27.0 %copy-start.2 = (bf16[512,512]{1,0:T(8,128)(2,1)S(1)}, bf16[512,512]{1,0:T(8,128)(2,1)}, u32[]{:S(2)}) copy-start(bf16[512,512]{1,0:T(8,128)(2,1)} %constant.14.clone.pick_ref) | copy-start | bytes 1572868

commit v8 on v7

--- a/solution.py
+++ b/solution.py
@@ -238,21 +238,22 @@
 
 def transport(codes, at, f):
     taps = []
+    weights = codes + pltpu.roll(codes, 124, 1)
     for i in range(4):
         part = codes[128 * i : 128 * i + 128]
+        whole = weights[128 * i : 128 * i + 128]
         rel = part[:, at : at + 1]
-        pieces = [[part[:, at + j + k : at + j + 1 + k] for k in range(4)] for j in (1, 5)]
+        levels = [whole[:, at + 1 + k : at + 2 + k] for k in range(4)]
         moved = []
         for tile, first, count in ((0, 0, 128), (-1, 0, 16), (1, 112, 16)):
             rows = slice(first, first + count)
             row = iota((count, 128), 0) + first
             lag = (iota((count, 128), 1) + 128 * tile - (row & -4)).astype(F32) - rel[rows]
-            band = []
-            for piece in pieces:
-                weight = jnp.zeros((count, 128), F32)
-                for k in range(4):
-                    weight = jnp.where(lag == k, piece[k][rows], weight)
-                band.append(weight.astype(BF))
+            weight = jnp.zeros((count, 128), F32)
+            for k in range(4):
+                weight = jnp.where(lag == k, levels[k][rows], weight)
+            high = weight.astype(BF)
+            band = [high, (weight - high.astype(F32)).astype(BF)]
             j = (i + tile) % 4
             source = f[128 * j : 128 * j + 128]
             moved.append(dot(jnp.concatenate(band, axis=1), jnp.concatenate([source, source], axis=0)))

time: 77.3 us -> 77.1 us (level)
  no operation moved by 1% of the time
where the time goes in v8:
time: 77.1 us; the launch traced here: 76.5 us
  blocking collectives  58.6 us (76%)
  Pallas kernels  8.21 us (11%)
  waiting for transfers between devices  4.7 us (6%)
  starting transfers between devices  4.22 us (5%)
    all_to_all x2, blocking collectives, swap(): lax.all_to_all(chunks_of, 'pencil', 0, 0, axis_index_groups=[order], tile...  58.6 us
    ppermute x3, waiting for transfers between devices, local(): lax.ppermute(parts[s], 'pencil', [(i ^ PARTNER[s], i) for i in range(128)])  4.7 us
    ppermute x3, starting transfers between devices, local(): lax.ppermute(parts[s], 'pencil', [(i ^ PARTNER[s], i) for i in range(128)])  4.22 us
    pallas_call x1, Pallas kernels, local(): call(pack_kernel, shape((32, 72, 128), BF), [ANY] * 6, VMEM, [vm(a.shape,...  2.79 us
    pallas_call x1, Pallas kernels, local(): call(transport_kernel, [piece] * 5, [VMEM] * 2, [VMEM] * 5, [vm((4, N, 12...  2.12 us
    pallas_call x1, Pallas kernels, local(): call(finish_kernel, [shape((4, 32, N), BF), shape((3, 4, 32, N), F32)], [...  1.8 us
  transfers between devices with their start and end apart: 3, of which 3 were waited for; matrix products, arithmetic and copies ran while one was open for 0% of the time, Pallas kernels for 0%

profile of v8, /device:TPU:2, one launch (start us, length us, event | category | flops | bytes accessed | tf_op | source)
XLA Modules:
  0.0 76.5 jit_solution(18110109295063387154)
XLA Ops:
  0.6 2.8 %shard_map.122 = bf16[32,72,128]{2,1,0:T(8,128)(2,1)} custom-call(s32[2,256]{1,0:T(2,128)} %owner_ref.1, s32[2,256]{1,0:T(2,128)} %offset_ref.1, s32[2,256]{1,0:T(2,128)} %weight_ref.1, bf16[4,32,512]{2,1,0:T(8,128)(2,1)} %template_ref.1, bf16[4,32,512]{2,1,0:T(8,128)(2,1)} %image_ref.1, bf16[768,320]{1,0:T(8,128)(2,1)} %constant.10.clone.pick_ref), custom_call_target="tpu_custom_call" | custom-call | tf_op jit(solution)/shard_map/pallas_call | solution.py:366
  3.4 0.0 copy-start
  3.4 31.7 %all_to_all.10 = bf16[1152,2,128]{2,1,0:T(2,128)(2,1)S(1)} all-to-all(bf16[1152,2,128]{2,1,0:T(2,128)(2,1)} %bitcast.7), channel_id=1, replica_groups={{108,109,110,111,12,13,14,15,88,89,90,91,72,73,74,75,92,93,94,95,68,69,..., dimensions={0} | all-to-all | bytes 1179648 | tf_op jit(solution)/shard_map/all_to_all | solution.py:355
  35.1 0.0 copy-done
  35.1 0.0 copy-start.3
  35.1 0.0 copy-start.4
  35.1 2.1 %shard_map.123 = (bf16[512,128]{1,0:T(8,128)(2,1)S(1)}, bf16[512,128]{1,0:T(8,128)(2,1)S(1)}, bf16[512,128]{1,0:T(8,128)(2,1)S(1)}, bf16[512,128]{1,0:T(8,128)(2,1)S(1)}, bf16[512,128]{1,0:T(8,128)(2,1)S(1)}) custom-call(bf16[32,72,128]{2,1,0:T(8,128)(2,1)S(1)} %bitcast.6, bf16[512,512]{1,0:T(8,128)(2,1)S(1)} %copy-done), custom_call_target="tpu_custom_call" | custom-call | tf_op jit(solution)/shard_map/pallas_call | solution.py:377
  37.2 0.6 collective-permute-start
  37.9 2.4 %collective-permute-start.1 = (bf16[512,128]{1,0:T(8,128)(2,1)S(1)}, bf16[512,128]{1,0:T(8,128)(2,1)S(1)}, u32[]{:S(2)}, u32[]{:S(2)}) collective-permute-start(bf16[512,128]{1,0:T(8,128)(2,1)S(1)} %get-tuple-element.9), channel_id=1, source_target_pairs={{4,0},{5,1},{6,2},{7,3},{0,4},{1,5},{2,6},{3,7},{12,8},{13,9},{14,... | collective-permute-start | bytes 393224 | tf_op jit(solution)/shard_map/ppermute | solution.py:385
  40.3 1.2 %collective-permute-start.2 = (bf16[512,128]{1,0:T(8,128)(2,1)S(1)}, bf16[512,128]{1,0:T(8,128)(2,1)S(1)}, u32[]{:S(2)}, u32[]{:S(2)}) collective-permute-start(bf16[512,128]{1,0:T(8,128)(2,1)S(1)} %get-tuple-element.10), channel_id=1, source_target_pairs={{5,0},{4,1},{7,2},{6,3},{1,4},{0,5},{3,6},{2,7},{13,8},{12,9},{15,... | collective-permute-start | bytes 393224 | tf_op jit(solution)/shard_map/ppermute | solution.py:385
  41.5 2.2 %collective-permute-done.p1_ref = bf16[512,128]{1,0:T(8,128)(2,1)S(1)} collective-permute-done((bf16[512,128]{1,0:T(8,128)(2,1)S(1)}, bf16[512,128]{1,0:T(8,128)(2,1)S(1)}, u32[]{:S(2)}, u32[]{:S(2)}) %collective-permute-start) | collective-permute-done | bytes 131104 | tf_op jit(solution)/shard_map/ppermute | solution.py:385
  43.7 0.8 collective-permute-done.1.p2_ref
  44.5 1.7 %collective-permute-done.2.p3_ref = bf16[512,128]{1,0:T(8,128)(2,1)S(1)} collective-permute-done((bf16[512,128]{1,0:T(8,128)(2,1)S(1)}, bf16[512,128]{1,0:T(8,128)(2,1)S(1)}, u32[]{:S(2)}, u32[]{:S(2)}) %collective-permute-start.2) | collective-permute-done | bytes 131104 | tf_op jit(solution)/shard_map/ppermute | solution.py:385
  46.2 0.0 copy-done.3
  46.2 0.0 copy-done.4
  46.2 1.5 %shard_map.124 = bf16[64,40,128]{2,1,0:T(8,128)(2,1)S(1)} custom-call(bf16[512,128]{1,0:T(8,128)(2,1)S(1)} %get-tuple-element.7.p0_ref, bf16[512,128]{1,0:T(8,128)(2,1)S(1)} %collective-permute-done.p1_ref, bf16[512,128]{1,0:T(8,128)(2,1)S(1)} %collective-permute-done.1.p2_ref, bf16[512,128]{1,0:T(8,128)(2,1)S(1)} %collective-permute-done.2.p3_ref, ...), custom_call_target="tpu_custom_call" | custom-call | tf_op jit(solution)/shard_map/pallas_call | solution.py:388
  47.7 0.0 copy-start.1
  47.7 0.0 copy-start.2
  47.7 27.0 %all_to_all.11 = bf16[640,4,128]{2,1,0:T(4,128)(2,1)S(1)} all-to-all(bf16[640,4,128]{2,1,0:T(4,128)(2,1)S(1)} %bitcast.4), channel_id=1, replica_groups={{90,91,38,39,32,33,60,61,4,5,76,77,100,101,74,75,120,121,54,55,64,65,40..., dimensions={0} | all-to-all | bytes 1310720 | tf_op jit(solution)/shard_map/all_to_all | solution.py:355
  74.7 0.0 copy-done.1
  74.7 0.0 copy-done.2
  74.7 1.8 %shard_map.125 = (bf16[4,32,512]{2,1,0:T(8,128)(2,1)}, f32[3,4,32,512]{3,2,1,0:T(8,128)}) custom-call(bf16[64,40,128]{2,1,0:T(8,128)(2,1)S(1)} %bitcast.5, bf16[512,512]{1,0:T(8,128)(2,1)S(1)} %copy-done.2, f32[3,4,32,512]{3,2,1,0:T(8,128)S(1)} %copy-done.1), custom_call_target="tpu_custom_call" | custom-call | tf_op jit(solution)/shard_map/pallas_call | solution.py:397
Async XLA Ops:
  3.4 31.7 %copy-start = (bf16[512,512]{1,0:T(8,128)(2,1)S(1)}, bf16[512,512]{1,0:T(8,128)(2,1)}, u32[]{:S(2)}) copy-start(bf16[512,512]{1,0:T(8,128)(2,1)} %constant.11.clone.deriv_ref) | copy-start | bytes 1572868
  35.1 11.1 %copy-start.3 = (bf16[512,512]{1,0:T(8,128)(2,1)S(1)}, bf16[512,512]{1,0:T(8,128)(2,1)}, u32[]{:S(2)}) copy-start(bf16[512,512]{1,0:T(8,128)(2,1)} %constant.13.clone.flip_ref) | copy-start | bytes 1572868
  35.1 11.1 %copy-start.4 = (bf16[512,512]{1,0:T(8,128)(2,1)S(1)}, bf16[512,512]{1,0:T(8,128)(2,1)}, u32[]{:S(2)}) copy-start(bf16[512,512]{1,0:T(8,128)(2,1)} %constant.12.clone.table_ref) | copy-start | bytes 1572868
  37.2 6.5 %collective-permute-start = (bf16[512,128]{1,0:T(8,128)(2,1)S(1)}, bf16[512,128]{1,0:T(8,128)(2,1)S(1)}, u32[]{:S(2)}, u32[]{:S(2)}) collective-permute-start(bf16[512,128]{1,0:T(8,128)(2,1)S(1)} %get-tuple-element.8), channel_id=1, source_target_pairs={{1,0},{0,1},{3,2},{2,3},{5,4},{4,5},{7,6},{6,7},{9,8},{8,9},{11,10... | collective-permute-start | bytes 393224 | tf_op jit(solution)/shard_map/ppermute | solution.py:385
  37.9 6.6 %collective-permute-start.1 = (bf16[512,128]{1,0:T(8,128)(2,1)S(1)}, bf16[512,128]{1,0:T(8,128)(2,1)S(1)}, u32[]{:S(2)}, u32[]{:S(2)}) collective-permute-start(bf16[512,128]{1,0:T(8,128)(2,1)S(1)} %get-tuple-element.9), channel_id=1, source_target_pairs={{4,0},{5,1},{6,2},{7,3},{0,4},{1,5},{2,6},{3,7},{12,8},{13,9},{14,... | collective-permute-start | bytes 393224 | tf_op jit(solution)/shard_map/ppermute | solution.py:385
  40.3 5.9 %collective-permute-start.2 = (bf16[512,128]{1,0:T(8,128)(2,1)S(1)}, bf16[512,128]{1,0:T(8,128)(2,1)S(1)}, u32[]{:S(2)}, u32[]{:S(2)}) collective-permute-start(bf16[512,128]{1,0:T(8,128)(2,1)S(1)} %get-tuple-element.10), channel_id=1, source_target_pairs={{5,0},{4,1},{7,2},{6,3},{1,4},{0,5},{3,6},{2,7},{13,8},{12,9},{15,... | collective-permute-start | bytes 393224 | tf_op jit(solution)/shard_map/ppermute | solution.py:385
  47.7 27.0 %copy-start.1 = (f32[3,4,32,512]{3,2,1,0:T(8,128)S(1)}, f32[3,4,32,512]{3,2,1,0:T(8,128)}, u32[]{:S(2)}) copy-start(f32[3,4,32,512]{3,2,1,0:T(8,128)} %velocity_ref.1) | copy-start | bytes 2359300
  47.7 27.0 %copy-start.2 = (bf16[512,512]{1,0:T(8,128)(2,1)S(1)}, bf16[512,512]{1,0:T(8,128)(2,1)}, u32[]{:S(2)}) copy-start(bf16[512,512]{1,0:T(8,128)(2,1)} %constant.14.clone.pick_ref) | copy-start | bytes 1572868
